TPU v7x, 32 devices: a whole 2x2x4 slice. The times are simulated.
32 devices in a mesh: rows: 4 (over y, core), cols: 8 (over z, x).
Axes of the slice: x: 2, y: 2, z: 4, core: 2. Of those that a mesh axis runs over, the one named last changes fastest.
Arguments:
- image: bfloat16 [128, 512, 128], P('rows', 'cols'), may hold values from -6 to 6
- routes: int32 [16, 64, 4], P('rows', 'cols'), may hold values from 0 to 1023, as said below
- norm_gain: float32 [128], replicated, may hold values from 0.1 to 1.9
- qkv_weight: bfloat16 [128, 384], replicated, may hold values from -25.455844 to 25.455844
- lce_weight: float32 [5, 5, 128], replicated, may hold values from -1.25 to 1.25
- out_weight: bfloat16 [128, 128], replicated, may hold values from -0.5 to 0.5
- mlp_gain: float32 [128], replicated, may hold values from 0.1 to 1.9
- up_weight: bfloat16 [128, 384], replicated, may hold values from -0.5 to 0.5
- down_weight: bfloat16 [384, 128], replicated, may hold values from -0.3125 to 0.3125
Outputs:
- refined: bfloat16 [128, 512, 128], P('rows', 'cols')
Inputs may be any that keep to these rules, and one draw needn't show every extreme that they name: Each region names 4 different regions. Of the routes of the regions of one device, at most 8 lead to the regions of any one device, and in every draw some device receives exactly 8 from every device.
All inputs are finite; a program needn't handle non-finite values.
Results may differ from a plain program's by a relative error of at most 0.0038.
The roundings to bfloat16 on the way count: a program that leaves them out, or rounds other values in their place, can miss the bound.
Values may be sent and summed in bfloat16 or wider, within the bound.
No kernel may reach another device: no remote copies, remote signals or barrier semaphores. Data moves between devices by JAX's collectives and lax.ppermute only.
A program may use at most 128 MiB of HBM per device.

v0:
```python
import functools
import math

import jax
import jax.numpy as jnp
from jax import lax
from jax.experimental import pallas as pl
from jax.experimental.pallas import tpu as pltpu
from jax.sharding import Mesh
from jax.sharding import PartitionSpec as P

HEADS = 4
PAIR = 2
EPSILON = 1e-06
F32 = jnp.float32
BF16 = jnp.bfloat16


def from_sides(low, high, axis):
    count = math.prod(lax.axis_size(name) for name in (axis if isinstance(axis, tuple) else (axis,)))
    forward = [(i, i + 1) for i in range(count - 1)]
    backward = [(target, source) for source, target in forward]
    return lax.ppermute(high, axis, forward), lax.ppermute(low, axis, backward)


def halo(image, margin, border):
    above, below = from_sides(image[:margin], image[-margin:], "rows")
    edges = lambda columns: jnp.concatenate(
        [above[:, columns], image[:, columns], below[:, columns]], axis=0
    )
    left, right = from_sides(
        edges(slice(0, border)), edges(slice(image.shape[1] - border, None)), ("z", "x")
    )
    return above, below, left, right


def normalize(floats, gain):
    centered = floats - jnp.mean(floats, axis=-1, keepdims=True)
    spread = jnp.mean(centered * centered, axis=-1, keepdims=True)
    return centered * lax.rsqrt(spread + EPSILON) * gain


def regions_of(strip, side):
    height, width, channels = strip.shape
    return (
        strip.reshape(height, width // side, side, channels)
        .transpose(1, 0, 2, 3)
        .reshape(height * width, channels)
    )


def strip_of(tokens, side, width):
    channels = tokens.shape[-1]
    return (
        tokens.reshape(width // side, side, side, channels)
        .transpose(1, 0, 2, 3)
        .reshape(side, width, channels)
    )


def norm_kernel(side, image_ref, gain_ref, out_ref):
    normed = normalize(image_ref[...].astype(F32), gain_ref[...])
    out_ref[...] = regions_of(normed, side).astype(BF16).reshape(out_ref.shape)


def norm_regions(image, gain, side):
    height, width, channels = image.shape
    per_row = width // side
    return pl.pallas_call(
        functools.partial(norm_kernel, side),
        grid=(height // side,),
        in_specs=[
            pl.BlockSpec((side, width, channels), lambda i: (i, 0, 0)),
            pl.BlockSpec((1, channels), lambda i: (0, 0)),
        ],
        out_specs=pl.BlockSpec((per_row, side * side, channels), lambda i: (i, 0, 0)),
        out_shape=jax.ShapeDtypeStruct(
            (height // side * per_row, side * side, channels), BF16
        ),
        cost_estimate=pl.CostEstimate(
            flops=10 * image.size, bytes_accessed=4 * image.size, transcendentals=0
        ),
        name="norm_regions",
    )(image, gain.reshape(1, channels))


def context_kernel(
    side,
    margin,
    image_ref,
    above_ref,
    below_ref,
    left_ref,
    right_ref,
    gain_ref,
    weight_ref,
    lce_ref,
    context_ref,
    query_ref,
    padded,
):
    step = pl.program_id(0)
    height, width, channels = image_ref.shape
    border = left_ref.shape[1]

    @pl.when(step == 0)
    def _():
        inner = pl.ds(border, width)
        padded[:margin, inner] = above_ref[...].astype(F32)
        padded[pl.ds(margin, height), inner] = image_ref[...].astype(F32)
        padded[pl.ds(margin + height, margin), inner] = below_ref[...].astype(F32)
        padded[:, :border] = left_ref[...].astype(F32)
        padded[:, pl.ds(border + width, border)] = right_ref[...].astype(F32)

    rows = side + 2 * margin
    strip = padded[pl.ds(step * side, rows)]
    wide = strip.shape[1]
    normed = normalize(strip, gain_ref[...]).astype(BF16).reshape(rows * wide, channels)
    weight = jnp.concatenate([weight_ref[:, :channels], weight_ref[:, 2 * channels :]], axis=1)
    projected = jnp.dot(normed, weight, preferred_element_type=F32).astype(BF16)
    values = projected[:, channels:].astype(F32).reshape(rows, wide, channels)
    summed = jnp.zeros((side, width, channels), F32)
    for col in range(2 * margin + 1):
        moved = pltpu.roll(values, wide - (border - margin + col), 1)[:, :width]
        for row in range(2 * margin + 1):
            summed = summed + moved[row : row + side] * lce_ref[row, pl.ds(col, 1), :]
    context_ref[...] = regions_of(summed, side)
    queries = projected[:, :channels].astype(F32).reshape(rows, wide, channels)
    inner = queries[margin : margin + side, border : border + width]
    query_ref[...] = regions_of(inner, side).astype(BF16)


def context_and_queries(image, around, gain, qkv_weight, lce_weight, side, margin):
    height, width, channels = image.shape
    border = around[-1].shape[1]
    tokens = height * width
    full = lambda a: pl.BlockSpec(a.shape, lambda i: (0,) * a.ndim)
    operands = (image, *around, gain.reshape(1, channels), qkv_weight, lce_weight)
    return pl.pallas_call(
        functools.partial(context_kernel, side, margin),
        grid=(height // side,),
        in_specs=[full(a) for a in operands],
        out_specs=[
            pl.BlockSpec((side * width, channels), lambda i: (i, 0)),
            pl.BlockSpec((side * width, channels), lambda i: (i, 0)),
        ],
        out_shape=[
            jax.ShapeDtypeStruct((tokens, channels), F32),
            jax.ShapeDtypeStruct((tokens, channels), BF16),
        ],
        scratch_shapes=[
            pltpu.VMEM((height + 2 * margin, width + 2 * border, channels), F32),
        ],
        cost_estimate=pl.CostEstimate(
            flops=tokens * channels * 600, bytes_accessed=10 * tokens * channels, transcendentals=0
        ),
        name="context",
    )(*operands)


def pack_kernel(chunks, capacity, layers, here_ref, wanted_ref, *refs):
    sources, out_refs = refs[: len(chunks)], refs[len(chunks) :]
    for distance, out_ref in enumerate(out_refs, 1):
        for place, (chunk, source_ref) in enumerate(zip(chunks, sources)):
            base = ((here_ref[0] ^ distance) * layers + (here_ref[1] ^ chunk)) * capacity
            for slot in range(capacity):
                out_ref[place * capacity + slot] = source_ref[wanted_ref[base + slot]]


def pack(sources, here, wanted, chunks, peers, layers, capacity):
    tile = sources[0].shape
    shape = (capacity * len(chunks), *tile[1:])
    count = peers - 1
    return pl.pallas_call(
        functools.partial(pack_kernel, chunks, capacity, layers),
        grid_spec=pltpu.PrefetchScalarGridSpec(
            num_scalar_prefetch=2,
            grid=(1,),
            in_specs=[pl.BlockSpec(tile, lambda i, *_: (0, 0, 0))] * len(chunks),
            out_specs=[pl.BlockSpec(shape, lambda i, *_: (0, 0, 0))] * count,
        ),
        out_shape=[jax.ShapeDtypeStruct(shape, BF16)] * count,
        cost_estimate=pl.CostEstimate(
            flops=0, bytes_accessed=4 * count * math.prod(shape), transcendentals=0
        ),
        name="pack",
    )(here, wanted, *sources)


def load_all(sources, landed, sems):
    copies, start = [], 0
    for i, source in enumerate(sources):
        copies.append(
            pltpu.make_async_copy(source, landed.at[pl.ds(start, source.shape[0])], sems.at[i])
        )
        start += source.shape[0]
    for copy in copies:
        copy.start()
    for copy in copies:
        copy.wait()


def collect_kernel(count, position_ref, *refs):
    sources, out_ref, landed, sems = refs[:count], refs[count], refs[-2], refs[-1]
    step = pl.program_id(0)

    @pl.when(step == 0)
    def _():
        load_all(sources, landed, sems)

    total = landed.shape[0]
    per_step = out_ref.shape[0]
    for i in range(per_step):
        at = position_ref[step * per_step + i]
        out_ref[i] = landed[jnp.where(at < total, at, 0)]


def collect(position, sources, steps):
    shape = sources[0].shape[1:]
    total = sum(source.shape[0] for source in sources)
    pairs = position.shape[0]
    return pl.pallas_call(
        functools.partial(collect_kernel, len(sources)),
        grid_spec=pltpu.PrefetchScalarGridSpec(
            num_scalar_prefetch=1,
            grid=(steps,),
            in_specs=[pl.BlockSpec(memory_space=pl.ANY)] * len(sources),
            out_specs=pl.BlockSpec((pairs // steps, *shape), lambda i, _: (i, 0, 0)),
            scratch_shapes=[
                pltpu.VMEM((total, *shape), BF16),
                pltpu.SemaphoreType.DMA((len(sources),)),
            ],
        ),
        out_shape=jax.ShapeDtypeStruct((pairs, *shape), BF16),
        cost_estimate=pl.CostEstimate(
            flops=0, bytes_accessed=2 * (total + pairs) * math.prod(shape), transcendentals=0
        ),
        name="collect",
    )(position, *sources)


def project(fetched, weight_ref):
    channels = fetched.shape[-1]
    projected = jnp.dot(
        fetched, weight_ref[:, channels : 3 * channels], preferred_element_type=F32
    ).astype(BF16)
    return projected[:, :channels], projected[:, channels:]


def score(queries, keys):
    area, channels = queries.shape
    lane = lax.broadcasted_iota(jnp.int32, (area, channels), 1) // (channels // HEADS)
    zero = jnp.zeros_like(queries)
    stacked = jnp.concatenate(
        [jnp.where(lane == head, queries, zero) for head in range(HEADS)], axis=0
    )
    return lax.dot_general(
        stacked, keys, (((1,), (1,)), ((), ())), preferred_element_type=F32
    )


def blend(weights, values):
    area, channels = weights.shape[0] // HEADS, values.shape[1]
    blended = jnp.dot(weights, values, preferred_element_type=F32)
    lane = lax.broadcasted_iota(jnp.int32, (area, channels), 1) // (channels // HEADS)
    picked = blended[:area]
    for head in range(1, HEADS):
        picked = jnp.where(lane == head, blended[head * area : (head + 1) * area], picked)
    return picked


def gelu(lifted):
    inner = lifted * (0.7978845608028654 + 0.035677408136300125 * (lifted * lifted))
    return lifted * (0.5 + 0.5 * jnp.tanh(inner))


def tail_kernel(side, picks, batch, early, late_count, position_ref, *refs):
    late = refs[:late_count]
    (
        fetched_ref,
        query_ref,
        context_ref,
        image_ref,
        qkv_ref,
        out_weight_ref,
        gain_ref,
        up_ref,
        down_ref,
        result_ref,
        landed,
        combined_ref,
        sems,
    ) = refs[late_count:]
    step = pl.program_id(0)
    last = pl.num_programs(0) - 2

    @pl.when(step == 0)
    def _():
        combined_ref[...] = jnp.zeros_like(combined_ref)
        load_all(late, landed, sems)

    area, channels = fetched_ref.shape[1:]
    exponent = (channels // HEADS) ** (-0.5) * math.log2(math.e)
    first = jnp.minimum(step, last) * (batch * picks)

    def piece(which):
        at = position_ref[first + which]
        is_late = at >= early
        return jnp.where(is_late, landed[jnp.where(is_late, at - early, 0)], fetched_ref[which])

    previous = combined_ref[...]
    chunk = PAIR * area

    def attention(region):
        rows = pl.ds(region * area, area)
        fetched = jnp.concatenate(
            [piece(which) for which in range(region * picks, (region + 1) * picks)], axis=0
        )
        keys, values = project(fetched, qkv_ref)
        yield True
        scores = score(query_ref[rows, :], keys)
        yield True
        highest = jnp.max(scores, axis=-1, keepdims=True)
        expons = jnp.exp2((scores - highest) * exponent)
        yield True
        total = jnp.sum(expons, axis=-1, keepdims=True)
        weights = (expons * (1.0 / total)).astype(BF16)
        yield True
        attended = blend(weights, values)
        combined_ref[rows, :] = (attended + context_ref[rows, :]).astype(BF16)
        yield True

    def feed_forward(part):
        columns = pl.ds(part * PAIR * side, PAIR * side)
        image = regions_of(image_ref[:, columns, :].astype(F32), side)
        combined = previous[part * chunk : (part + 1) * chunk]
        residual = image + jnp.dot(combined, out_weight_ref[...], preferred_element_type=F32)
        yield True
        stored = residual.astype(BF16).astype(F32)
        second = normalize(stored, gain_ref[...]).astype(BF16)
        yield True
        lifted = jnp.dot(second, up_ref[...], preferred_element_type=F32)
        yield True
        hidden = gelu(lifted).astype(BF16)
        yield True
        refined = stored + jnp.dot(hidden, down_ref[...], preferred_element_type=F32)
        result_ref[:, columns, :] = strip_of(refined, side, PAIR * side).astype(BF16)
        yield True

    lines = [feed_forward(part) for part in range(batch // PAIR)]
    lines += [attention(region) for region in range(batch)]
    while lines:
        lines = [line for line in lines if next(line, None) is not None]


def tail(position, early, fetched, late, queries, context, image, weights, side, picks):
    height, width, channels = image.shape
    area = side * side
    per_row = width // side
    batch = math.gcd(per_row, 4)
    halves = per_row // batch
    steps = height // side * halves
    full = lambda a: pl.BlockSpec(a.shape, lambda i, position: (0,) * a.ndim)
    now = lambda i: jnp.minimum(i, steps - 1)
    before = lambda i: jnp.maximum(i - 1, 0)
    tokens = pl.BlockSpec((batch * area, channels), lambda i, position: (now(i), 0))
    strip = pl.BlockSpec(
        (side, batch * side, channels),
        lambda i, position: (before(i) // halves, before(i) % halves, 0),
    )
    regions = pl.BlockSpec((batch * picks, area, channels), lambda i, position: (now(i), 0, 0))
    total = sum(a.shape[0] for a in late)
    return pl.pallas_call(
        functools.partial(tail_kernel, side, picks, batch, early, len(late)),
        grid_spec=pltpu.PrefetchScalarGridSpec(
            num_scalar_prefetch=1,
            grid=(steps + 1,),
            in_specs=[pl.BlockSpec(memory_space=pl.ANY)] * len(late)
            + [regions, tokens, tokens, strip]
            + [full(w) for w in weights],
            out_specs=strip,
            scratch_shapes=[
                pltpu.VMEM((total, area, channels), BF16),
                pltpu.VMEM((batch * area, channels), BF16),
                pltpu.SemaphoreType.DMA((len(late),)),
            ],
        ),
        out_shape=jax.ShapeDtypeStruct(image.shape, BF16),
        cost_estimate=pl.CostEstimate(
            flops=image.size * 4000, bytes_accessed=16 * image.size, transcendentals=40 * image.size
        ),
        name="tail",
    )(position, *late, fetched, queries, context, image, *weights)


def layer_blocks(block, layer, layers):
    if layers != 4:
        return [block] + [
            lax.ppermute(block, "z", [(i, i ^ step) for i in range(layers)])
            for step in range(1, layers)
        ]

    def hop(block, pairs):
        return lax.ppermute(block, "z", pairs)

    beside = hop(block, [(0, 1), (1, 0), (2, 3), (3, 2)])
    middle = hop(block, [(1, 2), (2, 1)])
    middle_two = hop(beside, [(1, 2), (2, 1)])
    ends_two = hop(middle, [(1, 0), (2, 3)])
    ends_three = hop(middle_two, [(1, 0), (2, 3)])
    inside = (layer == 1) | (layer == 2)
    return [
        block,
        beside,
        jnp.where(inside, middle_two, ends_two),
        jnp.where(inside, middle, ends_three),
    ]


def block(
    image, routes, norm_gain, qkv_weight, lce_weight, out_weight, mlp_gain, up_weight, down_weight
):
    height, _, channels = image.shape
    layers, across = lax.axis_size("z"), lax.axis_size("x")
    peers = lax.axis_size("rows") * across
    devices = peers * layers
    region_rows, region_cols, pick_count = routes.shape
    side = height // region_rows
    pair_count = region_rows * region_cols * pick_count
    capacity = max(2, 2 * pair_count // devices)
    all_cols = region_cols * layers * across

    regions = region_rows * region_cols
    peer = lax.axis_index("rows") * across + lax.axis_index("x")
    layer = lax.axis_index("z")
    here = jnp.stack([peer, layer])

    targets = routes.reshape(pair_count)
    target_row = targets // all_cols
    target_col = targets % all_cols
    owner_col = target_col // region_cols
    owner_layer = owner_col // across
    owner_peer = target_row // region_rows * across + owner_col % across
    local_index = target_row % region_rows * region_cols + target_col % region_cols
    owners = owner_peer * layers + owner_layer
    pairs = jnp.arange(pair_count, dtype=jnp.int32)
    earlier = (owners[:, None] == owners[None, :]) & (pairs[None, :] < pairs[:, None])
    slot = jnp.sum(earlier.astype(jnp.int32), axis=1)
    distance = owner_peer ^ peer
    chunk = owner_layer ^ layer
    groups = [(0, 1), *((step,) for step in range(2, layers))]
    position, start = jnp.zeros_like(slot), 0
    for members in groups:
        replies = start + len(members) * regions
        for place, step in enumerate(members):
            here_at = start + place * regions + local_index
            sent_at = (
                replies + ((distance - 1) * len(members) + place) * capacity + slot
            )
            position = jnp.where(
                chunk == step, jnp.where(distance == 0, here_at, sent_at), position
            )
        early = start
        start = replies + (peers - 1) * len(members) * capacity
    asked = owners * capacity + slot
    slots = jnp.arange(devices * capacity, dtype=jnp.int32)
    requests = jnp.sum(
        jnp.where(asked[None, :] == slots[:, None], local_index[None, :], 0), axis=1
    )
    wanted = lax.all_to_all(
        requests.reshape(peers, layers * capacity), ("rows", "x"), 0, 0, tiled=True
    ).reshape(-1)

    normed = norm_regions(image, norm_gain, side)

    held = layer_blocks(normed, layer, layers)
    arrived = []
    for members in groups:
        sources = [held[step] for step in members]
        packed = pack(sources, here, wanted, members, peers, layers, capacity)
        arrived.append(
            sources
            + [
                lax.ppermute(part, ("rows", "x"), [(i, i ^ far) for i in range(peers)])
                for far, part in enumerate(packed, 1)
            ]
        )
    late = arrived.pop()
    fetched = collect(position, sum(arrived, []), math.gcd(pair_count, 8))

    margin = (lce_weight.shape[0] - 1) // 2
    around = halo(image, margin, 8)
    context, queries = context_and_queries(
        image, around, norm_gain, qkv_weight, lce_weight, side, margin
    )
    weights = (
        qkv_weight,
        out_weight,
        mlp_gain.reshape(1, channels),
        up_weight,
        down_weight,
    )
    return tail(position, early, fetched, late, queries, context, image, weights, side, pick_count)


def solution(mesh):
    devices = mesh.devices
    layers = len({device.coords[2] for device in devices[0]})
    split = Mesh(
        devices.reshape(devices.shape[0], layers, devices.shape[1] // layers), ("rows", "z", "x")
    )
    grid = P("rows", ("z", "x"), None)
    in_specs = (grid, grid, P(), P(), P(), P(), P(), P(), P())
    return jax.shard_map(block, mesh=split, in_specs=in_specs, out_specs=grid, check_vma=False)
```

profile of v0, /device:TPU:17, one launch (start us, length us, event | category | flops | bytes accessed | tf_op | source)
XLA Modules:
  0.0 138.1 jit_solution(16541893218558657070)
XLA Ops:
  0.0 3.6 %norm_regions.1.refs_0_ = bf16[32,64,128]{2,1,0:T(8,128)(2,1)} custom-call(bf16[32,64,128]{2,1,0:T(8,128)(2,1)} %refs_11_.1, f32[1,128]{1,0:T(1,128)} %bitcast.4), custom_call_target="tpu_custom_call" | custom-call | flops 2621440 | bytes 1048576 | tf_op jit(solution)/shard_map/norm_regions/pallas_call | solution.py:69
  3.6 1.3 collective-permute-start.1
  4.9 1.9 %collective-permute-start = (bf16[32,64,128]{2,1,0:T(8,128)(2,1)}, bf16[32,64,128]{2,1,0:T(8,128)(2,1)S(1)}, u32[]{:S(2)}, u32[]{:S(2)}) collective-permute-start(bf16[32,64,128]{2,1,0:T(8,128)(2,1)} %norm_regions.1.refs_0_), channel_id=1, source_target_pairs={{2,4},{4,2},{3,5},{5,3},{10,12},{12,10},{11,13},{13,11},{18,20},{2... | collective-permute-start | bytes 1572872 | tf_op jit(solution)/shard_map/ppermute | solution.py:404
  6.8 0.8 copy.12
  8.7 0.7 all_to_all.6
  9.3 4.7 %all-to-all-start = ((s32[8,1,32]{2,1,0:T(1,128)}), s32[8,1,32]{2,1,0:T(1,128)S(1)}, u32[]{:S(2)}, u32[]{:S(2)}) async-start(s32[8,1,32]{2,1,0:T(1,128)} %all_to_all.6), calls=%async_computation | async-start | bytes 8192 | tf_op jit(solution)/shard_map/all_to_all | solution.py:470
  14.0 0.8 fusion.7
  14.8 3.5 %collective-permute-start.26 = (bf16[2,64,128]{2,1,0:T(8,128)(2,1)S(1)}, bf16[2,64,128]{2,1,0:T(8,128)(2,1)S(1)}, u32[]{:S(2)}, u32[]{:S(2)}) collective-permute-start(bf16[2,64,128]{2,1,0:T(8,128)(2,1)S(1)} %get-tuple-element.63), channel_id=1, source_target_pairs={{0,8},{8,16},{16,24},{1,9},{9,17},{17,25},{2,10},{10,18},{18,26},{... | collective-permute-start | bytes 98312 | tf_op jit(solution)/shard_map/ppermute | solution.py:23
  18.3 1.9 %collective-permute-start.27 = (bf16[2,64,128]{2,1,0:T(8,128)(2,1)S(1)}, bf16[2,64,128]{2,1,0:T(8,128)(2,1)S(1)}, u32[]{:S(2)}, u32[]{:S(2)}) collective-permute-start(bf16[2,64,128]{2,1,0:T(8,128)(2,1)S(1)} %get-tuple-element.62), channel_id=1, source_target_pairs={{8,0},{16,8},{24,16},{9,1},{17,9},{25,17},{10,2},{18,10},{26,18},{... | collective-permute-start | bytes 98312 | tf_op jit(solution)/shard_map/ppermute | solution.py:23
  20.3 0.9 fusion.6
  21.2 3.6 %collective-permute-start.2 = (bf16[32,64,128]{2,1,0:T(8,128)(2,1)S(1)}, bf16[32,64,128]{2,1,0:T(8,128)(2,1)S(1)}, u32[]{:S(2)}, u32[]{:S(2)}) collective-permute-start(bf16[32,64,128]{2,1,0:T(8,128)(2,1)S(1)} %collective-permute-done.1.refs_1_), channel_id=1, source_target_pairs={{2,4},{4,2},{3,5},{5,3},{10,12},{12,10},{11,13},{13,11},{18,20},{2... | collective-permute-start | bytes 1572872 | tf_op jit(solution)/shard_map/ppermute | solution.py:404
  24.8 0.7 pad_add_fusion.here_ref
  26.0 0.7 reduce.3
  26.7 0.7 reshape.294.wanted_ref
  27.3 0.6 copy-done.15
  28.0 1.3 collective-permute-start.18
  29.3 3.3 %pack.4 = (bf16[16,64,128]{2,1,0:T(8,128)(2,1)}, bf16[16,64,128]{2,1,0:T(8,128)(2,1)}, bf16[16,64,128]{2,1,0:T(8,128)(2,1)}, bf16[16,64,128]{2,1,0:T(8,128)(2,1)...) custom-call(s32[2]{0:T(128)} %pad_add_fusion.here_ref, ...), custom_call_target="tpu_custom_call" | custom-call | bytes 3670016 | tf_op jit(solution)/shard_map/pack/pallas_call | solution.py:174
  32.6 1.2 collective-permute-start.11
  33.8 1.9 %collective-permute-done.2 = bf16[32,64,128]{2,1,0:T(8,128)(2,1)S(1)} collective-permute-done((bf16[32,64,128]{2,1,0:T(8,128)(2,1)S(1)}, bf16[32,64,128]{2,1,0:T(8,128)(2,1)S(1)}, u32[]{:S(2)}, u32[]{:S(2)}) %collective-permute-start.2) | collective-permute-done | bytes 524320 | tf_op jit(solution)/shard_map/ppermute | solution.py:404
  35.7 1.3 collective-permute-start.3
  37.1 3.3 %collective-permute-start.28 = (bf16[36,8,128]{2,1,0:T(8,128)(2,1)S(1)}, bf16[36,8,128]{2,1,0:T(8,128)(2,1)}, u32[]{:S(2)}, u32[]{:S(2)}) collective-permute-start(bf16[36,8,128]{2,1,0:T(8,128)(2,1)S(1)} %pad_maximum_fusion), channel_id=1, source_target_pairs={{0,1},{1,2},{2,3},{3,4},{4,5},{5,6},{6,7},{8,9},{9,10},{10,11},{11... | collective-permute-start | bytes 221192 | tf_op jit(solution)/shard_map/ppermute | solution.py:23
  40.3 3.5 %collective-permute-done.28.left_ref = bf16[36,8,128]{2,1,0:T(8,128)(2,1)} collective-permute-done((bf16[36,8,128]{2,1,0:T(8,128)(2,1)S(1)}, bf16[36,8,128]{2,1,0:T(8,128)(2,1)}, u32[]{:S(2)}, u32[]{:S(2)}) %collective-permute-start.28) | collective-permute-done | bytes 73760 | tf_op jit(solution)/shard_map/ppermute | solution.py:23
  43.8 3.6 %collective-permute-start.29 = (bf16[36,8,128]{2,1,0:T(8,128)(2,1)S(1)}, bf16[36,8,128]{2,1,0:T(8,128)(2,1)S(1)}, u32[]{:S(2)}, u32[]{:S(2)}) collective-permute-start(bf16[36,8,128]{2,1,0:T(8,128)(2,1)S(1)} %pad_maximum_fusion.1), channel_id=1, source_target_pairs={{1,0},{2,1},{3,2},{4,3},{5,4},{6,5},{7,6},{9,8},{10,9},{11,10},{12... | collective-permute-start | bytes 221192 | tf_op jit(solution)/shard_map/ppermute | solution.py:23
  47.5 10.2 %collective-permute-done.29.right_ref = bf16[36,8,128]{2,1,0:T(8,128)(2,1)S(1)} collective-permute-done((bf16[36,8,128]{2,1,0:T(8,128)(2,1)S(1)}, bf16[36,8,128]{2,1,0:T(8,128)(2,1)S(1)}, u32[]{:S(2)}, u32[]{:S(2)}) %collective-permute-start.29) | collective-permute-done | bytes 73760 | tf_op jit(solution)/shard_map/ppermute | solution.py:23
  57.7 0.6 copy-done.14
  58.3 3.5 %collective-permute-start.13 = (bf16[16,64,128]{2,1,0:T(8,128)(2,1)}, bf16[16,64,128]{2,1,0:T(8,128)(2,1)S(1)}, u32[]{:S(2)}, u32[]{:S(2)}) collective-permute-start(bf16[16,64,128]{2,1,0:T(8,128)(2,1)} %get-tuple-element.37), channel_id=1, source_target_pairs={{0,9},{1,8},{8,1},{9,0},{16,25},{17,24},{24,17},{25,16},{2,11},{3,... | collective-permute-start | bytes 786440 | tf_op jit(solution)/shard_map/ppermute | solution.py:484
  61.9 1.9 %collective-permute-start.14 = (bf16[16,64,128]{2,1,0:T(8,128)(2,1)}, bf16[16,64,128]{2,1,0:T(8,128)(2,1)S(1)}, u32[]{:S(2)}, u32[]{:S(2)}) collective-permute-start(bf16[16,64,128]{2,1,0:T(8,128)(2,1)} %get-tuple-element.38), channel_id=1, source_target_pairs={{0,16},{1,17},{8,24},{9,25},{16,0},{17,1},{24,8},{25,9},{2,18},{3,... | collective-permute-start | bytes 786440 | tf_op jit(solution)/shard_map/ppermute | solution.py:484
  63.8 1.8 %collective-permute-start.16 = (bf16[16,64,128]{2,1,0:T(8,128)(2,1)}, bf16[16,64,128]{2,1,0:T(8,128)(2,1)}, u32[]{:S(2)}, u32[]{:S(2)}) collective-permute-start(bf16[16,64,128]{2,1,0:T(8,128)(2,1)} %get-tuple-element.40), channel_id=1, source_target_pairs={{0,24},{1,25},{8,16},{9,17},{16,8},{17,9},{24,0},{25,1},{2,26},{3,... | collective-permute-start | bytes 786440 | tf_op jit(solution)/shard_map/ppermute | solution.py:484
  65.6 0.9 broadcast_select_fusion.refs_0_.refs_9_
  66.5 2.8 %pack.5 = (bf16[8,64,128]{2,1,0:T(8,128)(2,1)}, bf16[8,64,128]{2,1,0:T(8,128)(2,1)}, bf16[8,64,128]{2,1,0:T(8,128)(2,1)}, bf16[8,64,128]{2,1,0:T(8,128)(2,1)}, b...) custom-call(s32[2]{0:T(128)} %pad_add_fusion.here_ref, ...), custom_call_target="tpu_custom_call" | custom-call | bytes 1835008 | tf_op jit(solution)/shard_map/pack/pallas_call | solution.py:174
  69.3 1.0 collective-permute-start.17
  70.3 11.8 %collective-permute-done.14.refs_5_ = bf16[16,64,128]{2,1,0:T(8,128)(2,1)S(1)} collective-permute-done((bf16[16,64,128]{2,1,0:T(8,128)(2,1)}, bf16[16,64,128]{2,1,0:T(8,128)(2,1)S(1)}, u32[]{:S(2)}, u32[]{:S(2)}) %collective-permute-start.14) | collective-permute-done | bytes 262176 | tf_op jit(solution)/shard_map/ppermute | solution.py:484
  82.0 1.1 collective-permute-start.20
  83.2 4.6 %collective-permute-done.16.refs_7_ = bf16[16,64,128]{2,1,0:T(8,128)(2,1)} collective-permute-done((bf16[16,64,128]{2,1,0:T(8,128)(2,1)}, bf16[16,64,128]{2,1,0:T(8,128)(2,1)}, u32[]{:S(2)}, u32[]{:S(2)}) %collective-permute-start.16) | collective-permute-done | bytes 262176 | tf_op jit(solution)/shard_map/ppermute | solution.py:484
  87.8 0.9 broadcast_select_fusion.1.refs_0_
  88.6 2.8 %pack.3 = (bf16[8,64,128]{2,1,0:T(8,128)(2,1)}, bf16[8,64,128]{2,1,0:T(8,128)(2,1)}, bf16[8,64,128]{2,1,0:T(8,128)(2,1)}, bf16[8,64,128]{2,1,0:T(8,128)(2,1)}, b...) custom-call(s32[2]{0:T(128)} %pad_add_fusion.here_ref, ...), custom_call_target="tpu_custom_call" | custom-call | bytes 1835008 | tf_op jit(solution)/shard_map/pack/pallas_call | solution.py:174
  91.4 3.0 %collective-permute-start.23 = (bf16[8,64,128]{2,1,0:T(8,128)(2,1)}, bf16[8,64,128]{2,1,0:T(8,128)(2,1)S(1)}, u32[]{:S(2)}, u32[]{:S(2)}) collective-permute-start(bf16[8,64,128]{2,1,0:T(8,128)(2,1)} %get-tuple-element.46), channel_id=1, source_target_pairs={{0,17},{1,16},{8,25},{9,24},{16,1},{17,0},{24,9},{25,8},{2,19},{3,... | collective-permute-start | bytes 393224 | tf_op jit(solution)/shard_map/ppermute | solution.py:484
  94.7 0.9 collective-permute-start.25
  95.6 1.7 %collective-permute-start.10 = (bf16[8,64,128]{2,1,0:T(8,128)(2,1)}, bf16[8,64,128]{2,1,0:T(8,128)(2,1)S(1)}, u32[]{:S(2)}, u32[]{:S(2)}) collective-permute-start(bf16[8,64,128]{2,1,0:T(8,128)(2,1)} %get-tuple-element.34), channel_id=1, source_target_pairs={{0,25},{1,24},{8,17},{9,16},{16,9},{17,8},{24,1},{25,0},{2,27},{3,... | collective-permute-start | bytes 393224 | tf_op jit(solution)/shard_map/ppermute | solution.py:484
  98.1 1.2 collective-permute-start.5
  99.3 7.8 %collective-permute-done.24.refs_15_ = bf16[8,64,128]{2,1,0:T(8,128)(2,1)S(1)} collective-permute-done((bf16[8,64,128]{2,1,0:T(8,128)(2,1)}, bf16[8,64,128]{2,1,0:T(8,128)(2,1)S(1)}, u32[]{:S(2)}, u32[]{:S(2)}) %collective-permute-start.24) | collective-permute-done | bytes 131104 | tf_op jit(solution)/shard_map/ppermute | solution.py:484
  107.1 1.5 %collective-permute-start.6 = (bf16[8,64,128]{2,1,0:T(8,128)(2,1)}, bf16[8,64,128]{2,1,0:T(8,128)(2,1)S(1)}, u32[]{:S(2)}, u32[]{:S(2)}) collective-permute-start(bf16[8,64,128]{2,1,0:T(8,128)(2,1)} %get-tuple-element.30), channel_id=1, source_target_pairs={{0,9},{1,8},{8,1},{9,0},{16,25},{17,24},{24,17},{25,16},{2,11},{3,... | collective-permute-start | bytes 393224 | tf_op jit(solution)/shard_map/ppermute | solution.py:484
  108.6 0.6 collective-permute-start.7
  109.2 0.8 collective-permute-start.8
  110.1 1.4 %collective-permute-start.9 = (bf16[8,64,128]{2,1,0:T(8,128)(2,1)}, bf16[8,64,128]{2,1,0:T(8,128)(2,1)S(1)}, u32[]{:S(2)}, u32[]{:S(2)}) collective-permute-start(bf16[8,64,128]{2,1,0:T(8,128)(2,1)} %get-tuple-element.33), channel_id=1, source_target_pairs={{0,24},{1,25},{8,16},{9,17},{16,8},{17,9},{24,0},{25,1},{2,26},{3,... | collective-permute-start | bytes 393224 | tf_op jit(solution)/shard_map/ppermute | solution.py:484
  111.5 5.9 %context.1 = (f32[2048,128]{1,0:T(8,128)}, bf16[2048,128]{1,0:T(8,128)(2,1)}) custom-call(bf16[32,64,128]{2,1,0:T(8,128)(2,1)} %refs_11_.1, bf16[2,64,128]{2,1,0:T(8,128)(2,1)} %copy-done.15, bf16[2,64,128]{2,1,0:T(8,128)(2,1)} %copy-done.16, bf16[36,8,128]{2,1,0:T(8,128)(2,1)} %collective-permute-done.28.left_ref, bf16[36,8,128]{2,1,0:T(8,128)(2,1)} %copy-done.14, ...), custom_call_target="tpu_custom_call" | custom-call | flops 157286400 | bytes 2621440 | tf_op jit(solution)/shard_map/context/pallas_call | solution.py:139
  117.5 6.0 %collect.1.refs_8_ = bf16[128,64,128]{2,1,0:T(8,128)(2,1)} custom-call(s32[128]{0:T(128)} %get-tuple-element.51.position_ref, bf16[32,64,128]{2,1,0:T(8,128)(2,1)} %norm_regions.1.refs_0_, bf16[32,64,128]{2,1,0:T(8,128)(2,1)} %copy-done, bf16[16,64,128]{2,1,0:T(8,128)(2,1)} %copy-done.1, bf16[16,64,128]{2,1,0:T(8,128)(2,1)} %copy-done.2, ...), custom_call_target="tpu_custom_call" | custom-call | bytes 6422528 | tf_op jit(solution)/shard_map/collect/pallas_call | solution.py:222
  124.4 13.7 %tail.1 = bf16[32,64,128]{2,1,0:T(8,128)(2,1)} custom-call(s32[128]{0:T(128)} %get-tuple-element.51.position_ref, bf16[32,64,128]{2,1,0:T(8,128)(2,1)} %broadcast_select_fusion.1.refs_0_, bf16[8,64,128]{2,1,0:T(8,128)(2,1)} %copy-done.18, bf16[8,64,128]{2,1,0:T(8,128)(2,1)} %copy-done.19, bf16[8,64,128]{2,1,0:T(8,128)(2,1)} %copy-done.20, ...), custom_call_target="tpu_custom_call" | custom-call | flops 1048576000 | bytes 4194304 | tf_op jit(solution)/shard_map/tail/pallas_call | solution.py:373
  (89 shorter events, 3.6 us)
Async XLA Ops:
  3.6 17.6 %collective-permute-start.1 = (bf16[32,64,128]{2,1,0:T(8,128)(2,1)}, bf16[32,64,128]{2,1,0:T(8,128)(2,1)S(1)}, u32[]{:S(2)}, u32[]{:S(2)}) collective-permute-start(bf16[32,64,128]{2,1,0:T(8,128)(2,1)} %norm_regions.1.refs_0_), channel_id=1, source_target_pairs={{0,2},{2,0},{4,6},{6,4},{1,3},{3,1},{5,7},{7,5},{8,10},{10,8},{12,... | collective-permute-start | bytes 1572872 | tf_op jit(solution)/shard_map/ppermute | solution.py:404
  4.9 23.1 %collective-permute-start = (bf16[32,64,128]{2,1,0:T(8,128)(2,1)}, bf16[32,64,128]{2,1,0:T(8,128)(2,1)S(1)}, u32[]{:S(2)}, u32[]{:S(2)}) collective-permute-start(bf16[32,64,128]{2,1,0:T(8,128)(2,1)} %norm_regions.1.refs_0_), channel_id=1, source_target_pairs={{2,4},{4,2},{3,5},{5,3},{10,12},{12,10},{11,13},{13,11},{18,20},{2... | collective-permute-start | bytes 1572872 | tf_op jit(solution)/shard_map/ppermute | solution.py:404
  9.3 16.1 %all-to-all-start = ((s32[8,1,32]{2,1,0:T(1,128)}), s32[8,1,32]{2,1,0:T(1,128)S(1)}, u32[]{:S(2)}, u32[]{:S(2)}) async-start(s32[8,1,32]{2,1,0:T(1,128)} %all_to_all.6), calls=%async_computation | async-start | bytes 8192 | tf_op jit(solution)/shard_map/all_to_all | solution.py:470
  14.8 12.5 %collective-permute-start.26 = (bf16[2,64,128]{2,1,0:T(8,128)(2,1)S(1)}, bf16[2,64,128]{2,1,0:T(8,128)(2,1)S(1)}, u32[]{:S(2)}, u32[]{:S(2)}) collective-permute-start(bf16[2,64,128]{2,1,0:T(8,128)(2,1)S(1)} %get-tuple-element.63), channel_id=1, source_target_pairs={{0,8},{8,16},{16,24},{1,9},{9,17},{17,25},{2,10},{10,18},{18,26},{... | collective-permute-start | bytes 98312 | tf_op jit(solution)/shard_map/ppermute | solution.py:23
  18.3 10.9 %collective-permute-start.27 = (bf16[2,64,128]{2,1,0:T(8,128)(2,1)S(1)}, bf16[2,64,128]{2,1,0:T(8,128)(2,1)S(1)}, u32[]{:S(2)}, u32[]{:S(2)}) collective-permute-start(bf16[2,64,128]{2,1,0:T(8,128)(2,1)S(1)} %get-tuple-element.62), channel_id=1, source_target_pairs={{8,0},{16,8},{24,16},{9,1},{17,9},{25,17},{10,2},{18,10},{26,18},{... | collective-permute-start | bytes 98312 | tf_op jit(solution)/shard_map/ppermute | solution.py:23
  21.2 8.2 %copy-start = (bf16[32,64,128]{2,1,0:T(8,128)(2,1)}, bf16[32,64,128]{2,1,0:T(8,128)(2,1)S(1)}, u32[]{:S(2)}) copy-start(bf16[32,64,128]{2,1,0:T(8,128)(2,1)S(1)} %collective-permute-done.1.refs_1_) | copy-start | bytes 1572868
  21.2 14.5 %collective-permute-start.2 = (bf16[32,64,128]{2,1,0:T(8,128)(2,1)S(1)}, bf16[32,64,128]{2,1,0:T(8,128)(2,1)S(1)}, u32[]{:S(2)}, u32[]{:S(2)}) collective-permute-start(bf16[32,64,128]{2,1,0:T(8,128)(2,1)S(1)} %collective-permute-done.1.refs_1_), channel_id=1, source_target_pairs={{2,4},{4,2},{3,5},{5,3},{10,12},{12,10},{11,13},{13,11},{18,20},{2... | collective-permute-start | bytes 1572872 | tf_op jit(solution)/shard_map/ppermute | solution.py:404
  28.0 35.9 %collective-permute-start.18 = (bf16[32,64,128]{2,1,0:T(8,128)(2,1)S(1)}, bf16[32,64,128]{2,1,0:T(8,128)(2,1)S(1)}, u32[]{:S(2)}, u32[]{:S(2)}) collective-permute-start(bf16[32,64,128]{2,1,0:T(8,128)(2,1)S(1)} %collective-permute-done), channel_id=1, source_target_pairs={{2,0},{4,6},{3,1},{5,7},{10,8},{12,14},{11,9},{13,15},{18,16},{20,... | collective-permute-start | bytes 1572872 | tf_op jit(solution)/shard_map/ppermute | solution.py:404
  29.3 3.3 %copy-start.16 = (bf16[2,64,128]{2,1,0:T(8,128)(2,1)}, bf16[2,64,128]{2,1,0:T(8,128)(2,1)S(1)}, u32[]{:S(2)}) copy-start(bf16[2,64,128]{2,1,0:T(8,128)(2,1)S(1)} %collective-permute-done.27.below_ref) | copy-start | bytes 98308
  32.6 29.3 %collective-permute-start.11 = (bf16[16,64,128]{2,1,0:T(8,128)(2,1)}, bf16[16,64,128]{2,1,0:T(8,128)(2,1)S(1)}, u32[]{:S(2)}, u32[]{:S(2)}) collective-permute-start(bf16[16,64,128]{2,1,0:T(8,128)(2,1)} %get-tuple-element.35), channel_id=1, source_target_pairs={{0,1},{1,0},{8,9},{9,8},{16,17},{17,16},{24,25},{25,24},{2,3},{3,2... | collective-permute-start | bytes 786440 | tf_op jit(solution)/shard_map/ppermute | solution.py:484
  33.8 30.0 %collective-permute-start.12 = (bf16[16,64,128]{2,1,0:T(8,128)(2,1)}, bf16[16,64,128]{2,1,0:T(8,128)(2,1)S(1)}, u32[]{:S(2)}, u32[]{:S(2)}) collective-permute-start(bf16[16,64,128]{2,1,0:T(8,128)(2,1)} %get-tuple-element.36), channel_id=1, source_target_pairs={{0,8},{1,9},{8,0},{9,1},{16,24},{17,25},{24,16},{25,17},{2,10},{3,... | collective-permute-start | bytes 786440 | tf_op jit(solution)/shard_map/ppermute | solution.py:484
  35.7 52.0 %collective-permute-start.3 = (bf16[32,64,128]{2,1,0:T(8,128)(2,1)S(1)}, bf16[32,64,128]{2,1,0:T(8,128)(2,1)S(1)}, u32[]{:S(2)}, u32[]{:S(2)}) collective-permute-start(bf16[32,64,128]{2,1,0:T(8,128)(2,1)S(1)} %collective-permute-done.2), channel_id=1, source_target_pairs={{2,0},{4,6},{3,1},{5,7},{10,8},{12,14},{11,9},{13,15},{18,16},{20,... | collective-permute-start | bytes 1572872 | tf_op jit(solution)/shard_map/ppermute | solution.py:404
  37.1 6.8 %collective-permute-start.28 = (bf16[36,8,128]{2,1,0:T(8,128)(2,1)S(1)}, bf16[36,8,128]{2,1,0:T(8,128)(2,1)}, u32[]{:S(2)}, u32[]{:S(2)}) collective-permute-start(bf16[36,8,128]{2,1,0:T(8,128)(2,1)S(1)} %pad_maximum_fusion), channel_id=1, source_target_pairs={{0,1},{1,2},{2,3},{3,4},{4,5},{5,6},{6,7},{8,9},{9,10},{10,11},{11... | collective-permute-start | bytes 221192 | tf_op jit(solution)/shard_map/ppermute | solution.py:23
  43.8 13.9 %collective-permute-start.29 = (bf16[36,8,128]{2,1,0:T(8,128)(2,1)S(1)}, bf16[36,8,128]{2,1,0:T(8,128)(2,1)S(1)}, u32[]{:S(2)}, u32[]{:S(2)}) collective-permute-start(bf16[36,8,128]{2,1,0:T(8,128)(2,1)S(1)} %pad_maximum_fusion.1), channel_id=1, source_target_pairs={{1,0},{2,1},{3,2},{4,3},{5,4},{6,5},{7,6},{9,8},{10,9},{11,10},{12... | collective-permute-start | bytes 221192 | tf_op jit(solution)/shard_map/ppermute | solution.py:23
  58.3 11.0 %collective-permute-start.13 = (bf16[16,64,128]{2,1,0:T(8,128)(2,1)}, bf16[16,64,128]{2,1,0:T(8,128)(2,1)S(1)}, u32[]{:S(2)}, u32[]{:S(2)}) collective-permute-start(bf16[16,64,128]{2,1,0:T(8,128)(2,1)} %get-tuple-element.37), channel_id=1, source_target_pairs={{0,9},{1,8},{8,1},{9,0},{16,25},{17,24},{24,17},{25,16},{2,11},{3,... | collective-permute-start | bytes 786440 | tf_op jit(solution)/shard_map/ppermute | solution.py:484
  61.9 29.6 %copy-start.1 = (bf16[16,64,128]{2,1,0:T(8,128)(2,1)}, bf16[16,64,128]{2,1,0:T(8,128)(2,1)S(1)}, u32[]{:S(2)}) copy-start(bf16[16,64,128]{2,1,0:T(8,128)(2,1)S(1)} %collective-permute-done.11.refs_2_) | copy-start | bytes 786436
  61.9 20.2 %collective-permute-start.14 = (bf16[16,64,128]{2,1,0:T(8,128)(2,1)}, bf16[16,64,128]{2,1,0:T(8,128)(2,1)S(1)}, u32[]{:S(2)}, u32[]{:S(2)}) collective-permute-start(bf16[16,64,128]{2,1,0:T(8,128)(2,1)} %get-tuple-element.38), channel_id=1, source_target_pairs={{0,16},{1,17},{8,24},{9,25},{16,0},{17,1},{24,8},{25,9},{2,18},{3,... | collective-permute-start | bytes 786440 | tf_op jit(solution)/shard_map/ppermute | solution.py:484
  63.8 27.6 %copy-start.2 = (bf16[16,64,128]{2,1,0:T(8,128)(2,1)}, bf16[16,64,128]{2,1,0:T(8,128)(2,1)S(1)}, u32[]{:S(2)}) copy-start(bf16[16,64,128]{2,1,0:T(8,128)(2,1)S(1)} %collective-permute-done.12.refs_3_) | copy-start | bytes 786436
  63.8 18.2 %collective-permute-start.15 = (bf16[16,64,128]{2,1,0:T(8,128)(2,1)}, bf16[16,64,128]{2,1,0:T(8,128)(2,1)S(1)}, u32[]{:S(2)}, u32[]{:S(2)}) collective-permute-start(bf16[16,64,128]{2,1,0:T(8,128)(2,1)} %get-tuple-element.39), channel_id=1, source_target_pairs={{0,17},{1,16},{8,25},{9,24},{16,1},{17,0},{24,9},{25,8},{2,19},{3,... | collective-permute-start | bytes 786440 | tf_op jit(solution)/shard_map/ppermute | solution.py:484
  63.8 23.9 %collective-permute-start.16 = (bf16[16,64,128]{2,1,0:T(8,128)(2,1)}, bf16[16,64,128]{2,1,0:T(8,128)(2,1)}, u32[]{:S(2)}, u32[]{:S(2)}) collective-permute-start(bf16[16,64,128]{2,1,0:T(8,128)(2,1)} %get-tuple-element.40), channel_id=1, source_target_pairs={{0,24},{1,25},{8,16},{9,17},{16,8},{17,9},{24,0},{25,1},{2,26},{3,... | collective-permute-start | bytes 786440 | tf_op jit(solution)/shard_map/ppermute | solution.py:484
  69.3 48.1 %copy-start.3 = (bf16[16,64,128]{2,1,0:T(8,128)(2,1)}, bf16[16,64,128]{2,1,0:T(8,128)(2,1)S(1)}, u32[]{:S(2)}) copy-start(bf16[16,64,128]{2,1,0:T(8,128)(2,1)S(1)} %collective-permute-done.13.refs_4_) | copy-start | bytes 786436
  69.3 22.1 %collective-permute-start.17 = (bf16[16,64,128]{2,1,0:T(8,128)(2,1)}, bf16[16,64,128]{2,1,0:T(8,128)(2,1)S(1)}, u32[]{:S(2)}, u32[]{:S(2)}) collective-permute-start(bf16[16,64,128]{2,1,0:T(8,128)(2,1)} %get-tuple-element.41), channel_id=1, source_target_pairs={{0,25},{1,24},{8,17},{9,16},{16,9},{17,8},{24,1},{25,0},{2,27},{3,... | collective-permute-start | bytes 786440 | tf_op jit(solution)/shard_map/ppermute | solution.py:484
  82.0 35.4 %copy-start.4 = (bf16[16,64,128]{2,1,0:T(8,128)(2,1)}, bf16[16,64,128]{2,1,0:T(8,128)(2,1)S(1)}, u32[]{:S(2)}) copy-start(bf16[16,64,128]{2,1,0:T(8,128)(2,1)S(1)} %collective-permute-done.14.refs_5_) | copy-start | bytes 786436
  82.0 12.4 %collective-permute-start.19 = (bf16[8,64,128]{2,1,0:T(8,128)(2,1)}, bf16[8,64,128]{2,1,0:T(8,128)(2,1)S(1)}, u32[]{:S(2)}, u32[]{:S(2)}) collective-permute-start(bf16[8,64,128]{2,1,0:T(8,128)(2,1)} %get-tuple-element.42), channel_id=1, source_target_pairs={{0,1},{1,0},{8,9},{9,8},{16,17},{17,16},{24,25},{25,24},{2,3},{3,2... | collective-permute-start | bytes 393224 | tf_op jit(solution)/shard_map/ppermute | solution.py:484
  82.0 35.4 %copy-start.5 = (bf16[16,64,128]{2,1,0:T(8,128)(2,1)}, bf16[16,64,128]{2,1,0:T(8,128)(2,1)S(1)}, u32[]{:S(2)}) copy-start(bf16[16,64,128]{2,1,0:T(8,128)(2,1)S(1)} %collective-permute-done.15.refs_6_) | copy-start | bytes 786436
  82.0 12.7 %collective-permute-start.20 = (bf16[8,64,128]{2,1,0:T(8,128)(2,1)}, bf16[8,64,128]{2,1,0:T(8,128)(2,1)S(1)}, u32[]{:S(2)}, u32[]{:S(2)}) collective-permute-start(bf16[8,64,128]{2,1,0:T(8,128)(2,1)} %get-tuple-element.43), channel_id=1, source_target_pairs={{0,8},{1,9},{8,0},{9,1},{16,24},{17,25},{24,16},{25,17},{2,10},{3,... | collective-permute-start | bytes 393224 | tf_op jit(solution)/shard_map/ppermute | solution.py:484
  87.7 7.9 %collective-permute-start.21 = (bf16[8,64,128]{2,1,0:T(8,128)(2,1)}, bf16[8,64,128]{2,1,0:T(8,128)(2,1)S(1)}, u32[]{:S(2)}, u32[]{:S(2)}) collective-permute-start(bf16[8,64,128]{2,1,0:T(8,128)(2,1)} %get-tuple-element.44), channel_id=1, source_target_pairs={{0,9},{1,8},{8,1},{9,0},{16,25},{17,24},{24,17},{25,16},{2,11},{3,... | collective-permute-start | bytes 393224 | tf_op jit(solution)/shard_map/ppermute | solution.py:484
  87.8 9.6 %collective-permute-start.22 = (bf16[8,64,128]{2,1,0:T(8,128)(2,1)}, bf16[8,64,128]{2,1,0:T(8,128)(2,1)S(1)}, u32[]{:S(2)}, u32[]{:S(2)}) collective-permute-start(bf16[8,64,128]{2,1,0:T(8,128)(2,1)} %get-tuple-element.45), channel_id=1, source_target_pairs={{0,16},{1,17},{8,24},{9,25},{16,0},{17,1},{24,8},{25,9},{2,18},{3,... | collective-permute-start | bytes 393224 | tf_op jit(solution)/shard_map/ppermute | solution.py:484
  91.4 26.0 %copy-start.6 = (bf16[16,64,128]{2,1,0:T(8,128)(2,1)}, bf16[16,64,128]{2,1,0:T(8,128)(2,1)S(1)}, u32[]{:S(2)}) copy-start(bf16[16,64,128]{2,1,0:T(8,128)(2,1)S(1)} %collective-permute-done.17.refs_8_) | copy-start | bytes 786436
  91.4 6.7 %collective-permute-start.23 = (bf16[8,64,128]{2,1,0:T(8,128)(2,1)}, bf16[8,64,128]{2,1,0:T(8,128)(2,1)S(1)}, u32[]{:S(2)}, u32[]{:S(2)}) collective-permute-start(bf16[8,64,128]{2,1,0:T(8,128)(2,1)} %get-tuple-element.46), channel_id=1, source_target_pairs={{0,17},{1,16},{8,25},{9,24},{16,1},{17,0},{24,9},{25,8},{2,19},{3,... | collective-permute-start | bytes 393224 | tf_op jit(solution)/shard_map/ppermute | solution.py:484
  94.4 23.0 %copy-start.7 = (bf16[8,64,128]{2,1,0:T(8,128)(2,1)}, bf16[8,64,128]{2,1,0:T(8,128)(2,1)S(1)}, u32[]{:S(2)}) copy-start(bf16[8,64,128]{2,1,0:T(8,128)(2,1)S(1)} %collective-permute-done.19.refs_10_) | copy-start | bytes 393220
  94.4 12.7 %collective-permute-start.24 = (bf16[8,64,128]{2,1,0:T(8,128)(2,1)}, bf16[8,64,128]{2,1,0:T(8,128)(2,1)S(1)}, u32[]{:S(2)}, u32[]{:S(2)}) collective-permute-start(bf16[8,64,128]{2,1,0:T(8,128)(2,1)} %get-tuple-element.47), channel_id=1, source_target_pairs={{0,24},{1,25},{8,16},{9,17},{16,8},{17,9},{24,0},{25,1},{2,26},{3,... | collective-permute-start | bytes 393224 | tf_op jit(solution)/shard_map/ppermute | solution.py:484
  94.7 22.7 %copy-start.8 = (bf16[8,64,128]{2,1,0:T(8,128)(2,1)}, bf16[8,64,128]{2,1,0:T(8,128)(2,1)S(1)}, u32[]{:S(2)}) copy-start(bf16[8,64,128]{2,1,0:T(8,128)(2,1)S(1)} %collective-permute-done.20.refs_11_) | copy-start | bytes 393220
  94.7 13.9 %collective-permute-start.25 = (bf16[8,64,128]{2,1,0:T(8,128)(2,1)}, bf16[8,64,128]{2,1,0:T(8,128)(2,1)S(1)}, u32[]{:S(2)}, u32[]{:S(2)}) collective-permute-start(bf16[8,64,128]{2,1,0:T(8,128)(2,1)} %get-tuple-element.48), channel_id=1, source_target_pairs={{0,25},{1,24},{8,17},{9,16},{16,9},{17,8},{24,1},{25,0},{2,27},{3,... | collective-permute-start | bytes 393224 | tf_op jit(solution)/shard_map/ppermute | solution.py:484
  95.6 21.8 %copy-start.9 = (bf16[8,64,128]{2,1,0:T(8,128)(2,1)}, bf16[8,64,128]{2,1,0:T(8,128)(2,1)S(1)}, u32[]{:S(2)}) copy-start(bf16[8,64,128]{2,1,0:T(8,128)(2,1)S(1)} %collective-permute-done.21.refs_12_) | copy-start | bytes 393220
  95.6 13.6 %collective-permute-start.10 = (bf16[8,64,128]{2,1,0:T(8,128)(2,1)}, bf16[8,64,128]{2,1,0:T(8,128)(2,1)S(1)}, u32[]{:S(2)}, u32[]{:S(2)}) collective-permute-start(bf16[8,64,128]{2,1,0:T(8,128)(2,1)} %get-tuple-element.34), channel_id=1, source_target_pairs={{0,25},{1,24},{8,17},{9,16},{16,9},{17,8},{24,1},{25,0},{2,27},{3,... | collective-permute-start | bytes 393224 | tf_op jit(solution)/shard_map/ppermute | solution.py:484
  97.4 20.1 %copy-start.10 = (bf16[8,64,128]{2,1,0:T(8,128)(2,1)}, bf16[8,64,128]{2,1,0:T(8,128)(2,1)S(1)}, u32[]{:S(2)}) copy-start(bf16[8,64,128]{2,1,0:T(8,128)(2,1)S(1)} %collective-permute-done.22.refs_13_) | copy-start | bytes 393220
  97.4 12.7 %collective-permute-start.4 = (bf16[8,64,128]{2,1,0:T(8,128)(2,1)}, bf16[8,64,128]{2,1,0:T(8,128)(2,1)S(1)}, u32[]{:S(2)}, u32[]{:S(2)}) collective-permute-start(bf16[8,64,128]{2,1,0:T(8,128)(2,1)} %get-tuple-element.28), channel_id=1, source_target_pairs={{0,1},{1,0},{8,9},{9,8},{16,17},{17,16},{24,25},{25,24},{2,3},{3,2... | collective-permute-start | bytes 393224 | tf_op jit(solution)/shard_map/ppermute | solution.py:484
  98.1 19.4 %copy-start.11 = (bf16[8,64,128]{2,1,0:T(8,128)(2,1)}, bf16[8,64,128]{2,1,0:T(8,128)(2,1)S(1)}, u32[]{:S(2)}) copy-start(bf16[8,64,128]{2,1,0:T(8,128)(2,1)S(1)} %collective-permute-done.23.refs_14_) | copy-start | bytes 393220
  98.1 25.4 %collective-permute-start.5 = (bf16[8,64,128]{2,1,0:T(8,128)(2,1)}, bf16[8,64,128]{2,1,0:T(8,128)(2,1)S(1)}, u32[]{:S(2)}, u32[]{:S(2)}) collective-permute-start(bf16[8,64,128]{2,1,0:T(8,128)(2,1)} %get-tuple-element.29), channel_id=1, source_target_pairs={{0,8},{1,9},{8,0},{9,1},{16,24},{17,25},{24,16},{25,17},{2,10},{3,... | collective-permute-start | bytes 393224 | tf_op jit(solution)/shard_map/ppermute | solution.py:484
  107.1 10.4 %copy-start.12 = (bf16[8,64,128]{2,1,0:T(8,128)(2,1)}, bf16[8,64,128]{2,1,0:T(8,128)(2,1)S(1)}, u32[]{:S(2)}) copy-start(bf16[8,64,128]{2,1,0:T(8,128)(2,1)S(1)} %collective-permute-done.24.refs_15_) | copy-start | bytes 393220
  107.1 16.4 %collective-permute-start.6 = (bf16[8,64,128]{2,1,0:T(8,128)(2,1)}, bf16[8,64,128]{2,1,0:T(8,128)(2,1)S(1)}, u32[]{:S(2)}, u32[]{:S(2)}) collective-permute-start(bf16[8,64,128]{2,1,0:T(8,128)(2,1)} %get-tuple-element.30), channel_id=1, source_target_pairs={{0,9},{1,8},{8,1},{9,0},{16,25},{17,24},{24,17},{25,16},{2,11},{3,... | collective-permute-start | bytes 393224 | tf_op jit(solution)/shard_map/ppermute | solution.py:484
  108.6 8.9 %copy-start.13 = (bf16[8,64,128]{2,1,0:T(8,128)(2,1)}, bf16[8,64,128]{2,1,0:T(8,128)(2,1)S(1)}, u32[]{:S(2)}) copy-start(bf16[8,64,128]{2,1,0:T(8,128)(2,1)S(1)} %collective-permute-done.25.refs_16_) | copy-start | bytes 393220
  108.6 15.0 %collective-permute-start.7 = (bf16[8,64,128]{2,1,0:T(8,128)(2,1)}, bf16[8,64,128]{2,1,0:T(8,128)(2,1)S(1)}, u32[]{:S(2)}, u32[]{:S(2)}) collective-permute-start(bf16[8,64,128]{2,1,0:T(8,128)(2,1)} %get-tuple-element.31), channel_id=1, source_target_pairs={{0,16},{1,17},{8,24},{9,25},{16,0},{17,1},{24,8},{25,9},{2,18},{3,... | collective-permute-start | bytes 393224 | tf_op jit(solution)/shard_map/ppermute | solution.py:484
  109.2 14.3 %copy-start.17 = (bf16[8,64,128]{2,1,0:T(8,128)(2,1)}, bf16[8,64,128]{2,1,0:T(8,128)(2,1)S(1)}, u32[]{:S(2)}) copy-start(bf16[8,64,128]{2,1,0:T(8,128)(2,1)S(1)} %collective-permute-done.10.refs_7_) | copy-start | bytes 393220
  109.2 14.4 %collective-permute-start.8 = (bf16[8,64,128]{2,1,0:T(8,128)(2,1)}, bf16[8,64,128]{2,1,0:T(8,128)(2,1)S(1)}, u32[]{:S(2)}, u32[]{:S(2)}) collective-permute-start(bf16[8,64,128]{2,1,0:T(8,128)(2,1)} %get-tuple-element.32), channel_id=1, source_target_pairs={{0,17},{1,16},{8,25},{9,24},{16,1},{17,0},{24,9},{25,8},{2,19},{3,... | collective-permute-start | bytes 393224 | tf_op jit(solution)/shard_map/ppermute | solution.py:484
  110.1 13.5 %copy-start.18 = (bf16[8,64,128]{2,1,0:T(8,128)(2,1)}, bf16[8,64,128]{2,1,0:T(8,128)(2,1)S(1)}, u32[]{:S(2)}) copy-start(bf16[8,64,128]{2,1,0:T(8,128)(2,1)S(1)} %collective-permute-done.4.refs_1_) | copy-start | bytes 393220
  110.1 13.5 %collective-permute-start.9 = (bf16[8,64,128]{2,1,0:T(8,128)(2,1)}, bf16[8,64,128]{2,1,0:T(8,128)(2,1)S(1)}, u32[]{:S(2)}, u32[]{:S(2)}) collective-permute-start(bf16[8,64,128]{2,1,0:T(8,128)(2,1)} %get-tuple-element.33), channel_id=1, source_target_pairs={{0,24},{1,25},{8,16},{9,17},{16,8},{17,9},{24,0},{25,1},{2,26},{3,... | collective-permute-start | bytes 393224 | tf_op jit(solution)/shard_map/ppermute | solution.py:484
  (7 other events, 5.0 us)
where the time goes:
time: 139 us; the launch traced here: 138 us
  starting transfers between devices  48.9 us (35%)
  waiting for transfers between devices  40.2 us (29%)
  Pallas kernels  38.1 us (27%)
  local copies, waits for them, and re-layouts  6.57 us (5%)
  other arithmetic  3.99 us (3%)
    ppermute x21, waiting for transfers between devices, block(): lax.ppermute(part, ('rows', 'x'), [(i, i ^ far) for i in range(peers)])  24.5 us
    ppermute x21, starting transfers between devices, block(): lax.ppermute(part, ('rows', 'x'), [(i, i ^ far) for i in range(peers)])  22.4 us
    pallas_call x1, Pallas kernels, tail(): pl.pallas_call(functools.partial(tail_kernel, side, picks, batch, early,...  13.7 us
    ppermute x2, waiting for transfers between devices, from_sides(): lax.ppermute(low, axis, backward)  10.2 us
    ppermute x5, starting transfers between devices, hop(): return lax.ppermute(block, 'z', pairs)  9.47 us
    pallas_call x3, Pallas kernels, pack(): pl.pallas_call(functools.partial(pack_kernel, chunks, capacity, layers),...  8.85 us
    ppermute x2, starting transfers between devices, from_sides(): lax.ppermute(high, axis, forward)  6.79 us
    pallas_call x1, Pallas kernels, collect(): pl.pallas_call(functools.partial(collect_kernel, len(sources)), grid_spec...  6 us
  transfers between devices with their start and end apart: 31, of which 7 were waited for; matrix products, arithmetic and copies ran while one was open for 6% of the time, Pallas kernels for 15%

commit v1 on v0

--- a/solution.py
+++ b/solution.py
@@ -23,14 +23,12 @@
     return lax.ppermute(high, axis, forward), lax.ppermute(low, axis, backward)
 
 
-def halo(image, margin, border):
-    above, below = from_sides(image[:margin], image[-margin:], "rows")
-    edges = lambda columns: jnp.concatenate(
-        [above[:, columns], image[:, columns], below[:, columns]], axis=0
-    )
-    left, right = from_sides(
-        edges(slice(0, border)), edges(slice(image.shape[1] - border, None)), ("z", "x")
-    )
+def halo(top, bottom, left, right):
+    border = left.shape[1]
+    above, below = from_sides(top, bottom, "rows")
+    low = jnp.concatenate([above[:, :border], left, below[:, :border]], axis=0)
+    high = jnp.concatenate([above[:, -border:], right, below[:, -border:]], axis=0)
+    left, right = from_sides(low, high, ("z", "x"))
     return above, below, left, right
 
 
@@ -58,14 +56,29 @@
     )
 
 
-def norm_kernel(side, image_ref, gain_ref, out_ref):
-    normed = normalize(image_ref[...].astype(F32), gain_ref[...])
+def norm_kernel(side, image_ref, gain_ref, out_ref, top_ref, bottom_ref, left_ref, right_ref):
+    step = pl.program_id(0)
+    tokens = image_ref[...]
+    normed = normalize(tokens.astype(F32), gain_ref[...])
     out_ref[...] = regions_of(normed, side).astype(BF16).reshape(out_ref.shape)
-
-
-def norm_regions(image, gain, side):
+    margin, width, border = top_ref.shape[0], tokens.shape[1], left_ref.shape[1]
+    left_ref[...] = image_ref[:, pl.ds(0, border), :]
+    right_ref[...] = image_ref[:, pl.ds(width - border, border), :]
+
+    @pl.when(step == 0)
+    def _():
+        top_ref[...] = image_ref[pl.ds(0, margin)]
+
+    @pl.when(step == pl.num_programs(0) - 1)
+    def _():
+        bottom_ref[...] = image_ref[pl.ds(side - margin, margin)]
+
+
+def norm_regions(image, gain, side, margin, border):
     height, width, channels = image.shape
     per_row = width // side
+    edge = jax.ShapeDtypeStruct((margin, width, channels), BF16)
+    flank = jax.ShapeDtypeStruct((height, border, channels), BF16)
     return pl.pallas_call(
         functools.partial(norm_kernel, side),
         grid=(height // side,),
@@ -73,10 +86,20 @@
             pl.BlockSpec((side, width, channels), lambda i: (i, 0, 0)),
             pl.BlockSpec((1, channels), lambda i: (0, 0)),
         ],
-        out_specs=pl.BlockSpec((per_row, side * side, channels), lambda i: (i, 0, 0)),
-        out_shape=jax.ShapeDtypeStruct(
-            (height // side * per_row, side * side, channels), BF16
-        ),
+        out_specs=[
+            pl.BlockSpec((per_row, side * side, channels), lambda i: (i, 0, 0)),
+            pl.BlockSpec(edge.shape, lambda i: (0, 0, 0)),
+            pl.BlockSpec(edge.shape, lambda i: (0, 0, 0)),
+            pl.BlockSpec((side, border, channels), lambda i: (i, 0, 0)),
+            pl.BlockSpec((side, border, channels), lambda i: (i, 0, 0)),
+        ],
+        out_shape=[
+            jax.ShapeDtypeStruct((height // side * per_row, side * side, channels), BF16),
+            edge,
+            edge,
+            flank,
+            flank,
+        ],
         cost_estimate=pl.CostEstimate(
             flops=10 * image.size, bytes_accessed=4 * image.size, transcendentals=0
         ),
@@ -158,55 +181,89 @@
     )(*operands)
 
 
-def pack_kernel(chunks, capacity, layers, here_ref, wanted_ref, *refs):
-    sources, out_refs = refs[: len(chunks)], refs[len(chunks) :]
-    for distance, out_ref in enumerate(out_refs, 1):
-        for place, (chunk, source_ref) in enumerate(zip(chunks, sources)):
-            base = ((here_ref[0] ^ distance) * layers + (here_ref[1] ^ chunk)) * capacity
+def is_inside(layer):
+    return (layer == 1) | (layer == 2)
+
+
+def pack_kernel(chunks, capacity, joint, place_of, wanted_ref, *refs):
+    peer, layer = place_of()
+    count = sum(options for _, options in chunks)
+    sources, out_refs = refs[:count], refs[count:]
+    distances = range(1, out_refs[0].shape[0] if joint else len(out_refs) + 1)
+    inside = is_inside(layer)
+
+    def fill(source_ref, chunk, place):
+        for distance in distances:
+            other = peer ^ distance
             for slot in range(capacity):
-                out_ref[place * capacity + slot] = source_ref[wanted_ref[base + slot]]
-
-
-def pack(sources, here, wanted, chunks, peers, layers, capacity):
+                region = source_ref[wanted_ref[other, 0, (layer ^ chunk) * capacity + slot]]
+                if joint:
+                    out_refs[0][other, place * capacity + slot] = region
+                else:
+                    out_refs[distance - 1][place * capacity + slot] = region
+
+    at = 0
+    for place, (chunk, options) in enumerate(chunks):
+        if options == 1:
+            fill(sources[at], chunk, place)
+        else:
+            pl.when(inside)(functools.partial(fill, sources[at], chunk, place))
+            pl.when(~inside)(functools.partial(fill, sources[at + 1], chunk, place))
+        at += options
+
+
+def pack(chunks, place_of, wanted, peers, capacity, joint):
+    sources = sum(chunks.values(), [])
     tile = sources[0].shape
     shape = (capacity * len(chunks), *tile[1:])
-    count = peers - 1
+    shapes = [(peers, *shape)] if joint else [shape] * (peers - 1)
     return pl.pallas_call(
-        functools.partial(pack_kernel, chunks, capacity, layers),
-        grid_spec=pltpu.PrefetchScalarGridSpec(
-            num_scalar_prefetch=2,
-            grid=(1,),
-            in_specs=[pl.BlockSpec(tile, lambda i, *_: (0, 0, 0))] * len(chunks),
-            out_specs=[pl.BlockSpec(shape, lambda i, *_: (0, 0, 0))] * count,
-        ),
-        out_shape=[jax.ShapeDtypeStruct(shape, BF16)] * count,
+        functools.partial(
+            pack_kernel, tuple((k, len(v)) for k, v in chunks.items()), capacity, joint, place_of
+        ),
+        in_specs=[pl.BlockSpec(memory_space=pltpu.SMEM)]
+        + [pl.BlockSpec(memory_space=pltpu.VMEM)] * len(sources),
+        out_specs=[pl.BlockSpec(memory_space=pltpu.VMEM)] * len(shapes),
+        out_shape=[jax.ShapeDtypeStruct(a, BF16) for a in shapes],
         cost_estimate=pl.CostEstimate(
-            flops=0, bytes_accessed=4 * count * math.prod(shape), transcendentals=0
+            flops=0, bytes_accessed=4 * peers * math.prod(shape), transcendentals=0
         ),
         name="pack",
-    )(here, wanted, *sources)
-
-
-def load_all(sources, landed, sems):
-    copies, start = [], 0
-    for i, source in enumerate(sources):
-        copies.append(
-            pltpu.make_async_copy(source, landed.at[pl.ds(start, source.shape[0])], sems.at[i])
-        )
-        start += source.shape[0]
-    for copy in copies:
-        copy.start()
-    for copy in copies:
+    )(wanted, *sources)
+
+
+def load_all(options, sources, landed, sems, layer):
+    waits, start, at = [], 0, 0
+    inside = is_inside(layer)
+    for i, count in enumerate(options):
+        size = sources[at].shape[0]
+        copies = [
+            pltpu.make_async_copy(source, landed.at[pl.ds(start, size)], sems.at[i])
+            for source in sources[at : at + count]
+        ]
+        if count == 1:
+            copies[0].start()
+        else:
+            pl.when(inside)(copies[0].start)
+            pl.when(~inside)(copies[1].start)
+        waits.append(copies[0])
+        start += size
+        at += count
+    for copy in waits:
         copy.wait()
 
 
-def collect_kernel(count, position_ref, *refs):
-    sources, out_ref, landed, sems = refs[:count], refs[count], refs[-2], refs[-1]
+def rows_of(sources):
+    return sum(options[0].shape[0] for options in sources)
+
+
+def collect_kernel(options, place_of, position_ref, *refs):
+    sources, out_ref, landed, sems = refs[: sum(options)], refs[-3], refs[-2], refs[-1]
     step = pl.program_id(0)
 
     @pl.when(step == 0)
     def _():
-        load_all(sources, landed, sems)
+        load_all(options, sources, landed, sems, place_of()[1])
 
     total = landed.shape[0]
     per_step = out_ref.shape[0]
@@ -215,16 +272,17 @@
         out_ref[i] = landed[jnp.where(at < total, at, 0)]
 
 
-def collect(position, sources, steps):
-    shape = sources[0].shape[1:]
-    total = sum(source.shape[0] for source in sources)
+def collect(position, sources, place_of, steps):
+    shape = sources[0][0].shape[1:]
+    total = rows_of(sources)
     pairs = position.shape[0]
+    flat = sum(sources, [])
     return pl.pallas_call(
-        functools.partial(collect_kernel, len(sources)),
+        functools.partial(collect_kernel, tuple(map(len, sources)), place_of),
         grid_spec=pltpu.PrefetchScalarGridSpec(
             num_scalar_prefetch=1,
             grid=(steps,),
-            in_specs=[pl.BlockSpec(memory_space=pl.ANY)] * len(sources),
+            in_specs=[pl.BlockSpec(memory_space=pl.ANY)] * len(flat),
             out_specs=pl.BlockSpec((pairs // steps, *shape), lambda i, _: (i, 0, 0)),
             scratch_shapes=[
                 pltpu.VMEM((total, *shape), BF16),
@@ -236,7 +294,7 @@
             flops=0, bytes_accessed=2 * (total + pairs) * math.prod(shape), transcendentals=0
         ),
         name="collect",
-    )(position, *sources)
+    )(position, *flat)
 
 
 def project(fetched, weight_ref):
@@ -274,7 +332,8 @@
     return lifted * (0.5 + 0.5 * jnp.tanh(inner))
 
 
-def tail_kernel(side, picks, batch, early, late_count, position_ref, *refs):
+def tail_kernel(side, picks, batch, early, options, place_of, position_ref, *refs):
+    late_count = sum(options)
     late = refs[:late_count]
     (
         fetched_ref,
@@ -297,7 +356,7 @@
     @pl.when(step == 0)
     def _():
         combined_ref[...] = jnp.zeros_like(combined_ref)
-        load_all(late, landed, sems)
+        load_all(options, late, landed, sems, place_of()[1])
 
     area, channels = fetched_ref.shape[1:]
     exponent = (channels // HEADS) ** (-0.5) * math.log2(math.e)
@@ -353,7 +412,7 @@
         lines = [line for line in lines if next(line, None) is not None]
 
 
-def tail(position, early, fetched, late, queries, context, image, weights, side, picks):
+def tail(position, early, fetched, late, place_of, queries, context, image, weights, side, picks):
     height, width, channels = image.shape
     area = side * side
     per_row = width // side
@@ -369,13 +428,16 @@
         lambda i, position: (before(i) // halves, before(i) % halves, 0),
     )
     regions = pl.BlockSpec((batch * picks, area, channels), lambda i, position: (now(i), 0, 0))
-    total = sum(a.shape[0] for a in late)
+    total = rows_of(late)
+    flat = sum(late, [])
     return pl.pallas_call(
-        functools.partial(tail_kernel, side, picks, batch, early, len(late)),
+        functools.partial(
+            tail_kernel, side, picks, batch, early, tuple(map(len, late)), place_of
+        ),
         grid_spec=pltpu.PrefetchScalarGridSpec(
             num_scalar_prefetch=1,
             grid=(steps + 1,),
-            in_specs=[pl.BlockSpec(memory_space=pl.ANY)] * len(late)
+            in_specs=[pl.BlockSpec(memory_space=pl.ANY)] * len(flat)
             + [regions, tokens, tokens, strip]
             + [full(w) for w in weights],
             out_specs=strip,
@@ -390,13 +452,13 @@
             flops=image.size * 4000, bytes_accessed=16 * image.size, transcendentals=40 * image.size
         ),
         name="tail",
-    )(position, *late, fetched, queries, context, image, *weights)
-
-
-def layer_blocks(block, layer, layers):
+    )(position, *flat, fetched, queries, context, image, *weights)
+
+
+def layer_blocks(block, layers):
     if layers != 4:
-        return [block] + [
-            lax.ppermute(block, "z", [(i, i ^ step) for i in range(layers)])
+        return [[block]] + [
+            [lax.ppermute(block, "z", [(i, i ^ step) for i in range(layers)])]
             for step in range(1, layers)
         ]
 
@@ -408,13 +470,7 @@
     middle_two = hop(beside, [(1, 2), (2, 1)])
     ends_two = hop(middle, [(1, 0), (2, 3)])
     ends_three = hop(middle_two, [(1, 0), (2, 3)])
-    inside = (layer == 1) | (layer == 2)
-    return [
-        block,
-        beside,
-        jnp.where(inside, middle_two, ends_two),
-        jnp.where(inside, middle, ends_three),
-    ]
+    return [[block], [beside], [middle_two, ends_two], [middle, ends_three]]
 
 
 def block(
@@ -431,9 +487,11 @@
     all_cols = region_cols * layers * across
 
     regions = region_rows * region_cols
-    peer = lax.axis_index("rows") * across + lax.axis_index("x")
-    layer = lax.axis_index("z")
-    here = jnp.stack([peer, layer])
+
+    def place_of():
+        return lax.axis_index("rows") * across + lax.axis_index("x"), lax.axis_index("z")
+
+    peer, layer = place_of()
 
     targets = routes.reshape(pair_count)
     target_row = targets // all_cols
@@ -450,46 +508,50 @@
     chunk = owner_layer ^ layer
     groups = [(0, 1), *((step,) for step in range(2, layers))]
     position, start = jnp.zeros_like(slot), 0
-    for members in groups:
+    for number, members in enumerate(groups):
+        joint = number == 0
         replies = start + len(members) * regions
+        sender = owner_peer if joint else distance - 1
         for place, step in enumerate(members):
             here_at = start + place * regions + local_index
-            sent_at = (
-                replies + ((distance - 1) * len(members) + place) * capacity + slot
-            )
+            sent_at = replies + (sender * len(members) + place) * capacity + slot
             position = jnp.where(
                 chunk == step, jnp.where(distance == 0, here_at, sent_at), position
             )
         early = start
-        start = replies + (peers - 1) * len(members) * capacity
-    asked = owners * capacity + slot
-    slots = jnp.arange(devices * capacity, dtype=jnp.int32)
+        start = replies + (peers - 1 + joint) * len(members) * capacity
+    lanes = -(-layers * capacity // 128) * 128
+    asked = owner_peer * lanes + owner_layer * capacity + slot
+    slots = jnp.arange(peers * lanes, dtype=jnp.int32)
     requests = jnp.sum(
         jnp.where(asked[None, :] == slots[:, None], local_index[None, :], 0), axis=1
     )
     wanted = lax.all_to_all(
-        requests.reshape(peers, layers * capacity), ("rows", "x"), 0, 0, tiled=True
-    ).reshape(-1)
-
-    normed = norm_regions(image, norm_gain, side)
-
-    held = layer_blocks(normed, layer, layers)
+        requests.reshape(peers, 1, lanes), ("rows", "x"), 0, 0, tiled=True
+    )
+
+    margin = (lce_weight.shape[0] - 1) // 2
+    normed, *edges = norm_regions(image, norm_gain, side, margin, 8)
+
+    held = layer_blocks(normed, layers)
     arrived = []
-    for members in groups:
-        sources = [held[step] for step in members]
-        packed = pack(sources, here, wanted, members, peers, layers, capacity)
-        arrived.append(
-            sources
-            + [
+    for number, members in enumerate(groups):
+        chunks = {step: held[step] for step in members}
+        joint = number == 0
+        packed = pack(chunks, place_of, wanted, peers, capacity, joint)
+        if joint:
+            got = lax.all_to_all(packed[0], ("rows", "x"), 0, 0, tiled=True)
+            got = [got.reshape(-1, *normed.shape[1:])]
+        else:
+            got = [
                 lax.ppermute(part, ("rows", "x"), [(i, i ^ far) for i in range(peers)])
                 for far, part in enumerate(packed, 1)
             ]
-        )
+        arrived.append([*chunks.values(), *([part] for part in got)])
     late = arrived.pop()
-    fetched = collect(position, sum(arrived, []), math.gcd(pair_count, 8))
-
-    margin = (lce_weight.shape[0] - 1) // 2
-    around = halo(image, margin, 8)
+    fetched = collect(position, sum(arrived, []), place_of, math.gcd(pair_count, 8))
+
+    around = halo(*edges)
     context, queries = context_and_queries(
         image, around, norm_gain, qkv_weight, lce_weight, side, margin
     )
@@ -500,7 +562,7 @@
         up_weight,
         down_weight,
     )
-    return tail(position, early, fetched, late, queries, context, image, weights, side, pick_count)
+    return tail(position, early, fetched, late, place_of, queries, context, image, weights, side, pick_count)
 
 
 def solution(mesh):

time: 139 us -> 121 us (0.87)
  waiting for transfers between devices: 40.2 us -> 23.6 us
  blocking collectives: 0 us -> 8.57 us
  other arithmetic: 3.99 us -> 1.06 us
  local copies, waits for them, and re-layouts: 6.57 us -> 3.86 us
  starting transfers between devices: 48.9 us -> 46.4 us
    ppermute x21 -> x14, waiting for transfers between devices: 24.5 us -> 7.43 us  [block(): lax.ppermute(part, ('rows', 'x'), [(i, i ^ far) for i in range(peers)])]
    ppermute x2, waiting for transfers between devices: 10.2 us -> 1.05 us  [from_sides(): lax.ppermute(low, axis, backward)]
    all_to_all x0 -> x1, blocking collectives: none -> 8.57 us  [block(): lax.all_to_all(requests.reshape(peers, 1, lanes), ('rows', 'x'), 0, 0, ti...]
    ppermute x5, waiting for transfers between devices: 1.95 us -> 8.57 us  [hop(): return lax.ppermute(block, 'z', pairs)]
    ppermute x21 -> x14, starting transfers between devices: 22.4 us -> 19 us  [block(): lax.ppermute(part, ('rows', 'x'), [(i, i ^ far) for i in range(peers)])]
    ppermute x2, waiting for transfers between devices: 3.5 us -> 6.54 us  [from_sides(): lax.ppermute(high, axis, forward)]
    select_n x2 -> x0, other arithmetic: 1.73 us -> none  [the longest x1 0.87 us: layer_blocks(): jnp.where(inside, middle, ends_three)]
    slice x4 -> x2, local copies, waits for them, and re-layouts: 1.67 us -> 0.01 us  [halo(): low = jnp.concatenate([above[:, :border], left, below[:, :border]], axis=0)]
  transfers between devices with their start and end apart: 31 -> 24, of which waited for: 7 -> 6; matrix products, arithmetic and copies ran while one was open for 6% -> 2% of each run, Pallas kernels for 15% -> 14%
where the time goes in v1:
time: 121 us
  starting transfers between devices  46.4 us (38%)
  Pallas kernels  36.9 us (30%)
  waiting for transfers between devices  23.6 us (20%)
  blocking collectives  8.57 us (7%)
  local copies, waits for them, and re-layouts  3.86 us (3%)
    ppermute x14, starting transfers between devices, block(): lax.ppermute(part, ('rows', 'x'), [(i, i ^ far) for i in range(peers)])  19 us
    pallas_call x1, Pallas kernels, tail(): pl.pallas_call(functools.partial(tail_kernel, side, picks, batch, early,...  13.7 us
    ppermute x5, starting transfers between devices, hop(): return lax.ppermute(block, 'z', pairs)  10 us
    all_to_all x1, blocking collectives, block(): lax.all_to_all(requests.reshape(peers, 1, lanes), ('rows', 'x'), 0, 0, ti...  8.57 us
    ppermute x5, waiting for transfers between devices, hop(): return lax.ppermute(block, 'z', pairs)  8.57 us
    pallas_call x3, Pallas kernels, pack(): pl.pallas_call(functools.partial(pack_kernel, tuple(((k, len(v)) for k, v...  7.5 us
    ppermute x14, waiting for transfers between devices, block(): lax.ppermute(part, ('rows', 'x'), [(i, i ^ far) for i in range(peers)])  7.43 us
    ppermute x2, starting transfers between devices, from_sides(): lax.ppermute(high, axis, forward)  6.99 us
  transfers between devices with their start and end apart: 24, of which 6 were waited for; matrix products, arithmetic and copies ran while one was open for 2% of the time, Pallas kernels for 14%

profile of v1, /device:TPU:17, one launch (start us, length us, event | category | flops | bytes accessed | tf_op | source)
XLA Modules:
  0.0 120.8 jit_solution(8412408587756468241)
XLA Ops:
  0.0 3.6 %norm_regions.1 = (bf16[32,64,128]{2,1,0:T(8,128)(2,1)}, bf16[2,64,128]{2,1,0:T(8,128)(2,1)}, bf16[2,64,128]{2,1,0:T(8,128)(2,1)}, bf16[32,8,128]{2,1,0:T(8,128)(2,1)}, bf16[32,8,128]{2,1,0:T(8,128)(2,1)}) custom-call(bf16[32,64,128]{2,1,0:T(8,128)(2,1)} %refs_12_.1, f32[1,128]{1,0:T(1,128)} %bitcast.6), custom_call_target="tpu_custom_call" | custom-call | flops 2621440 | bytes 1048576 | tf_op jit(solution)/shard_map/norm_regions/pallas_call | solution.py:82
  3.7 1.4 %collective-permute-start.1 = (bf16[32,64,128]{2,1,0:T(8,128)(2,1)}, bf16[32,64,128]{2,1,0:T(8,128)(2,1)S(1)}, u32[]{:S(2)}, u32[]{:S(2)}) collective-permute-start(bf16[32,64,128]{2,1,0:T(8,128)(2,1)} %get-tuple-element.26.refs_0_), channel_id=1, source_target_pairs={{0,2},{2,0},{4,6},{6,4},{1,3},{3,1},{5,7},{7,5},{8,10},{10,8},{12,... | collective-permute-start | bytes 1572872 | tf_op jit(solution)/shard_map/ppermute | solution.py:466
  5.0 0.8 copy.12
  5.8 0.1 reshape.292
  6.0 0.2 convert_reduce_fusion
  6.1 0.6 compare_select_fusion.3
  6.8 0.2 select_reduce_fusion
  7.0 8.6 %all_to_all.10.wanted_ref = s32[8,1,128]{2,1,0:T(1,128)} all-to-all(s32[8,1,128]{2,1,0:T(1,128)S(1)} %bitcast.5), channel_id=1, replica_groups=mesh['rows'=4,'z'=4,'x'=2] {'rows','x'}, dimensions={0} | all-to-all | bytes 8192 | tf_op jit(solution)/shard_map/all_to_all | solution.py:529
  15.5 1.2 collective-permute-done.1.refs_1_
  16.7 0.8 copy-done.4
  17.5 2.9 %pack.4 = bf16[8,16,64,128]{3,2,1,0:T(8,128)(2,1)} custom-call(s32[8,1,128]{2,1,0:T(1,128)} %all_to_all.10.wanted_ref, bf16[32,64,128]{2,1,0:T(8,128)(2,1)} %get-tuple-element.26.refs_0_, bf16[32,64,128]{2,1,0:T(8,128)(2,1)} %copy-done.4), custom_call_target="tpu_custom_call" | custom-call | bytes 4194304 | tf_op jit(solution)/shard_map/pack/pallas_call | solution.py:220
  20.5 5.4 %all-to-all-start.1 = ((bf16[8,16,64,128]{3,2,1,0:T(8,128)(2,1)}), bf16[8,16,64,128]{3,2,1,0:T(8,128)(2,1)S(1)}, u32[]{:S(2)}, u32[]{:S(2)}) async-start(bf16[8,16,64,128]{3,2,1,0:T(8,128)(2,1)} %pack.4), calls=%async_computation.1 | async-start | bytes 4194304 | tf_op jit(solution)/shard_map/all_to_all | solution.py:543
  25.9 2.1 %collective-permute-start = (bf16[32,64,128]{2,1,0:T(8,128)(2,1)S(1)}, bf16[32,64,128]{2,1,0:T(8,128)(2,1)S(1)}, u32[]{:S(2)}, u32[]{:S(2)}) collective-permute-start(bf16[32,64,128]{2,1,0:T(8,128)(2,1)S(1)} %copy-done.3), channel_id=1, source_target_pairs={{2,4},{4,2},{3,5},{5,3},{10,12},{12,10},{11,13},{13,11},{18,20},{2... | collective-permute-start | bytes 1572872 | tf_op jit(solution)/shard_map/ppermute | solution.py:466
  27.9 3.2 %collective-permute-start.2 = (bf16[32,64,128]{2,1,0:T(8,128)(2,1)}, bf16[32,64,128]{2,1,0:T(8,128)(2,1)S(1)}, u32[]{:S(2)}, u32[]{:S(2)}) collective-permute-start(bf16[32,64,128]{2,1,0:T(8,128)(2,1)} %copy-done.4), channel_id=1, source_target_pairs={{2,4},{4,2},{3,5},{5,3},{10,12},{12,10},{11,13},{13,11},{18,20},{2... | collective-permute-start | bytes 1572872 | tf_op jit(solution)/shard_map/ppermute | solution.py:466
  31.2 4.1 %collective-permute-start.19 = (bf16[2,64,128]{2,1,0:T(8,128)(2,1)S(1)}, bf16[2,64,128]{2,1,0:T(8,128)(2,1)S(1)}, u32[]{:S(2)}, u32[]{:S(2)}) collective-permute-start(bf16[2,64,128]{2,1,0:T(8,128)(2,1)S(1)} %copy-done.22), channel_id=1, source_target_pairs={{0,8},{8,16},{16,24},{1,9},{9,17},{17,25},{2,10},{10,18},{18,26},{... | collective-permute-start | bytes 98312 | tf_op jit(solution)/shard_map/ppermute | solution.py:23
  35.3 1.9 %collective-permute-start.20 = (bf16[2,64,128]{2,1,0:T(8,128)(2,1)S(1)}, bf16[2,64,128]{2,1,0:T(8,128)(2,1)S(1)}, u32[]{:S(2)}, u32[]{:S(2)}) collective-permute-start(bf16[2,64,128]{2,1,0:T(8,128)(2,1)S(1)} %copy-done.21), channel_id=1, source_target_pairs={{8,0},{16,8},{24,16},{9,1},{17,9},{25,17},{10,2},{18,10},{26,18},{... | collective-permute-start | bytes 98312 | tf_op jit(solution)/shard_map/ppermute | solution.py:23
  37.2 4.0 %collective-permute-done.refs_0_ = bf16[32,64,128]{2,1,0:T(8,128)(2,1)S(1)} collective-permute-done((bf16[32,64,128]{2,1,0:T(8,128)(2,1)S(1)}, bf16[32,64,128]{2,1,0:T(8,128)(2,1)S(1)}, u32[]{:S(2)}, u32[]{:S(2)}) %collective-permute-start) | collective-permute-done | bytes 524320 | tf_op jit(solution)/shard_map/ppermute | solution.py:466
  41.2 1.3 %collective-permute-start.11 = (bf16[32,64,128]{2,1,0:T(8,128)(2,1)S(1)}, bf16[32,64,128]{2,1,0:T(8,128)(2,1)S(1)}, u32[]{:S(2)}, u32[]{:S(2)}) collective-permute-start(bf16[32,64,128]{2,1,0:T(8,128)(2,1)S(1)} %collective-permute-done.refs_0_), channel_id=1, source_target_pairs={{2,0},{4,6},{3,1},{5,7},{10,8},{12,14},{11,9},{13,15},{18,16},{20,... | collective-permute-start | bytes 1572872 | tf_op jit(solution)/shard_map/ppermute | solution.py:466
  42.5 6.5 %collective-permute-done.19.above_ref = bf16[2,64,128]{2,1,0:T(8,128)(2,1)S(1)} collective-permute-done((bf16[2,64,128]{2,1,0:T(8,128)(2,1)S(1)}, bf16[2,64,128]{2,1,0:T(8,128)(2,1)S(1)}, u32[]{:S(2)}, u32[]{:S(2)}) %collective-permute-start.19) | collective-permute-done | bytes 32800 | tf_op jit(solution)/shard_map/ppermute | solution.py:23
  49.1 3.4 %collective-permute-done.2.refs_0_.refs_3_ = bf16[32,64,128]{2,1,0:T(8,128)(2,1)S(1)} collective-permute-done((bf16[32,64,128]{2,1,0:T(8,128)(2,1)}, bf16[32,64,128]{2,1,0:T(8,128)(2,1)S(1)}, u32[]{:S(2)}, u32[]{:S(2)}) %collective-permute-start.2) | collective-permute-done | bytes 524320 | tf_op jit(solution)/shard_map/ppermute | solution.py:466
  52.4 2.1 %collective-permute-start.3 = (bf16[32,64,128]{2,1,0:T(8,128)(2,1)S(1)}, bf16[32,64,128]{2,1,0:T(8,128)(2,1)}, u32[]{:S(2)}, u32[]{:S(2)}) collective-permute-start(bf16[32,64,128]{2,1,0:T(8,128)(2,1)S(1)} %collective-permute-done.2.refs_0_.refs_3_), channel_id=1, source_target_pairs={{2,0},{4,6},{3,1},{5,7},{10,8},{12,14},{11,9},{13,15},{18,16},{20,... | collective-permute-start | bytes 1572872 | tf_op jit(solution)/shard_map/ppermute | solution.py:466
  54.5 0.0 collective-permute-done.20.below_ref
  54.6 2.9 %collective-permute-start.21 = (bf16[36,8,128]{2,1,0:T(8,128)(2,1)S(1)}, bf16[36,8,128]{2,1,0:T(8,128)(2,1)S(1)}, u32[]{:S(2)}, u32[]{:S(2)}) collective-permute-start(bf16[36,8,128]{2,1,0:T(8,128)(2,1)S(1)} %pad_maximum_fusion), channel_id=1, source_target_pairs={{0,1},{1,2},{2,3},{3,4},{4,5},{5,6},{6,7},{8,9},{9,10},{10,11},{11... | collective-permute-start | bytes 221192 | tf_op jit(solution)/shard_map/ppermute | solution.py:23
  57.5 0.8 copy-done.2
  58.3 2.3 %pack.5 = (bf16[8,64,128]{2,1,0:T(8,128)(2,1)}, bf16[8,64,128]{2,1,0:T(8,128)(2,1)}, bf16[8,64,128]{2,1,0:T(8,128)(2,1)}, bf16[8,64,128]{2,1,0:T(8,128)(2,1)}, b...) custom-call(s32[8,1,128]{2,1,0:T(1,128)} %all_to_all.10.wanted_ref, ...), custom_call_target="tpu_custom_call" | custom-call | bytes 2097152 | tf_op jit(solution)/shard_map/pack/pallas_call | solution.py:220
  60.6 0.0 collective-permute-start.12
  60.6 1.5 %collective-permute-start.13 = (bf16[8,64,128]{2,1,0:T(8,128)(2,1)}, bf16[8,64,128]{2,1,0:T(8,128)(2,1)S(1)}, u32[]{:S(2)}, u32[]{:S(2)}) collective-permute-start(bf16[8,64,128]{2,1,0:T(8,128)(2,1)} %get-tuple-element.35), channel_id=1, source_target_pairs={{0,8},{1,9},{8,0},{9,1},{16,24},{17,25},{24,16},{25,17},{2,10},{3,... | collective-permute-start | bytes 393224 | tf_op jit(solution)/shard_map/ppermute | solution.py:547
  62.2 1.6 %collective-permute-start.14 = (bf16[8,64,128]{2,1,0:T(8,128)(2,1)}, bf16[8,64,128]{2,1,0:T(8,128)(2,1)S(1)}, u32[]{:S(2)}, u32[]{:S(2)}) collective-permute-start(bf16[8,64,128]{2,1,0:T(8,128)(2,1)} %get-tuple-element.36), channel_id=1, source_target_pairs={{0,9},{1,8},{8,1},{9,0},{16,25},{17,24},{24,17},{25,16},{2,11},{3,... | collective-permute-start | bytes 393224 | tf_op jit(solution)/shard_map/ppermute | solution.py:547
  63.8 1.2 collective-permute-start.15
  65.0 3.1 %collective-permute-start.22 = (bf16[36,8,128]{2,1,0:T(8,128)(2,1)S(1)}, bf16[36,8,128]{2,1,0:T(8,128)(2,1)S(1)}, u32[]{:S(2)}, u32[]{:S(2)}) collective-permute-start(bf16[36,8,128]{2,1,0:T(8,128)(2,1)S(1)} %pad_maximum_fusion.1), channel_id=1, source_target_pairs={{1,0},{2,1},{3,2},{4,3},{5,4},{6,5},{7,6},{9,8},{10,9},{11,10},{12... | collective-permute-start | bytes 221192 | tf_op jit(solution)/shard_map/ppermute | solution.py:23
  68.1 2.3 %pack.3 = (bf16[8,64,128]{2,1,0:T(8,128)(2,1)}, bf16[8,64,128]{2,1,0:T(8,128)(2,1)}, bf16[8,64,128]{2,1,0:T(8,128)(2,1)}, bf16[8,64,128]{2,1,0:T(8,128)(2,1)}, b...) custom-call(s32[8,1,128]{2,1,0:T(1,128)} %all_to_all.10.wanted_ref, ...), custom_call_target="tpu_custom_call" | custom-call | bytes 2097152 | tf_op jit(solution)/shard_map/pack/pallas_call | solution.py:220
  70.4 1.1 collective-permute-done.22.right_ref
  71.5 2.8 %collective-permute-start.16 = (bf16[8,64,128]{2,1,0:T(8,128)(2,1)}, bf16[8,64,128]{2,1,0:T(8,128)(2,1)S(1)}, u32[]{:S(2)}, u32[]{:S(2)}) collective-permute-start(bf16[8,64,128]{2,1,0:T(8,128)(2,1)} %get-tuple-element.38), channel_id=1, source_target_pairs={{0,17},{1,16},{8,25},{9,24},{16,1},{17,0},{24,9},{25,8},{2,19},{3,... | collective-permute-start | bytes 393224 | tf_op jit(solution)/shard_map/ppermute | solution.py:547
  74.3 0.0 collective-permute-done.12.refs_5_
  74.3 4.6 %collective-permute-start.17 = (bf16[8,64,128]{2,1,0:T(8,128)(2,1)}, bf16[8,64,128]{2,1,0:T(8,128)(2,1)S(1)}, u32[]{:S(2)}, u32[]{:S(2)}) collective-permute-start(bf16[8,64,128]{2,1,0:T(8,128)(2,1)} %get-tuple-element.39), channel_id=1, source_target_pairs={{0,24},{1,25},{8,16},{9,17},{16,8},{17,9},{24,0},{25,1},{2,26},{3,... | collective-permute-start | bytes 393224 | tf_op jit(solution)/shard_map/ppermute | solution.py:547
  78.9 0.0 collective-permute-start.18
  78.9 0.0 collective-permute-done.14.refs_7_
  78.9 2.6 %collective-permute-start.10 = (bf16[8,64,128]{2,1,0:T(8,128)(2,1)}, bf16[8,64,128]{2,1,0:T(8,128)(2,1)S(1)}, u32[]{:S(2)}, u32[]{:S(2)}) collective-permute-start(bf16[8,64,128]{2,1,0:T(8,128)(2,1)} %get-tuple-element.33), channel_id=1, source_target_pairs={{0,25},{1,24},{8,17},{9,16},{16,9},{17,8},{24,1},{25,0},{2,27},{3,... | collective-permute-start | bytes 393224 | tf_op jit(solution)/shard_map/ppermute | solution.py:547
  81.5 0.0 collective-permute-done.15.refs_8_
  81.6 0.1 collective-permute-start.5
  81.6 7.4 %collective-permute-done.17.refs_10_ = bf16[8,64,128]{2,1,0:T(8,128)(2,1)S(1)} collective-permute-done((bf16[8,64,128]{2,1,0:T(8,128)(2,1)}, bf16[8,64,128]{2,1,0:T(8,128)(2,1)S(1)}, u32[]{:S(2)}, u32[]{:S(2)}) %collective-permute-start.17) | collective-permute-done | bytes 131104 | tf_op jit(solution)/shard_map/ppermute | solution.py:547
  89.1 1.7 %collective-permute-start.7 = (bf16[8,64,128]{2,1,0:T(8,128)(2,1)}, bf16[8,64,128]{2,1,0:T(8,128)(2,1)}, u32[]{:S(2)}, u32[]{:S(2)}) collective-permute-start(bf16[8,64,128]{2,1,0:T(8,128)(2,1)} %get-tuple-element.30), channel_id=1, source_target_pairs={{0,16},{1,17},{8,24},{9,25},{16,0},{17,1},{24,8},{25,9},{2,18},{3,... | collective-permute-start | bytes 393224 | tf_op jit(solution)/shard_map/ppermute | solution.py:547
  90.8 1.2 collective-permute-start.8
  92.0 1.6 %collective-permute-start.9 = (bf16[8,64,128]{2,1,0:T(8,128)(2,1)}, bf16[8,64,128]{2,1,0:T(8,128)(2,1)}, u32[]{:S(2)}, u32[]{:S(2)}) collective-permute-start(bf16[8,64,128]{2,1,0:T(8,128)(2,1)} %get-tuple-element.32), channel_id=1, source_target_pairs={{0,24},{1,25},{8,16},{9,17},{16,8},{17,9},{24,0},{25,1},{2,26},{3,... | collective-permute-start | bytes 393224 | tf_op jit(solution)/shard_map/ppermute | solution.py:547
  93.6 6.0 %context.1 = (f32[2048,128]{1,0:T(8,128)}, bf16[2048,128]{1,0:T(8,128)(2,1)}) custom-call(bf16[32,64,128]{2,1,0:T(8,128)(2,1)} %refs_12_.1, bf16[2,64,128]{2,1,0:T(8,128)(2,1)} %copy-done.17, bf16[2,64,128]{2,1,0:T(8,128)(2,1)} %copy-done.18, bf16[36,8,128]{2,1,0:T(8,128)(2,1)} %copy-done.13, bf16[36,8,128]{2,1,0:T(8,128)(2,1)} %copy-done.14, ...), custom_call_target="tpu_custom_call" | custom-call | flops 157286400 | bytes 2621440 | tf_op jit(solution)/shard_map/context/pallas_call | solution.py:162
  99.7 1.3 %copy-done = bf16[8,16,64,128]{3,2,1,0:T(8,128)(2,1)} copy-done((bf16[8,16,64,128]{3,2,1,0:T(8,128)(2,1)}, bf16[8,16,64,128]{3,2,1,0:T(8,128)(2,1)S(1)}, u32[]{:S(2)}) %copy-start) | copy-done | bytes 2097176
  100.9 6.0 %collect.1.refs_9_ = bf16[128,64,128]{2,1,0:T(8,128)(2,1)} custom-call(s32[128]{0:T(128)} %get-tuple-element.47.position_ref, bf16[32,64,128]{2,1,0:T(8,128)(2,1)} %get-tuple-element.26.refs_0_, bf16[32,64,128]{2,1,0:T(8,128)(2,1)} %copy-done.4, bf16[128,64,128]{2,1,0:T(8,128)(2,1)} %bitcast.4, bf16[32,64,128]{2,1,0:T(8,128)(2,1)} %copy-done.1, ...), custom_call_target="tpu_custom_call" | custom-call | bytes 6684672 | tf_op jit(solution)/shard_map/collect/pallas_call | solution.py:280
  107.0 13.7 %tail.1 = bf16[32,64,128]{2,1,0:T(8,128)(2,1)} custom-call(s32[128]{0:T(128)} %get-tuple-element.47.position_ref, bf16[32,64,128]{2,1,0:T(8,128)(2,1)} %copy-done.5, bf16[32,64,128]{2,1,0:T(8,128)(2,1)} %collective-permute-done.3.refs_1_, bf16[8,64,128]{2,1,0:T(8,128)(2,1)} %copy-done.20, bf16[8,64,128]{2,1,0:T(8,128)(2,1)} %collective-permute-done.5.refs_3_, ...), custom_call_target="tpu_custom_call" | custom-call | flops 1048576000 | bytes 4194304 | tf_op jit(solution)/shard_map/tail/pallas_call | solution.py:433
  (65 shorter events, 0.2 us)
Async XLA Ops:
  3.7 13.1 %collective-permute-start.1 = (bf16[32,64,128]{2,1,0:T(8,128)(2,1)}, bf16[32,64,128]{2,1,0:T(8,128)(2,1)S(1)}, u32[]{:S(2)}, u32[]{:S(2)}) collective-permute-start(bf16[32,64,128]{2,1,0:T(8,128)(2,1)} %get-tuple-element.26.refs_0_), channel_id=1, source_target_pairs={{0,2},{2,0},{4,6},{6,4},{1,3},{3,1},{5,7},{7,5},{8,10},{10,8},{12,... | collective-permute-start | bytes 1572872 | tf_op jit(solution)/shard_map/ppermute | solution.py:466
  16.7 0.8 copy-start.4
  20.4 5.4 %copy-start.3 = (bf16[32,64,128]{2,1,0:T(8,128)(2,1)S(1)}, bf16[32,64,128]{2,1,0:T(8,128)(2,1)}, u32[]{:S(2)}) copy-start(bf16[32,64,128]{2,1,0:T(8,128)(2,1)} %get-tuple-element.26.refs_0_) | copy-start | bytes 1572868
  20.5 10.7 %copy-start.22 = (bf16[2,64,128]{2,1,0:T(8,128)(2,1)S(1)}, bf16[2,64,128]{2,1,0:T(8,128)(2,1)}, u32[]{:S(2)}) copy-start(bf16[2,64,128]{2,1,0:T(8,128)(2,1)} %get-tuple-element.41) | copy-start | bytes 98308
  20.5 14.8 %copy-start.21 = (bf16[2,64,128]{2,1,0:T(8,128)(2,1)S(1)}, bf16[2,64,128]{2,1,0:T(8,128)(2,1)}, u32[]{:S(2)}) copy-start(bf16[2,64,128]{2,1,0:T(8,128)(2,1)} %get-tuple-element.42) | copy-start | bytes 98308
  20.5 34.1 %copy-start.16 = (bf16[32,8,128]{2,1,0:T(8,128)(2,1)S(1)}, bf16[32,8,128]{2,1,0:T(8,128)(2,1)}, u32[]{:S(2)}) copy-start(bf16[32,8,128]{2,1,0:T(8,128)(2,1)} %get-tuple-element.43) | copy-start | bytes 196612
  20.5 44.5 %copy-start.15 = (bf16[32,8,128]{2,1,0:T(8,128)(2,1)S(1)}, bf16[32,8,128]{2,1,0:T(8,128)(2,1)}, u32[]{:S(2)}) copy-start(bf16[32,8,128]{2,1,0:T(8,128)(2,1)} %get-tuple-element.44) | copy-start | bytes 196612
  20.5 79.1 %all-to-all-start.1 = ((bf16[8,16,64,128]{3,2,1,0:T(8,128)(2,1)}), bf16[8,16,64,128]{3,2,1,0:T(8,128)(2,1)S(1)}, u32[]{:S(2)}, u32[]{:S(2)}) async-start(bf16[8,16,64,128]{3,2,1,0:T(8,128)(2,1)} %pack.4), calls=%async_computation.1 | async-start | bytes 4194304 | tf_op jit(solution)/shard_map/all_to_all | solution.py:543
  25.9 15.3 %collective-permute-start = (bf16[32,64,128]{2,1,0:T(8,128)(2,1)S(1)}, bf16[32,64,128]{2,1,0:T(8,128)(2,1)S(1)}, u32[]{:S(2)}, u32[]{:S(2)}) collective-permute-start(bf16[32,64,128]{2,1,0:T(8,128)(2,1)S(1)} %copy-done.3), channel_id=1, source_target_pairs={{2,4},{4,2},{3,5},{5,3},{10,12},{12,10},{11,13},{13,11},{18,20},{2... | collective-permute-start | bytes 1572872 | tf_op jit(solution)/shard_map/ppermute | solution.py:466
  27.9 24.5 %collective-permute-start.2 = (bf16[32,64,128]{2,1,0:T(8,128)(2,1)}, bf16[32,64,128]{2,1,0:T(8,128)(2,1)S(1)}, u32[]{:S(2)}, u32[]{:S(2)}) collective-permute-start(bf16[32,64,128]{2,1,0:T(8,128)(2,1)} %copy-done.4), channel_id=1, source_target_pairs={{2,4},{4,2},{3,5},{5,3},{10,12},{12,10},{11,13},{13,11},{18,20},{2... | collective-permute-start | bytes 1572872 | tf_op jit(solution)/shard_map/ppermute | solution.py:466
  31.2 17.9 %collective-permute-start.19 = (bf16[2,64,128]{2,1,0:T(8,128)(2,1)S(1)}, bf16[2,64,128]{2,1,0:T(8,128)(2,1)S(1)}, u32[]{:S(2)}, u32[]{:S(2)}) collective-permute-start(bf16[2,64,128]{2,1,0:T(8,128)(2,1)S(1)} %copy-done.22), channel_id=1, source_target_pairs={{0,8},{8,16},{16,24},{1,9},{9,17},{17,25},{2,10},{10,18},{18,26},{... | collective-permute-start | bytes 98312 | tf_op jit(solution)/shard_map/ppermute | solution.py:23
  35.3 19.3 %collective-permute-start.20 = (bf16[2,64,128]{2,1,0:T(8,128)(2,1)S(1)}, bf16[2,64,128]{2,1,0:T(8,128)(2,1)S(1)}, u32[]{:S(2)}, u32[]{:S(2)}) collective-permute-start(bf16[2,64,128]{2,1,0:T(8,128)(2,1)S(1)} %copy-done.21), channel_id=1, source_target_pairs={{8,0},{16,8},{24,16},{9,1},{17,9},{25,17},{10,2},{18,10},{26,18},{... | collective-permute-start | bytes 98312 | tf_op jit(solution)/shard_map/ppermute | solution.py:23
  41.2 13.4 %copy-start.5 = (bf16[32,64,128]{2,1,0:T(8,128)(2,1)}, bf16[32,64,128]{2,1,0:T(8,128)(2,1)S(1)}, u32[]{:S(2)}) copy-start(bf16[32,64,128]{2,1,0:T(8,128)(2,1)S(1)} %collective-permute-done.refs_0_) | copy-start | bytes 1572868
  41.2 16.3 %collective-permute-start.11 = (bf16[32,64,128]{2,1,0:T(8,128)(2,1)S(1)}, bf16[32,64,128]{2,1,0:T(8,128)(2,1)S(1)}, u32[]{:S(2)}, u32[]{:S(2)}) collective-permute-start(bf16[32,64,128]{2,1,0:T(8,128)(2,1)S(1)} %collective-permute-done.refs_0_), channel_id=1, source_target_pairs={{2,0},{4,6},{3,1},{5,7},{10,8},{12,14},{11,9},{13,15},{18,16},{20,... | collective-permute-start | bytes 1572872 | tf_op jit(solution)/shard_map/ppermute | solution.py:466
  49.1 44.5 %copy-start.17 = (bf16[2,64,128]{2,1,0:T(8,128)(2,1)}, bf16[2,64,128]{2,1,0:T(8,128)(2,1)S(1)}, u32[]{:S(2)}) copy-start(bf16[2,64,128]{2,1,0:T(8,128)(2,1)S(1)} %collective-permute-done.19.above_ref) | copy-start | bytes 98308
  52.4 5.0 %copy-start.1 = (bf16[32,64,128]{2,1,0:T(8,128)(2,1)}, bf16[32,64,128]{2,1,0:T(8,128)(2,1)S(1)}, u32[]{:S(2)}) copy-start(bf16[32,64,128]{2,1,0:T(8,128)(2,1)S(1)} %collective-permute-done.2.refs_0_.refs_3_) | copy-start | bytes 1572868
  52.4 12.5 %collective-permute-start.3 = (bf16[32,64,128]{2,1,0:T(8,128)(2,1)S(1)}, bf16[32,64,128]{2,1,0:T(8,128)(2,1)}, u32[]{:S(2)}, u32[]{:S(2)}) collective-permute-start(bf16[32,64,128]{2,1,0:T(8,128)(2,1)S(1)} %collective-permute-done.2.refs_0_.refs_3_), channel_id=1, source_target_pairs={{2,0},{4,6},{3,1},{5,7},{10,8},{12,14},{11,9},{13,15},{18,16},{20,... | collective-permute-start | bytes 1572872 | tf_op jit(solution)/shard_map/ppermute | solution.py:466
  54.5 39.1 %copy-start.18 = (bf16[2,64,128]{2,1,0:T(8,128)(2,1)}, bf16[2,64,128]{2,1,0:T(8,128)(2,1)S(1)}, u32[]{:S(2)}) copy-start(bf16[2,64,128]{2,1,0:T(8,128)(2,1)S(1)} %collective-permute-done.20.below_ref) | copy-start | bytes 98308
  54.6 9.2 %collective-permute-start.21 = (bf16[36,8,128]{2,1,0:T(8,128)(2,1)S(1)}, bf16[36,8,128]{2,1,0:T(8,128)(2,1)S(1)}, u32[]{:S(2)}, u32[]{:S(2)}) collective-permute-start(bf16[36,8,128]{2,1,0:T(8,128)(2,1)S(1)} %pad_maximum_fusion), channel_id=1, source_target_pairs={{0,1},{1,2},{2,3},{3,4},{4,5},{5,6},{6,7},{8,9},{9,10},{10,11},{11... | collective-permute-start | bytes 221192 | tf_op jit(solution)/shard_map/ppermute | solution.py:23
  57.5 0.8 copy-start.2
  60.6 13.7 %collective-permute-start.12 = (bf16[8,64,128]{2,1,0:T(8,128)(2,1)}, bf16[8,64,128]{2,1,0:T(8,128)(2,1)S(1)}, u32[]{:S(2)}, u32[]{:S(2)}) collective-permute-start(bf16[8,64,128]{2,1,0:T(8,128)(2,1)} %get-tuple-element.34), channel_id=1, source_target_pairs={{0,1},{1,0},{8,9},{9,8},{16,17},{17,16},{24,25},{25,24},{2,3},{3,2... | collective-permute-start | bytes 393224 | tf_op jit(solution)/shard_map/ppermute | solution.py:547
  60.6 18.3 %collective-permute-start.13 = (bf16[8,64,128]{2,1,0:T(8,128)(2,1)}, bf16[8,64,128]{2,1,0:T(8,128)(2,1)S(1)}, u32[]{:S(2)}, u32[]{:S(2)}) collective-permute-start(bf16[8,64,128]{2,1,0:T(8,128)(2,1)} %get-tuple-element.35), channel_id=1, source_target_pairs={{0,8},{1,9},{8,0},{9,1},{16,24},{17,25},{24,16},{25,17},{2,10},{3,... | collective-permute-start | bytes 393224 | tf_op jit(solution)/shard_map/ppermute | solution.py:547
  62.2 16.7 %collective-permute-start.14 = (bf16[8,64,128]{2,1,0:T(8,128)(2,1)}, bf16[8,64,128]{2,1,0:T(8,128)(2,1)S(1)}, u32[]{:S(2)}, u32[]{:S(2)}) collective-permute-start(bf16[8,64,128]{2,1,0:T(8,128)(2,1)} %get-tuple-element.36), channel_id=1, source_target_pairs={{0,9},{1,8},{8,1},{9,0},{16,25},{17,24},{24,17},{25,16},{2,11},{3,... | collective-permute-start | bytes 393224 | tf_op jit(solution)/shard_map/ppermute | solution.py:547
  63.8 29.8 %copy-start.13 = (bf16[36,8,128]{2,1,0:T(8,128)(2,1)}, bf16[36,8,128]{2,1,0:T(8,128)(2,1)S(1)}, u32[]{:S(2)}) copy-start(bf16[36,8,128]{2,1,0:T(8,128)(2,1)S(1)} %collective-permute-done.21.left_ref) | copy-start | bytes 221188
  63.8 17.8 %collective-permute-start.15 = (bf16[8,64,128]{2,1,0:T(8,128)(2,1)}, bf16[8,64,128]{2,1,0:T(8,128)(2,1)S(1)}, u32[]{:S(2)}, u32[]{:S(2)}) collective-permute-start(bf16[8,64,128]{2,1,0:T(8,128)(2,1)} %get-tuple-element.37), channel_id=1, source_target_pairs={{0,16},{1,17},{8,24},{9,25},{16,0},{17,1},{24,8},{25,9},{2,18},{3,... | collective-permute-start | bytes 393224 | tf_op jit(solution)/shard_map/ppermute | solution.py:547
  65.0 6.5 %collective-permute-start.22 = (bf16[36,8,128]{2,1,0:T(8,128)(2,1)S(1)}, bf16[36,8,128]{2,1,0:T(8,128)(2,1)S(1)}, u32[]{:S(2)}, u32[]{:S(2)}) collective-permute-start(bf16[36,8,128]{2,1,0:T(8,128)(2,1)S(1)} %pad_maximum_fusion.1), channel_id=1, source_target_pairs={{1,0},{2,1},{3,2},{4,3},{5,4},{6,5},{7,6},{9,8},{10,9},{11,10},{12... | collective-permute-start | bytes 221192 | tf_op jit(solution)/shard_map/ppermute | solution.py:23
  71.4 22.2 %copy-start.14 = (bf16[36,8,128]{2,1,0:T(8,128)(2,1)}, bf16[36,8,128]{2,1,0:T(8,128)(2,1)S(1)}, u32[]{:S(2)}) copy-start(bf16[36,8,128]{2,1,0:T(8,128)(2,1)S(1)} %collective-permute-done.22.right_ref) | copy-start | bytes 221188
  71.5 10.1 %collective-permute-start.16 = (bf16[8,64,128]{2,1,0:T(8,128)(2,1)}, bf16[8,64,128]{2,1,0:T(8,128)(2,1)S(1)}, u32[]{:S(2)}, u32[]{:S(2)}) collective-permute-start(bf16[8,64,128]{2,1,0:T(8,128)(2,1)} %get-tuple-element.38), channel_id=1, source_target_pairs={{0,17},{1,16},{8,25},{9,24},{16,1},{17,0},{24,9},{25,8},{2,19},{3,... | collective-permute-start | bytes 393224 | tf_op jit(solution)/shard_map/ppermute | solution.py:547
  74.3 25.4 %copy-start.6 = (bf16[8,64,128]{2,1,0:T(8,128)(2,1)}, bf16[8,64,128]{2,1,0:T(8,128)(2,1)S(1)}, u32[]{:S(2)}) copy-start(bf16[8,64,128]{2,1,0:T(8,128)(2,1)S(1)} %collective-permute-done.12.refs_5_) | copy-start | bytes 393220
  74.3 14.8 %collective-permute-start.17 = (bf16[8,64,128]{2,1,0:T(8,128)(2,1)}, bf16[8,64,128]{2,1,0:T(8,128)(2,1)S(1)}, u32[]{:S(2)}, u32[]{:S(2)}) collective-permute-start(bf16[8,64,128]{2,1,0:T(8,128)(2,1)} %get-tuple-element.39), channel_id=1, source_target_pairs={{0,24},{1,25},{8,16},{9,17},{16,8},{17,9},{24,0},{25,1},{2,26},{3,... | collective-permute-start | bytes 393224 | tf_op jit(solution)/shard_map/ppermute | solution.py:547
  78.9 20.7 %copy-start.7 = (bf16[8,64,128]{2,1,0:T(8,128)(2,1)}, bf16[8,64,128]{2,1,0:T(8,128)(2,1)S(1)}, u32[]{:S(2)}) copy-start(bf16[8,64,128]{2,1,0:T(8,128)(2,1)S(1)} %collective-permute-done.13.refs_6_) | copy-start | bytes 393220
  78.9 10.2 %collective-permute-start.18 = (bf16[8,64,128]{2,1,0:T(8,128)(2,1)}, bf16[8,64,128]{2,1,0:T(8,128)(2,1)S(1)}, u32[]{:S(2)}, u32[]{:S(2)}) collective-permute-start(bf16[8,64,128]{2,1,0:T(8,128)(2,1)} %get-tuple-element.40), channel_id=1, source_target_pairs={{0,25},{1,24},{8,17},{9,16},{16,9},{17,8},{24,1},{25,0},{2,27},{3,... | collective-permute-start | bytes 393224 | tf_op jit(solution)/shard_map/ppermute | solution.py:547
  78.9 20.7 %copy-start.8 = (bf16[8,64,128]{2,1,0:T(8,128)(2,1)}, bf16[8,64,128]{2,1,0:T(8,128)(2,1)S(1)}, u32[]{:S(2)}) copy-start(bf16[8,64,128]{2,1,0:T(8,128)(2,1)S(1)} %collective-permute-done.14.refs_7_) | copy-start | bytes 393220
  78.9 11.9 %collective-permute-start.10 = (bf16[8,64,128]{2,1,0:T(8,128)(2,1)}, bf16[8,64,128]{2,1,0:T(8,128)(2,1)S(1)}, u32[]{:S(2)}, u32[]{:S(2)}) collective-permute-start(bf16[8,64,128]{2,1,0:T(8,128)(2,1)} %get-tuple-element.33), channel_id=1, source_target_pairs={{0,25},{1,24},{8,17},{9,16},{16,9},{17,8},{24,1},{25,0},{2,27},{3,... | collective-permute-start | bytes 393224 | tf_op jit(solution)/shard_map/ppermute | solution.py:547
  81.5 18.1 %copy-start.9 = (bf16[8,64,128]{2,1,0:T(8,128)(2,1)}, bf16[8,64,128]{2,1,0:T(8,128)(2,1)S(1)}, u32[]{:S(2)}) copy-start(bf16[8,64,128]{2,1,0:T(8,128)(2,1)S(1)} %collective-permute-done.15.refs_8_) | copy-start | bytes 393220
  81.5 10.4 %collective-permute-start.4 = (bf16[8,64,128]{2,1,0:T(8,128)(2,1)}, bf16[8,64,128]{2,1,0:T(8,128)(2,1)S(1)}, u32[]{:S(2)}, u32[]{:S(2)}) collective-permute-start(bf16[8,64,128]{2,1,0:T(8,128)(2,1)} %get-tuple-element.27), channel_id=1, source_target_pairs={{0,1},{1,0},{8,9},{9,8},{16,17},{17,16},{24,25},{25,24},{2,3},{3,2... | collective-permute-start | bytes 393224 | tf_op jit(solution)/shard_map/ppermute | solution.py:547
  81.6 18.1 %copy-start.10 = (bf16[8,64,128]{2,1,0:T(8,128)(2,1)}, bf16[8,64,128]{2,1,0:T(8,128)(2,1)S(1)}, u32[]{:S(2)}) copy-start(bf16[8,64,128]{2,1,0:T(8,128)(2,1)S(1)} %collective-permute-done.16.refs_9_) | copy-start | bytes 393220
  81.6 25.4 %collective-permute-start.5 = (bf16[8,64,128]{2,1,0:T(8,128)(2,1)}, bf16[8,64,128]{2,1,0:T(8,128)(2,1)}, u32[]{:S(2)}, u32[]{:S(2)}) collective-permute-start(bf16[8,64,128]{2,1,0:T(8,128)(2,1)} %get-tuple-element.28), channel_id=1, source_target_pairs={{0,8},{1,9},{8,0},{9,1},{16,24},{17,25},{24,16},{25,17},{2,10},{3,... | collective-permute-start | bytes 393224 | tf_op jit(solution)/shard_map/ppermute | solution.py:547
  89.0 10.6 %copy-start.11 = (bf16[8,64,128]{2,1,0:T(8,128)(2,1)}, bf16[8,64,128]{2,1,0:T(8,128)(2,1)S(1)}, u32[]{:S(2)}) copy-start(bf16[8,64,128]{2,1,0:T(8,128)(2,1)S(1)} %collective-permute-done.17.refs_10_) | copy-start | bytes 393220
  89.0 17.9 %collective-permute-start.6 = (bf16[8,64,128]{2,1,0:T(8,128)(2,1)}, bf16[8,64,128]{2,1,0:T(8,128)(2,1)}, u32[]{:S(2)}, u32[]{:S(2)}) collective-permute-start(bf16[8,64,128]{2,1,0:T(8,128)(2,1)} %get-tuple-element.29), channel_id=1, source_target_pairs={{0,9},{1,8},{8,1},{9,0},{16,25},{17,24},{24,17},{25,16},{2,11},{3,... | collective-permute-start | bytes 393224 | tf_op jit(solution)/shard_map/ppermute | solution.py:547
  89.1 10.6 %copy-start.12 = (bf16[8,64,128]{2,1,0:T(8,128)(2,1)}, bf16[8,64,128]{2,1,0:T(8,128)(2,1)S(1)}, u32[]{:S(2)}) copy-start(bf16[8,64,128]{2,1,0:T(8,128)(2,1)S(1)} %collective-permute-done.18.refs_11_) | copy-start | bytes 393220
  89.1 17.9 %collective-permute-start.7 = (bf16[8,64,128]{2,1,0:T(8,128)(2,1)}, bf16[8,64,128]{2,1,0:T(8,128)(2,1)}, u32[]{:S(2)}, u32[]{:S(2)}) collective-permute-start(bf16[8,64,128]{2,1,0:T(8,128)(2,1)} %get-tuple-element.30), channel_id=1, source_target_pairs={{0,16},{1,17},{8,24},{9,25},{16,0},{17,1},{24,8},{25,9},{2,18},{3,... | collective-permute-start | bytes 393224 | tf_op jit(solution)/shard_map/ppermute | solution.py:547
  90.8 16.2 %copy-start.19 = (bf16[8,64,128]{2,1,0:T(8,128)(2,1)}, bf16[8,64,128]{2,1,0:T(8,128)(2,1)S(1)}, u32[]{:S(2)}) copy-start(bf16[8,64,128]{2,1,0:T(8,128)(2,1)S(1)} %collective-permute-done.10.refs_8_) | copy-start | bytes 393220
  90.8 16.2 %collective-permute-start.8 = (bf16[8,64,128]{2,1,0:T(8,128)(2,1)}, bf16[8,64,128]{2,1,0:T(8,128)(2,1)}, u32[]{:S(2)}, u32[]{:S(2)}) collective-permute-start(bf16[8,64,128]{2,1,0:T(8,128)(2,1)} %get-tuple-element.31), channel_id=1, source_target_pairs={{0,17},{1,16},{8,25},{9,24},{16,1},{17,0},{24,9},{25,8},{2,19},{3,... | collective-permute-start | bytes 393224 | tf_op jit(solution)/shard_map/ppermute | solution.py:547
  92.0 15.1 %copy-start.20 = (bf16[8,64,128]{2,1,0:T(8,128)(2,1)}, bf16[8,64,128]{2,1,0:T(8,128)(2,1)S(1)}, u32[]{:S(2)}) copy-start(bf16[8,64,128]{2,1,0:T(8,128)(2,1)S(1)} %collective-permute-done.4.refs_2_) | copy-start | bytes 393220
  92.0 15.0 %collective-permute-start.9 = (bf16[8,64,128]{2,1,0:T(8,128)(2,1)}, bf16[8,64,128]{2,1,0:T(8,128)(2,1)}, u32[]{:S(2)}, u32[]{:S(2)}) collective-permute-start(bf16[8,64,128]{2,1,0:T(8,128)(2,1)} %get-tuple-element.32), channel_id=1, source_target_pairs={{0,24},{1,25},{8,16},{9,17},{16,8},{17,9},{24,0},{25,1},{2,26},{3,... | collective-permute-start | bytes 393224 | tf_op jit(solution)/shard_map/ppermute | solution.py:547
  99.6 1.3 %copy-start = (bf16[8,16,64,128]{3,2,1,0:T(8,128)(2,1)}, bf16[8,16,64,128]{3,2,1,0:T(8,128)(2,1)S(1)}, u32[]{:S(2)}) copy-start(bf16[8,16,64,128]{3,2,1,0:T(8,128)(2,1)S(1)} %all-to-all-done.1) | copy-start | bytes 6291460

commit v2 on v1

--- a/solution.py
+++ b/solution.py
@@ -21,15 +21,6 @@
     forward = [(i, i + 1) for i in range(count - 1)]
     backward = [(target, source) for source, target in forward]
     return lax.ppermute(high, axis, forward), lax.ppermute(low, axis, backward)
-
-
-def halo(top, bottom, left, right):
-    border = left.shape[1]
-    above, below = from_sides(top, bottom, "rows")
-    low = jnp.concatenate([above[:, :border], left, below[:, :border]], axis=0)
-    high = jnp.concatenate([above[:, -border:], right, below[:, -border:]], axis=0)
-    left, right = from_sides(low, high, ("z", "x"))
-    return above, below, left, right
 
 
 def normalize(floats, gain):
@@ -185,51 +176,70 @@
     return (layer == 1) | (layer == 2)
 
 
-def pack_kernel(chunks, capacity, joint, place_of, wanted_ref, *refs):
+def frame_kernel(above_ref, below_ref, left_ref, right_ref, low_ref, high_ref):
+    margin, width = above_ref.shape[:2]
+    height, border = left_ref.shape[:2]
+    for out_ref, flank_ref, first in ((low_ref, left_ref, 0), (high_ref, right_ref, width - border)):
+        out_ref[pl.ds(0, margin)] = above_ref[:, pl.ds(first, border), :]
+        out_ref[pl.ds(margin, height)] = flank_ref[...]
+        out_ref[pl.ds(margin + height, margin)] = below_ref[:, pl.ds(first, border), :]
+
+
+def pack_kernel(jobs, options, outputs, framed, capacity, layers, place_of, wanted_ref, *refs):
     peer, layer = place_of()
-    count = sum(options for _, options in chunks)
-    sources, out_refs = refs[:count], refs[count:]
-    distances = range(1, out_refs[0].shape[0] if joint else len(out_refs) + 1)
+    sources = refs[: sum(options)]
+    outs = refs[len(refs) - outputs :]
+    if framed:
+        frame_kernel(*refs[sum(options) : sum(options) + 4], *outs[-2:])
     inside = is_inside(layer)
 
-    def fill(source_ref, chunk, place):
-        for distance in distances:
-            other = peer ^ distance
-            for slot in range(capacity):
-                region = source_ref[wanted_ref[other, 0, (layer ^ chunk) * capacity + slot]]
-                if joint:
-                    out_refs[0][other, place * capacity + slot] = region
-                else:
-                    out_refs[distance - 1][place * capacity + slot] = region
-
-    at = 0
-    for place, (chunk, options) in enumerate(chunks):
-        if options == 1:
-            fill(sources[at], chunk, place)
-        else:
-            pl.when(inside)(functools.partial(fill, sources[at], chunk, place))
-            pl.when(~inside)(functools.partial(fill, sources[at + 1], chunk, place))
-        at += options
-
-
-def pack(chunks, place_of, wanted, peers, capacity, joint):
-    sources = sum(chunks.values(), [])
-    tile = sources[0].shape
-    shape = (capacity * len(chunks), *tile[1:])
-    shapes = [(peers, *shape)] if joint else [shape] * (peers - 1)
+    def fill(source_ref, out_ref, place, distance, column):
+        other = peer ^ distance
+        base = ((layer ^ column) if column < layers else column) * capacity
+        for slot in range(capacity):
+            region = source_ref[wanted_ref[other, 0, base + slot]]
+            if place is None:
+                out_ref[other, slot] = region
+            else:
+                out_ref[place * capacity + slot] = region
+
+    def fill_all(shift, chosen):
+        for out, place, source, distance, column in chosen:
+            at = sum(options[:source]) + shift
+            fill(sources[at], outs[out], place, distance, column)
+
+    fill_all(0, [job for job in jobs if options[job[2]] == 1])
+    paired = [job for job in jobs if options[job[2]] == 2]
+    if paired:
+        pl.when(inside)(functools.partial(fill_all, 0, paired))
+        pl.when(~inside)(functools.partial(fill_all, 1, paired))
+
+
+def pack(jobs, shapes, sources, place_of, wanted, capacity, layers, frame=()):
+    flat = sum(sources, [])
+    if frame:
+        margin, (height, border, channels) = frame[0].shape[0], frame[2].shape
+        shapes = shapes + [(height + 2 * margin, border, channels)] * 2
+    in_vmem = pl.BlockSpec(memory_space=pltpu.VMEM)
     return pl.pallas_call(
         functools.partial(
-            pack_kernel, tuple((k, len(v)) for k, v in chunks.items()), capacity, joint, place_of
-        ),
-        in_specs=[pl.BlockSpec(memory_space=pltpu.SMEM)]
-        + [pl.BlockSpec(memory_space=pltpu.VMEM)] * len(sources),
-        out_specs=[pl.BlockSpec(memory_space=pltpu.VMEM)] * len(shapes),
+            pack_kernel,
+            tuple(jobs),
+            tuple(map(len, sources)),
+            len(shapes),
+            len(frame) > 0,
+            capacity,
+            layers,
+            place_of,
+        ),
+        in_specs=[pl.BlockSpec(memory_space=pltpu.SMEM)] + [in_vmem] * (len(flat) + len(frame)),
+        out_specs=[in_vmem] * len(shapes),
         out_shape=[jax.ShapeDtypeStruct(a, BF16) for a in shapes],
         cost_estimate=pl.CostEstimate(
-            flops=0, bytes_accessed=4 * peers * math.prod(shape), transcendentals=0
+            flops=0, bytes_accessed=4 * sum(map(math.prod, shapes)), transcendentals=0
         ),
         name="pack",
-    )(wanted, *sources)
+    )(wanted, *flat, *frame)
 
 
 def load_all(options, sources, landed, sems, layer):
@@ -486,8 +496,6 @@
     capacity = max(2, 2 * pair_count // devices)
     all_cols = region_cols * layers * across
 
-    regions = region_rows * region_cols
-
     def place_of():
         return lax.axis_index("rows") * across + lax.axis_index("x"), lax.axis_index("z")
 
@@ -505,23 +513,13 @@
     earlier = (owners[:, None] == owners[None, :]) & (pairs[None, :] < pairs[:, None])
     slot = jnp.sum(earlier.astype(jnp.int32), axis=1)
     distance = owner_peer ^ peer
-    chunk = owner_layer ^ layer
-    groups = [(0, 1), *((step,) for step in range(2, layers))]
-    position, start = jnp.zeros_like(slot), 0
-    for number, members in enumerate(groups):
-        joint = number == 0
-        replies = start + len(members) * regions
-        sender = owner_peer if joint else distance - 1
-        for place, step in enumerate(members):
-            here_at = start + place * regions + local_index
-            sent_at = replies + (sender * len(members) + place) * capacity + slot
-            position = jnp.where(
-                chunk == step, jnp.where(distance == 0, here_at, sent_at), position
-            )
-        early = start
-        start = replies + (peers - 1 + joint) * len(members) * capacity
-    lanes = -(-layers * capacity // 128) * 128
+    step = owner_layer ^ layer
+    whole, twin = (1, peers // 2), across
+    lanes = -(-(layers + len(whole)) * capacity // 128) * 128
     asked = owner_peer * lanes + owner_layer * capacity + slot
+    for number, far in enumerate(whole):
+        through = (peer ^ twin) * lanes + (layers + number) * capacity + slot
+        asked = jnp.where((step == 0) & (distance == far ^ twin), through, asked)
     slots = jnp.arange(peers * lanes, dtype=jnp.int32)
     requests = jnp.sum(
         jnp.where(asked[None, :] == slots[:, None], local_index[None, :], 0), axis=1
@@ -533,25 +531,79 @@
     margin = (lce_weight.shape[0] - 1) // 2
     normed, *edges = norm_regions(image, norm_gain, side, margin, 8)
 
+    def swap(part, far):
+        return lax.ppermute(part, ("rows", "x"), [(i, i ^ far) for i in range(peers)])
+
     held = layer_blocks(normed, layers)
+    given = [swap(normed, far) for far in whole]
+    above, below = from_sides(*edges[:2], "rows")
+
+    tile = normed.shape[1:]
+    position, total = jnp.zeros_like(slot), 0
     arrived = []
-    for number, members in enumerate(groups):
-        chunks = {step: held[step] for step in members}
-        joint = number == 0
-        packed = pack(chunks, place_of, wanted, peers, capacity, joint)
-        if joint:
-            got = lax.all_to_all(packed[0], ("rows", "x"), 0, 0, tiled=True)
-            got = [got.reshape(-1, *normed.shape[1:])]
+
+    def landing(options, *places):
+        nonlocal position, total
+        for condition, index in places:
+            position = jnp.where(condition, total + index, position)
+        total += options[0].shape[0]
+        arrived[-1].append(options)
+
+    relayed = [twin, *(far ^ twin for far in whole)]
+    direct = [far for far in range(1, peers) if far not in relayed and far not in whole]
+    jobs = [(0, 0, 0, twin, 0)]
+    jobs += [(0, 1 + i, 1 + i, twin, layers + i) for i in range(len(whole))]
+    jobs += [(1 + i, 0, 0, far, 0) for i, far in enumerate(direct)]
+    jobs += [(1 + len(direct), None, 1 + len(whole), far, 1) for far in range(1, peers)]
+    shapes = [(len(relayed) * capacity, *tile)] + [(capacity, *tile)] * len(direct)
+    shapes += [(peers, capacity, *tile)]
+    sources = [[normed], *([part] for part in given), held[1]]
+    *parts, joint, low, high = pack(
+        jobs, shapes, sources, place_of, wanted, capacity, layers, (above, below, *edges[2:])
+    )
+    got = [swap(part, far) for part, far in zip(parts, [twin, *direct])]
+    joint = lax.all_to_all(joint, ("rows", "x"), 0, 0, tiled=True)
+    around = (above, below, *from_sides(low, high, ("z", "x")))
+    arrived.append([])
+    landing([normed], ((step == 0) & (distance == 0), local_index))
+    for far, part in zip(whole, given):
+        landing([part], ((step == 0) & (distance == far), local_index))
+    landing(
+        [got[0]],
+        *(
+            ((step == 0) & (distance == far), i * capacity + slot)
+            for i, far in enumerate(relayed)
+        ),
+    )
+    for far, part in zip(direct, got[1:]):
+        landing([part], ((step == 0) & (distance == far), slot))
+    landing(held[1], ((step == 1) & (distance == 0), local_index))
+    landing(
+        [joint.reshape(-1, *tile)],
+        ((step == 1) & (distance != 0), owner_peer * capacity + slot),
+    )
+
+    for chunk in range(2, layers):
+        last = chunk == layers - 1
+        jobs = [(0 if last else far - 1, None if last else 0, 0, far, chunk) for far in range(1, peers)]
+        shapes = [(peers, capacity, *tile)] if last else [(capacity, *tile)] * (peers - 1)
+        parts = pack(jobs, shapes, [held[chunk]], place_of, wanted, capacity, layers)
+        if last:
+            got = lax.all_to_all(parts[0], ("rows", "x"), 0, 0, tiled=True)
         else:
-            got = [
-                lax.ppermute(part, ("rows", "x"), [(i, i ^ far) for i in range(peers)])
-                for far, part in enumerate(packed, 1)
-            ]
-        arrived.append([*chunks.values(), *([part] for part in got)])
+            got = [swap(part, far) for far, part in enumerate(parts, 1)]
+        early = total
+        arrived.append([])
+        landing(held[chunk], ((step == chunk) & (distance == 0), local_index))
+        if last:
+            elsewhere = (step == chunk) & (distance != 0)
+            landing([got.reshape(-1, *tile)], (elsewhere, owner_peer * capacity + slot))
+        else:
+            for far, part in enumerate(got, 1):
+                landing([part], ((step == chunk) & (distance == far), slot))
     late = arrived.pop()
     fetched = collect(position, sum(arrived, []), place_of, math.gcd(pair_count, 8))
 
-    around = halo(*edges)
     context, queries = context_and_queries(
         image, around, norm_gain, qkv_weight, lce_weight, side, margin
     )

time: 121 us -> 124 us (1.025)
  the two profiles are of different devices: /device:TPU:17 before, /device:TPU:0 now
where the time goes in v2:
time: 124 us; the launch traced here: 123 us
  starting transfers between devices  40.3 us (32%)
  Pallas kernels  37.3 us (30%)
  waiting for transfers between devices  31.5 us (25%)
  blocking collectives  8.31 us (7%)
  local copies, waits for them, and re-layouts  4.27 us (3%)
    ppermute x5, waiting for transfers between devices, hop(): return lax.ppermute(block, 'z', pairs)  29.8 us
    ppermute x12, starting transfers between devices, swap(): lax.ppermute(part, ('rows', 'x'), [(i, i ^ far) for i in range(peers)])  18.3 us
    pallas_call x1, Pallas kernels, tail(): pl.pallas_call(functools.partial(tail_kernel, side, picks, batch, early,...  13.7 us
    all_to_all x1, blocking collectives, block(): lax.all_to_all(requests.reshape(peers, 1, lanes), ('rows', 'x'), 0, 0, ti...  8.31 us
    pallas_call x3, Pallas kernels, pack(): pl.pallas_call(functools.partial(pack_kernel, tuple(jobs), tuple(map(len,...  7.74 us
    ppermute x5, starting transfers between devices, hop(): return lax.ppermute(block, 'z', pairs)  7.2 us
    pallas_call x1, Pallas kernels, collect(): pl.pallas_call(functools.partial(collect_kernel, tuple(map(len, sources))...  6.27 us
    pallas_call x1, Pallas kernels, context_and_queries(): pl.pallas_call(functools.partial(context_kernel, side, margin), grid=(hei...  5.93 us
  transfers between devices with their start and end apart: 23, of which 5 were waited for; matrix products, arithmetic and copies ran while one was open for 2% of the time, Pallas kernels for 16%

profile of v2, /device:TPU:0, one launch (start us, length us, event | category | flops | bytes accessed | tf_op | source)
XLA Modules:
  0.0 123.1 jit_solution(7929924620714987418)
XLA Ops:
  0.0 3.7 %norm_regions.1 = (bf16[32,64,128]{2,1,0:T(8,128)(2,1)}, bf16[2,64,128]{2,1,0:T(8,128)(2,1)}, bf16[2,64,128]{2,1,0:T(8,128)(2,1)}, bf16[32,8,128]{2,1,0:T(8,128)(2,1)}, bf16[32,8,128]{2,1,0:T(8,128)(2,1)}) custom-call(bf16[32,64,128]{2,1,0:T(8,128)(2,1)} %refs_6_.1, f32[1,128]{1,0:T(1,128)} %bitcast.8), custom_call_target="tpu_custom_call" | custom-call | flops 2621440 | bytes 1048576 | tf_op jit(solution)/shard_map/norm_regions/pallas_call | solution.py:73
  3.7 3.1 %collective-permute-start.1 = (bf16[32,64,128]{2,1,0:T(8,128)(2,1)}, bf16[32,64,128]{2,1,0:T(8,128)(2,1)S(1)}, u32[]{:S(2)}, u32[]{:S(2)}) collective-permute-start(bf16[32,64,128]{2,1,0:T(8,128)(2,1)} %get-tuple-element.25.refs_0_), channel_id=1, source_target_pairs={{0,2},{2,0},{4,6},{6,4},{1,3},{3,1},{5,7},{7,5},{8,10},{10,8},{12,... | collective-permute-start | bytes 1572872 | tf_op jit(solution)/shard_map/ppermute | solution.py:476
  6.8 1.5 %collective-permute-start.4 = (bf16[32,64,128]{2,1,0:T(8,128)(2,1)}, bf16[32,64,128]{2,1,0:T(8,128)(2,1)S(1)}, u32[]{:S(2)}, u32[]{:S(2)}) collective-permute-start(bf16[32,64,128]{2,1,0:T(8,128)(2,1)} %get-tuple-element.25.refs_0_), channel_id=1, source_target_pairs={{0,1},{1,0},{8,9},{9,8},{16,17},{17,16},{24,25},{25,24},{2,3},{3,2... | collective-permute-start | bytes 1572872 | tf_op jit(solution)/shard_map/ppermute | solution.py:535
  8.3 1.5 %collective-permute-start.5 = (bf16[32,64,128]{2,1,0:T(8,128)(2,1)}, bf16[32,64,128]{2,1,0:T(8,128)(2,1)S(1)}, u32[]{:S(2)}, u32[]{:S(2)}) collective-permute-start(bf16[32,64,128]{2,1,0:T(8,128)(2,1)} %get-tuple-element.25.refs_0_), channel_id=1, source_target_pairs={{0,16},{1,17},{8,24},{9,25},{16,0},{17,1},{24,8},{25,9},{2,18},{3,... | collective-permute-start | bytes 1572872 | tf_op jit(solution)/shard_map/ppermute | solution.py:535
  9.8 1.3 %collective-permute-start.6 = (bf16[2,64,128]{2,1,0:T(8,128)(2,1)}, bf16[2,64,128]{2,1,0:T(8,128)(2,1)S(1)}, u32[]{:S(2)}, u32[]{:S(2)}) collective-permute-start(bf16[2,64,128]{2,1,0:T(8,128)(2,1)} %get-tuple-element.26), channel_id=1, source_target_pairs={{0,8},{8,16},{16,24},{1,9},{9,17},{17,25},{2,10},{10,18},{18,26},{... | collective-permute-start | bytes 98312 | tf_op jit(solution)/shard_map/ppermute | solution.py:23
  11.1 1.3 %collective-permute-start.7 = (bf16[2,64,128]{2,1,0:T(8,128)(2,1)}, bf16[2,64,128]{2,1,0:T(8,128)(2,1)S(1)}, u32[]{:S(2)}, u32[]{:S(2)}) collective-permute-start(bf16[2,64,128]{2,1,0:T(8,128)(2,1)} %get-tuple-element.27), channel_id=1, source_target_pairs={{8,0},{16,8},{24,16},{9,1},{17,9},{25,17},{10,2},{18,10},{26,18},{... | collective-permute-start | bytes 98312 | tf_op jit(solution)/shard_map/ppermute | solution.py:23
  12.4 0.8 copy.12
  13.2 0.1 reshape.306
  13.3 0.2 convert_reduce_fusion
  13.5 5.4 %collective-permute-done.1.refs_3_.refs_6_ = bf16[32,64,128]{2,1,0:T(8,128)(2,1)S(1)} collective-permute-done((bf16[32,64,128]{2,1,0:T(8,128)(2,1)}, bf16[32,64,128]{2,1,0:T(8,128)(2,1)S(1)}, u32[]{:S(2)}, u32[]{:S(2)}) %collective-permute-start.1) | collective-permute-done | bytes 524320 | tf_op jit(solution)/shard_map/ppermute | solution.py:476
  18.9 0.7 collective-permute-start.2
  19.6 0.5 and_select_fusion.19
  20.2 0.2 select_reduce_fusion
  20.4 8.3 %all_to_all.15.wanted_ref = s32[8,1,128]{2,1,0:T(1,128)} all-to-all(s32[8,1,128]{2,1,0:T(1,128)S(1)} %bitcast.7), channel_id=1, replica_groups=mesh['rows'=4,'z'=4,'x'=2] {'rows','x'}, dimensions={0} | all-to-all | bytes 8192 | tf_op jit(solution)/shard_map/all_to_all | solution.py:527
  28.7 0.0 collective-permute-done.6.refs_4_.above_ref
  28.7 0.0 collective-permute-done.4.refs_1_
  28.8 0.5 copy-done.19
  29.3 0.0 copy-done.20
  29.3 0.2 copy-done.5
  29.5 0.2 copy-done.6
  29.7 3.1 %pack.4 = (bf16[24,64,128]{2,1,0:T(8,128)(2,1)}, bf16[8,64,128]{2,1,0:T(8,128)(2,1)}, bf16[8,64,128]{2,1,0:T(8,128)(2,1)}, bf16[8,8,64,128]{3,2,1,0:T(8,128)(2,1...) custom-call(s32[8,1,128]{2,1,0:T(1,128)} %all_to_all.15.wanted_ref, ...), custom_call_target="tpu_custom_call" | custom-call | bytes 3702784 | tf_op jit(solution)/shard_map/pack/pallas_call | solution.py:224
  32.9 3.6 %all-to-all-start.2 = ((bf16[8,8,64,128]{3,2,1,0:T(8,128)(2,1)}), bf16[8,8,64,128]{3,2,1,0:T(8,128)(2,1)S(1)}, u32[]{:S(2)}, u32[]{:S(2)}) async-start(bf16[8,8,64,128]{3,2,1,0:T(8,128)(2,1)} %get-tuple-element.33), calls=%async_computation.2 | async-start | bytes 2097152 | tf_op jit(solution)/shard_map/all_to_all | solution.py:565
  36.4 0.8 collective-permute-start
  37.3 1.3 %collective-permute-start.3 = (bf16[32,64,128]{2,1,0:T(8,128)(2,1)S(1)}, bf16[32,64,128]{2,1,0:T(8,128)(2,1)S(1)}, u32[]{:S(2)}, u32[]{:S(2)}) collective-permute-start(bf16[32,64,128]{2,1,0:T(8,128)(2,1)S(1)} %collective-permute-done.2.refs_0_.refs_8_), channel_id=1, source_target_pairs={{2,0},{4,6},{3,1},{5,7},{10,8},{12,14},{11,9},{13,15},{18,16},{20,... | collective-permute-start | bytes 1572872 | tf_op jit(solution)/shard_map/ppermute | solution.py:476
  38.6 18.2 %collective-permute-done.3.refs_1_ = bf16[32,64,128]{2,1,0:T(8,128)(2,1)S(1)} collective-permute-done((bf16[32,64,128]{2,1,0:T(8,128)(2,1)S(1)}, bf16[32,64,128]{2,1,0:T(8,128)(2,1)S(1)}, u32[]{:S(2)}, u32[]{:S(2)}) %collective-permute-start.3) | collective-permute-done | bytes 524320 | tf_op jit(solution)/shard_map/ppermute | solution.py:476
  56.8 0.8 copy-done.9
  57.6 2.3 %pack.3 = bf16[8,8,64,128]{3,2,1,0:T(8,128)(2,1)} custom-call(s32[8,1,128]{2,1,0:T(1,128)} %all_to_all.15.wanted_ref, bf16[32,64,128]{2,1,0:T(8,128)(2,1)} %copy-done.8, bf16[32,64,128]{2,1,0:T(8,128)(2,1)} %copy-done.9), custom_call_target="tpu_custom_call" | custom-call | bytes 2097152 | tf_op jit(solution)/shard_map/pack/pallas_call | solution.py:224
  60.0 3.9 %all-to-all-start.1 = ((bf16[8,8,64,128]{3,2,1,0:T(8,128)(2,1)}), bf16[8,8,64,128]{3,2,1,0:T(8,128)(2,1)S(1)}, u32[]{:S(2)}, u32[]{:S(2)}) async-start(bf16[8,8,64,128]{3,2,1,0:T(8,128)(2,1)} %pack.3), calls=%async_computation.1 | async-start | bytes 2097152 | tf_op jit(solution)/shard_map/all_to_all | solution.py:592
  63.8 1.3 %collective-permute-start.11 = (bf16[32,64,128]{2,1,0:T(8,128)(2,1)}, bf16[32,64,128]{2,1,0:T(8,128)(2,1)S(1)}, u32[]{:S(2)}, u32[]{:S(2)}) collective-permute-start(bf16[32,64,128]{2,1,0:T(8,128)(2,1)} %copy-done.8), channel_id=1, source_target_pairs={{2,0},{4,6},{3,1},{5,7},{10,8},{12,14},{11,9},{13,15},{18,16},{20,... | collective-permute-start | bytes 1572872 | tf_op jit(solution)/shard_map/ppermute | solution.py:476
  65.1 0.6 collective-permute-start.8
  65.7 3.5 %collective-permute-start.19 = (bf16[36,8,128]{2,1,0:T(8,128)(2,1)}, bf16[36,8,128]{2,1,0:T(8,128)(2,1)S(1)}, u32[]{:S(2)}, u32[]{:S(2)}) collective-permute-start(bf16[36,8,128]{2,1,0:T(8,128)(2,1)} %get-tuple-element.41), channel_id=1, source_target_pairs={{0,1},{1,2},{2,3},{3,4},{4,5},{5,6},{6,7},{8,9},{9,10},{10,11},{11... | collective-permute-start | bytes 221192 | tf_op jit(solution)/shard_map/ppermute | solution.py:23
  69.2 1.3 %collective-permute-start.20 = (bf16[36,8,128]{2,1,0:T(8,128)(2,1)}, bf16[36,8,128]{2,1,0:T(8,128)(2,1)S(1)}, u32[]{:S(2)}, u32[]{:S(2)}) collective-permute-start(bf16[36,8,128]{2,1,0:T(8,128)(2,1)} %get-tuple-element.42), channel_id=1, source_target_pairs={{1,0},{2,1},{3,2},{4,3},{5,4},{6,5},{7,6},{9,8},{10,9},{11,10},{12... | collective-permute-start | bytes 221192 | tf_op jit(solution)/shard_map/ppermute | solution.py:23
  70.5 4.0 %collective-permute-start.10 = (bf16[8,64,128]{2,1,0:T(8,128)(2,1)}, bf16[8,64,128]{2,1,0:T(8,128)(2,1)S(1)}, u32[]{:S(2)}, u32[]{:S(2)}) collective-permute-start(bf16[8,64,128]{2,1,0:T(8,128)(2,1)} %get-tuple-element.32), channel_id=1, source_target_pairs={{0,25},{1,24},{8,17},{9,16},{16,9},{17,8},{24,1},{25,0},{2,27},{3,... | collective-permute-start | bytes 393224 | tf_op jit(solution)/shard_map/ppermute | solution.py:535
  74.5 6.2 %collective-permute-done.11.refs_1_.refs_9_ = bf16[32,64,128]{2,1,0:T(8,128)(2,1)S(1)} collective-permute-done((bf16[32,64,128]{2,1,0:T(8,128)(2,1)}, bf16[32,64,128]{2,1,0:T(8,128)(2,1)S(1)}, u32[]{:S(2)}, u32[]{:S(2)}) %collective-permute-start.11) | collective-permute-done | bytes 524320 | tf_op jit(solution)/shard_map/ppermute | solution.py:476
  80.7 2.1 %collective-permute-start.9 = (bf16[8,64,128]{2,1,0:T(8,128)(2,1)S(1)}, bf16[8,64,128]{2,1,0:T(8,128)(2,1)S(1)}, u32[]{:S(2)}, u32[]{:S(2)}) collective-permute-start(bf16[8,64,128]{2,1,0:T(8,128)(2,1)S(1)} %copy-done.23), channel_id=1, source_target_pairs={{0,17},{1,16},{8,25},{9,24},{16,1},{17,0},{24,9},{25,8},{2,19},{3,... | collective-permute-start | bytes 393224 | tf_op jit(solution)/shard_map/ppermute | solution.py:535
  82.8 2.3 %pack.5 = (bf16[8,64,128]{2,1,0:T(8,128)(2,1)}, bf16[8,64,128]{2,1,0:T(8,128)(2,1)}, bf16[8,64,128]{2,1,0:T(8,128)(2,1)}, bf16[8,64,128]{2,1,0:T(8,128)(2,1)}, b...) custom-call(s32[8,1,128]{2,1,0:T(1,128)} %all_to_all.15.wanted_ref, ...), custom_call_target="tpu_custom_call" | custom-call | bytes 1835008 | tf_op jit(solution)/shard_map/pack/pallas_call | solution.py:224
  85.1 1.4 %collective-permute-start.12 = (bf16[8,64,128]{2,1,0:T(8,128)(2,1)}, bf16[8,64,128]{2,1,0:T(8,128)(2,1)S(1)}, u32[]{:S(2)}, u32[]{:S(2)}) collective-permute-start(bf16[8,64,128]{2,1,0:T(8,128)(2,1)} %get-tuple-element.34), channel_id=1, source_target_pairs={{0,1},{1,0},{8,9},{9,8},{16,17},{17,16},{24,25},{25,24},{2,3},{3,2... | collective-permute-start | bytes 393224 | tf_op jit(solution)/shard_map/ppermute | solution.py:535
  86.5 0.8 collective-permute-start.14
  87.3 1.4 %collective-permute-start.15 = (bf16[8,64,128]{2,1,0:T(8,128)(2,1)}, bf16[8,64,128]{2,1,0:T(8,128)(2,1)S(1)}, u32[]{:S(2)}, u32[]{:S(2)}) collective-permute-start(bf16[8,64,128]{2,1,0:T(8,128)(2,1)} %get-tuple-element.37), channel_id=1, source_target_pairs={{0,16},{1,17},{8,24},{9,25},{16,0},{17,1},{24,8},{25,9},{2,18},{3,... | collective-permute-start | bytes 393224 | tf_op jit(solution)/shard_map/ppermute | solution.py:535
  88.7 1.9 %collective-permute-start.16 = (bf16[8,64,128]{2,1,0:T(8,128)(2,1)}, bf16[8,64,128]{2,1,0:T(8,128)(2,1)S(1)}, u32[]{:S(2)}, u32[]{:S(2)}) collective-permute-start(bf16[8,64,128]{2,1,0:T(8,128)(2,1)} %get-tuple-element.38), channel_id=1, source_target_pairs={{0,17},{1,16},{8,25},{9,24},{16,1},{17,0},{24,9},{25,8},{2,19},{3,... | collective-permute-start | bytes 393224 | tf_op jit(solution)/shard_map/ppermute | solution.py:535
  90.6 0.3 collective-permute-done.12.refs_10_
  90.9 3.2 %collective-permute-start.18 = (bf16[8,64,128]{2,1,0:T(8,128)(2,1)}, bf16[8,64,128]{2,1,0:T(8,128)(2,1)}, u32[]{:S(2)}, u32[]{:S(2)}) collective-permute-start(bf16[8,64,128]{2,1,0:T(8,128)(2,1)} %get-tuple-element.40), channel_id=1, source_target_pairs={{0,25},{1,24},{8,17},{9,16},{16,9},{17,8},{24,1},{25,0},{2,27},{3,... | collective-permute-start | bytes 393224 | tf_op jit(solution)/shard_map/ppermute | solution.py:535
  94.1 5.9 %context.1 = (f32[2048,128]{1,0:T(8,128)}, bf16[2048,128]{1,0:T(8,128)(2,1)}) custom-call(bf16[32,64,128]{2,1,0:T(8,128)(2,1)} %refs_6_.1, bf16[2,64,128]{2,1,0:T(8,128)(2,1)} %copy-done.19, bf16[2,64,128]{2,1,0:T(8,128)(2,1)} %copy-done.20, bf16[36,8,128]{2,1,0:T(8,128)(2,1)} %copy-done.21, bf16[36,8,128]{2,1,0:T(8,128)(2,1)} %copy-done.22, ...), custom_call_target="tpu_custom_call" | custom-call | flops 157286400 | bytes 2621440 | tf_op jit(solution)/shard_map/context/pallas_call | solution.py:153
  100.1 1.4 %collective-permute-done.17.refs_15_ = bf16[8,64,128]{2,1,0:T(8,128)(2,1)S(1)} collective-permute-done((bf16[8,64,128]{2,1,0:T(8,128)(2,1)}, bf16[8,64,128]{2,1,0:T(8,128)(2,1)S(1)}, u32[]{:S(2)}, u32[]{:S(2)}) %collective-permute-start.17) | collective-permute-done | bytes 131104 | tf_op jit(solution)/shard_map/ppermute | solution.py:535
  101.5 0.6 copy-done.18
  102.1 6.3 %collect.1.refs_3_ = bf16[128,64,128]{2,1,0:T(8,128)(2,1)} custom-call(s32[128]{0:T(128)} %get-tuple-element.45.position_ref, bf16[32,64,128]{2,1,0:T(8,128)(2,1)} %get-tuple-element.25.refs_0_, bf16[32,64,128]{2,1,0:T(8,128)(2,1)} %copy-done.5, bf16[32,64,128]{2,1,0:T(8,128)(2,1)} %copy-done.6, bf16[24,64,128]{2,1,0:T(8,128)(2,1)} %copy-done.10, ...), custom_call_target="tpu_custom_call" | custom-call | bytes 7340032 | tf_op jit(solution)/shard_map/collect/pallas_call | solution.py:290
  108.4 1.0 copy-done.7
  109.3 13.7 %tail.1 = bf16[32,64,128]{2,1,0:T(8,128)(2,1)} custom-call(s32[128]{0:T(128)} %get-tuple-element.45.position_ref, bf16[32,64,128]{2,1,0:T(8,128)(2,1)} %copy-done.8, bf16[32,64,128]{2,1,0:T(8,128)(2,1)} %copy-done.9, bf16[64,64,128]{2,1,0:T(8,128)(2,1)} %bitcast.6, bf16[128,64,128]{2,1,0:T(8,128)(2,1)} %collect.1.refs_3_, ...), custom_call_target="tpu_custom_call" | custom-call | flops 1048576000 | bytes 4194304 | tf_op jit(solution)/shard_map/tail/pallas_call | solution.py:443
  (61 shorter events, 0.2 us)
Async XLA Ops:
  3.7 15.3 %collective-permute-start.1 = (bf16[32,64,128]{2,1,0:T(8,128)(2,1)}, bf16[32,64,128]{2,1,0:T(8,128)(2,1)S(1)}, u32[]{:S(2)}, u32[]{:S(2)}) collective-permute-start(bf16[32,64,128]{2,1,0:T(8,128)(2,1)} %get-tuple-element.25.refs_0_), channel_id=1, source_target_pairs={{0,2},{2,0},{4,6},{6,4},{1,3},{3,1},{5,7},{7,5},{8,10},{10,8},{12,... | collective-permute-start | bytes 1572872 | tf_op jit(solution)/shard_map/ppermute | solution.py:476
  6.8 21.9 %collective-permute-start.4 = (bf16[32,64,128]{2,1,0:T(8,128)(2,1)}, bf16[32,64,128]{2,1,0:T(8,128)(2,1)S(1)}, u32[]{:S(2)}, u32[]{:S(2)}) collective-permute-start(bf16[32,64,128]{2,1,0:T(8,128)(2,1)} %get-tuple-element.25.refs_0_), channel_id=1, source_target_pairs={{0,1},{1,0},{8,9},{9,8},{16,17},{17,16},{24,25},{25,24},{2,3},{3,2... | collective-permute-start | bytes 1572872 | tf_op jit(solution)/shard_map/ppermute | solution.py:535
  8.3 20.4 %collective-permute-start.5 = (bf16[32,64,128]{2,1,0:T(8,128)(2,1)}, bf16[32,64,128]{2,1,0:T(8,128)(2,1)S(1)}, u32[]{:S(2)}, u32[]{:S(2)}) collective-permute-start(bf16[32,64,128]{2,1,0:T(8,128)(2,1)} %get-tuple-element.25.refs_0_), channel_id=1, source_target_pairs={{0,16},{1,17},{8,24},{9,25},{16,0},{17,1},{24,8},{25,9},{2,18},{3,... | collective-permute-start | bytes 1572872 | tf_op jit(solution)/shard_map/ppermute | solution.py:535
  9.8 18.9 %collective-permute-start.6 = (bf16[2,64,128]{2,1,0:T(8,128)(2,1)}, bf16[2,64,128]{2,1,0:T(8,128)(2,1)S(1)}, u32[]{:S(2)}, u32[]{:S(2)}) collective-permute-start(bf16[2,64,128]{2,1,0:T(8,128)(2,1)} %get-tuple-element.26), channel_id=1, source_target_pairs={{0,8},{8,16},{16,24},{1,9},{9,17},{17,25},{2,10},{10,18},{18,26},{... | collective-permute-start | bytes 98312 | tf_op jit(solution)/shard_map/ppermute | solution.py:23
  11.1 17.6 %collective-permute-start.7 = (bf16[2,64,128]{2,1,0:T(8,128)(2,1)}, bf16[2,64,128]{2,1,0:T(8,128)(2,1)S(1)}, u32[]{:S(2)}, u32[]{:S(2)}) collective-permute-start(bf16[2,64,128]{2,1,0:T(8,128)(2,1)} %get-tuple-element.27), channel_id=1, source_target_pairs={{8,0},{16,8},{24,16},{9,1},{17,9},{25,17},{10,2},{18,10},{26,18},{... | collective-permute-start | bytes 98312 | tf_op jit(solution)/shard_map/ppermute | solution.py:23
  18.9 9.8 %copy-start.4 = (bf16[32,64,128]{2,1,0:T(8,128)(2,1)}, bf16[32,64,128]{2,1,0:T(8,128)(2,1)S(1)}, u32[]{:S(2)}) copy-start(bf16[32,64,128]{2,1,0:T(8,128)(2,1)S(1)} %collective-permute-done.1.refs_3_.refs_6_) | copy-start | bytes 1572868
  18.9 18.4 %collective-permute-start.2 = (bf16[32,64,128]{2,1,0:T(8,128)(2,1)S(1)}, bf16[32,64,128]{2,1,0:T(8,128)(2,1)S(1)}, u32[]{:S(2)}, u32[]{:S(2)}) collective-permute-start(bf16[32,64,128]{2,1,0:T(8,128)(2,1)S(1)} %collective-permute-done.1.refs_3_.refs_6_), channel_id=1, source_target_pairs={{2,4},{4,2},{3,5},{5,3},{10,12},{12,10},{11,13},{13,11},{18,20},{2... | collective-permute-start | bytes 1572872 | tf_op jit(solution)/shard_map/ppermute | solution.py:476
  28.7 0.6 copy-start.19
  28.7 0.6 copy-start.20
  28.7 0.8 copy-start.5
  28.7 1.0 copy-start.6
  29.7 6.7 %copy-start.3 = (bf16[32,64,128]{2,1,0:T(8,128)(2,1)S(1)}, bf16[32,64,128]{2,1,0:T(8,128)(2,1)}, u32[]{:S(2)}) copy-start(bf16[32,64,128]{2,1,0:T(8,128)(2,1)} %get-tuple-element.25.refs_0_) | copy-start | bytes 1572868
  32.9 27.1 %all-to-all-start.2 = ((bf16[8,8,64,128]{3,2,1,0:T(8,128)(2,1)}), bf16[8,8,64,128]{3,2,1,0:T(8,128)(2,1)S(1)}, u32[]{:S(2)}, u32[]{:S(2)}) async-start(bf16[8,8,64,128]{3,2,1,0:T(8,128)(2,1)} %get-tuple-element.33), calls=%async_computation.2 | async-start | bytes 2097152 | tf_op jit(solution)/shard_map/all_to_all | solution.py:565
  36.4 44.3 %copy-start.23 = (bf16[8,64,128]{2,1,0:T(8,128)(2,1)S(1)}, bf16[8,64,128]{2,1,0:T(8,128)(2,1)}, u32[]{:S(2)}) copy-start(bf16[8,64,128]{2,1,0:T(8,128)(2,1)} %get-tuple-element.31) | copy-start | bytes 393220
  36.4 2.2 %collective-permute-start = (bf16[32,64,128]{2,1,0:T(8,128)(2,1)S(1)}, bf16[32,64,128]{2,1,0:T(8,128)(2,1)S(1)}, u32[]{:S(2)}, u32[]{:S(2)}) collective-permute-start(bf16[32,64,128]{2,1,0:T(8,128)(2,1)S(1)} %copy-done.3), channel_id=1, source_target_pairs={{2,4},{4,2},{3,5},{5,3},{10,12},{12,10},{11,13},{13,11},{18,20},{2... | collective-permute-start | bytes 1572872 | tf_op jit(solution)/shard_map/ppermute | solution.py:476
  37.3 22.7 %copy-start.1 = (bf16[32,64,128]{2,1,0:T(8,128)(2,1)}, bf16[32,64,128]{2,1,0:T(8,128)(2,1)S(1)}, u32[]{:S(2)}) copy-start(bf16[32,64,128]{2,1,0:T(8,128)(2,1)S(1)} %collective-permute-done.2.refs_0_.refs_8_) | copy-start | bytes 1572868
  37.3 19.5 %collective-permute-start.3 = (bf16[32,64,128]{2,1,0:T(8,128)(2,1)S(1)}, bf16[32,64,128]{2,1,0:T(8,128)(2,1)S(1)}, u32[]{:S(2)}, u32[]{:S(2)}) collective-permute-start(bf16[32,64,128]{2,1,0:T(8,128)(2,1)S(1)} %collective-permute-done.2.refs_0_.refs_8_), channel_id=1, source_target_pairs={{2,0},{4,6},{3,1},{5,7},{10,8},{12,14},{11,9},{13,15},{18,16},{20,... | collective-permute-start | bytes 1572872 | tf_op jit(solution)/shard_map/ppermute | solution.py:476
  38.6 18.2 %copy-start.8 = (bf16[32,64,128]{2,1,0:T(8,128)(2,1)}, bf16[32,64,128]{2,1,0:T(8,128)(2,1)S(1)}, u32[]{:S(2)}) copy-start(bf16[32,64,128]{2,1,0:T(8,128)(2,1)S(1)} %collective-permute-done.refs_0_) | copy-start | bytes 1572868
  56.8 0.8 copy-start.9
  59.9 41.5 %copy-start = (bf16[8,8,64,128]{3,2,1,0:T(8,128)(2,1)}, bf16[8,8,64,128]{3,2,1,0:T(8,128)(2,1)S(1)}, u32[]{:S(2)}) copy-start(bf16[8,8,64,128]{3,2,1,0:T(8,128)(2,1)S(1)} %all-to-all-done.2) | copy-start | bytes 3145732
  60.0 48.4 %all-to-all-start.1 = ((bf16[8,8,64,128]{3,2,1,0:T(8,128)(2,1)}), bf16[8,8,64,128]{3,2,1,0:T(8,128)(2,1)S(1)}, u32[]{:S(2)}, u32[]{:S(2)}) async-start(bf16[8,8,64,128]{3,2,1,0:T(8,128)(2,1)} %pack.3), calls=%async_computation.1 | async-start | bytes 2097152 | tf_op jit(solution)/shard_map/all_to_all | solution.py:592
  63.8 16.9 %collective-permute-start.11 = (bf16[32,64,128]{2,1,0:T(8,128)(2,1)}, bf16[32,64,128]{2,1,0:T(8,128)(2,1)S(1)}, u32[]{:S(2)}, u32[]{:S(2)}) collective-permute-start(bf16[32,64,128]{2,1,0:T(8,128)(2,1)} %copy-done.8), channel_id=1, source_target_pairs={{2,0},{4,6},{3,1},{5,7},{10,8},{12,14},{11,9},{13,15},{18,16},{20,... | collective-permute-start | bytes 1572872 | tf_op jit(solution)/shard_map/ppermute | solution.py:476
  65.1 23.6 %collective-permute-start.8 = (bf16[24,64,128]{2,1,0:T(8,128)(2,1)}, bf16[24,64,128]{2,1,0:T(8,128)(2,1)S(1)}, u32[]{:S(2)}, u32[]{:S(2)}) collective-permute-start(bf16[24,64,128]{2,1,0:T(8,128)(2,1)} %get-tuple-element.30), channel_id=1, source_target_pairs={{0,8},{1,9},{8,0},{9,1},{16,24},{17,25},{24,16},{25,17},{2,10},{3,... | collective-permute-start | bytes 1179656 | tf_op jit(solution)/shard_map/ppermute | solution.py:535
  65.7 19.4 %collective-permute-start.19 = (bf16[36,8,128]{2,1,0:T(8,128)(2,1)}, bf16[36,8,128]{2,1,0:T(8,128)(2,1)S(1)}, u32[]{:S(2)}, u32[]{:S(2)}) collective-permute-start(bf16[36,8,128]{2,1,0:T(8,128)(2,1)} %get-tuple-element.41), channel_id=1, source_target_pairs={{0,1},{1,2},{2,3},{3,4},{4,5},{5,6},{6,7},{8,9},{9,10},{10,11},{11... | collective-permute-start | bytes 221192 | tf_op jit(solution)/shard_map/ppermute | solution.py:23
  69.2 17.3 %collective-permute-start.20 = (bf16[36,8,128]{2,1,0:T(8,128)(2,1)}, bf16[36,8,128]{2,1,0:T(8,128)(2,1)S(1)}, u32[]{:S(2)}, u32[]{:S(2)}) collective-permute-start(bf16[36,8,128]{2,1,0:T(8,128)(2,1)} %get-tuple-element.42), channel_id=1, source_target_pairs={{1,0},{2,1},{3,2},{4,3},{5,4},{6,5},{7,6},{9,8},{10,9},{11,10},{12... | collective-permute-start | bytes 221192 | tf_op jit(solution)/shard_map/ppermute | solution.py:23
  70.5 16.0 %collective-permute-start.10 = (bf16[8,64,128]{2,1,0:T(8,128)(2,1)}, bf16[8,64,128]{2,1,0:T(8,128)(2,1)S(1)}, u32[]{:S(2)}, u32[]{:S(2)}) collective-permute-start(bf16[8,64,128]{2,1,0:T(8,128)(2,1)} %get-tuple-element.32), channel_id=1, source_target_pairs={{0,25},{1,24},{8,17},{9,16},{16,9},{17,8},{24,1},{25,0},{2,27},{3,... | collective-permute-start | bytes 393224 | tf_op jit(solution)/shard_map/ppermute | solution.py:535
  80.7 2.1 %copy-start.2 = (bf16[32,64,128]{2,1,0:T(8,128)(2,1)}, bf16[32,64,128]{2,1,0:T(8,128)(2,1)S(1)}, u32[]{:S(2)}) copy-start(bf16[32,64,128]{2,1,0:T(8,128)(2,1)S(1)} %collective-permute-done.11.refs_1_.refs_9_) | copy-start | bytes 1572868
  80.7 6.6 %collective-permute-start.9 = (bf16[8,64,128]{2,1,0:T(8,128)(2,1)S(1)}, bf16[8,64,128]{2,1,0:T(8,128)(2,1)S(1)}, u32[]{:S(2)}, u32[]{:S(2)}) collective-permute-start(bf16[8,64,128]{2,1,0:T(8,128)(2,1)S(1)} %copy-done.23), channel_id=1, source_target_pairs={{0,17},{1,16},{8,25},{9,24},{16,1},{17,0},{24,9},{25,8},{2,19},{3,... | collective-permute-start | bytes 393224 | tf_op jit(solution)/shard_map/ppermute | solution.py:535
  85.1 3.6 %copy-start.21 = (bf16[36,8,128]{2,1,0:T(8,128)(2,1)}, bf16[36,8,128]{2,1,0:T(8,128)(2,1)S(1)}, u32[]{:S(2)}) copy-start(bf16[36,8,128]{2,1,0:T(8,128)(2,1)S(1)} %collective-permute-done.19.left_ref) | copy-start | bytes 221188
  85.1 5.8 %collective-permute-start.12 = (bf16[8,64,128]{2,1,0:T(8,128)(2,1)}, bf16[8,64,128]{2,1,0:T(8,128)(2,1)S(1)}, u32[]{:S(2)}, u32[]{:S(2)}) collective-permute-start(bf16[8,64,128]{2,1,0:T(8,128)(2,1)} %get-tuple-element.34), channel_id=1, source_target_pairs={{0,1},{1,0},{8,9},{9,8},{16,17},{17,16},{24,25},{25,24},{2,3},{3,2... | collective-permute-start | bytes 393224 | tf_op jit(solution)/shard_map/ppermute | solution.py:535
  86.5 2.2 %copy-start.22 = (bf16[36,8,128]{2,1,0:T(8,128)(2,1)}, bf16[36,8,128]{2,1,0:T(8,128)(2,1)S(1)}, u32[]{:S(2)}) copy-start(bf16[36,8,128]{2,1,0:T(8,128)(2,1)S(1)} %collective-permute-done.20.right_ref) | copy-start | bytes 221188
  86.5 4.4 %collective-permute-start.13 = (bf16[8,64,128]{2,1,0:T(8,128)(2,1)}, bf16[8,64,128]{2,1,0:T(8,128)(2,1)S(1)}, u32[]{:S(2)}, u32[]{:S(2)}) collective-permute-start(bf16[8,64,128]{2,1,0:T(8,128)(2,1)} %get-tuple-element.35), channel_id=1, source_target_pairs={{0,8},{1,9},{8,0},{9,1},{16,24},{17,25},{24,16},{25,17},{2,10},{3,... | collective-permute-start | bytes 393224 | tf_op jit(solution)/shard_map/ppermute | solution.py:535
  86.5 14.9 %copy-start.11 = (bf16[8,64,128]{2,1,0:T(8,128)(2,1)}, bf16[8,64,128]{2,1,0:T(8,128)(2,1)S(1)}, u32[]{:S(2)}) copy-start(bf16[8,64,128]{2,1,0:T(8,128)(2,1)S(1)} %collective-permute-done.10.refs_5_) | copy-start | bytes 393220
  86.5 13.5 %collective-permute-start.14 = (bf16[8,64,128]{2,1,0:T(8,128)(2,1)}, bf16[8,64,128]{2,1,0:T(8,128)(2,1)S(1)}, u32[]{:S(2)}, u32[]{:S(2)}) collective-permute-start(bf16[8,64,128]{2,1,0:T(8,128)(2,1)} %get-tuple-element.36), channel_id=1, source_target_pairs={{0,9},{1,8},{8,1},{9,0},{16,25},{17,24},{24,17},{25,16},{2,11},{3,... | collective-permute-start | bytes 393224 | tf_op jit(solution)/shard_map/ppermute | solution.py:535
  87.3 14.2 %copy-start.12 = (bf16[8,64,128]{2,1,0:T(8,128)(2,1)}, bf16[8,64,128]{2,1,0:T(8,128)(2,1)S(1)}, u32[]{:S(2)}) copy-start(bf16[8,64,128]{2,1,0:T(8,128)(2,1)S(1)} %collective-permute-done.9.refs_4_) | copy-start | bytes 393220
  87.3 12.7 %collective-permute-start.15 = (bf16[8,64,128]{2,1,0:T(8,128)(2,1)}, bf16[8,64,128]{2,1,0:T(8,128)(2,1)S(1)}, u32[]{:S(2)}, u32[]{:S(2)}) collective-permute-start(bf16[8,64,128]{2,1,0:T(8,128)(2,1)} %get-tuple-element.37), channel_id=1, source_target_pairs={{0,16},{1,17},{8,24},{9,25},{16,0},{17,1},{24,8},{25,9},{2,18},{3,... | collective-permute-start | bytes 393224 | tf_op jit(solution)/shard_map/ppermute | solution.py:535
  88.7 12.8 %copy-start.10 = (bf16[24,64,128]{2,1,0:T(8,128)(2,1)}, bf16[24,64,128]{2,1,0:T(8,128)(2,1)S(1)}, u32[]{:S(2)}) copy-start(bf16[24,64,128]{2,1,0:T(8,128)(2,1)S(1)} %collective-permute-done.8.refs_3_) | copy-start | bytes 1179652
  88.7 11.3 %collective-permute-start.16 = (bf16[8,64,128]{2,1,0:T(8,128)(2,1)}, bf16[8,64,128]{2,1,0:T(8,128)(2,1)S(1)}, u32[]{:S(2)}, u32[]{:S(2)}) collective-permute-start(bf16[8,64,128]{2,1,0:T(8,128)(2,1)} %get-tuple-element.38), channel_id=1, source_target_pairs={{0,17},{1,16},{8,25},{9,24},{16,1},{17,0},{24,9},{25,8},{2,19},{3,... | collective-permute-start | bytes 393224 | tf_op jit(solution)/shard_map/ppermute | solution.py:535
  90.8 10.6 %copy-start.13 = (bf16[8,64,128]{2,1,0:T(8,128)(2,1)}, bf16[8,64,128]{2,1,0:T(8,128)(2,1)S(1)}, u32[]{:S(2)}) copy-start(bf16[8,64,128]{2,1,0:T(8,128)(2,1)S(1)} %collective-permute-done.12.refs_10_) | copy-start | bytes 393220
  90.8 10.6 %collective-permute-start.17 = (bf16[8,64,128]{2,1,0:T(8,128)(2,1)}, bf16[8,64,128]{2,1,0:T(8,128)(2,1)S(1)}, u32[]{:S(2)}, u32[]{:S(2)}) collective-permute-start(bf16[8,64,128]{2,1,0:T(8,128)(2,1)} %get-tuple-element.39), channel_id=1, source_target_pairs={{0,24},{1,25},{8,16},{9,17},{16,8},{17,9},{24,0},{25,1},{2,26},{3,... | collective-permute-start | bytes 393224 | tf_op jit(solution)/shard_map/ppermute | solution.py:535
  90.9 10.6 %copy-start.14 = (bf16[8,64,128]{2,1,0:T(8,128)(2,1)}, bf16[8,64,128]{2,1,0:T(8,128)(2,1)S(1)}, u32[]{:S(2)}) copy-start(bf16[8,64,128]{2,1,0:T(8,128)(2,1)S(1)} %collective-permute-done.13.refs_11_) | copy-start | bytes 393220
  90.9 10.6 %collective-permute-start.18 = (bf16[8,64,128]{2,1,0:T(8,128)(2,1)}, bf16[8,64,128]{2,1,0:T(8,128)(2,1)}, u32[]{:S(2)}, u32[]{:S(2)}) collective-permute-start(bf16[8,64,128]{2,1,0:T(8,128)(2,1)} %get-tuple-element.40), channel_id=1, source_target_pairs={{0,25},{1,24},{8,17},{9,16},{16,9},{17,8},{24,1},{25,0},{2,27},{3,... | collective-permute-start | bytes 393224 | tf_op jit(solution)/shard_map/ppermute | solution.py:535
  100.0 1.5 %copy-start.15 = (bf16[8,64,128]{2,1,0:T(8,128)(2,1)}, bf16[8,64,128]{2,1,0:T(8,128)(2,1)S(1)}, u32[]{:S(2)}) copy-start(bf16[8,64,128]{2,1,0:T(8,128)(2,1)S(1)} %collective-permute-done.14.refs_12_) | copy-start | bytes 393220
  100.0 1.5 %copy-start.16 = (bf16[8,64,128]{2,1,0:T(8,128)(2,1)}, bf16[8,64,128]{2,1,0:T(8,128)(2,1)S(1)}, u32[]{:S(2)}) copy-start(bf16[8,64,128]{2,1,0:T(8,128)(2,1)S(1)} %collective-permute-done.15.refs_13_) | copy-start | bytes 393220
  100.0 1.5 %copy-start.17 = (bf16[8,64,128]{2,1,0:T(8,128)(2,1)}, bf16[8,64,128]{2,1,0:T(8,128)(2,1)S(1)}, u32[]{:S(2)}) copy-start(bf16[8,64,128]{2,1,0:T(8,128)(2,1)S(1)} %collective-permute-done.16.refs_14_) | copy-start | bytes 393220
  101.4 0.6 copy-start.18
  108.4 1.0 copy-start.7

commit v3 on v2

--- a/solution.py
+++ b/solution.py
@@ -16,11 +16,15 @@
 BF16 = jnp.bfloat16
 
 
-def from_sides(low, high, axis):
-    count = math.prod(lax.axis_size(name) for name in (axis if isinstance(axis, tuple) else (axis,)))
-    forward = [(i, i + 1) for i in range(count - 1)]
-    backward = [(target, source) for source, target in forward]
-    return lax.ppermute(high, axis, forward), lax.ppermute(low, axis, backward)
+def with_pairs(parts, axis, count):
+    links = ([], [])
+    for i in range(count - 1):
+        links[i % 2].extend([(i, i + 1), (i + 1, i)])
+    return [lax.ppermute(part, axis, pairs) for part, pairs in zip(parts, links)]
+
+
+def either(flag, yes, no):
+    return jnp.where(flag, yes, no)
 
 
 def normalize(floats, gain):
@@ -47,31 +51,35 @@
     )
 
 
-def norm_kernel(side, image_ref, gain_ref, out_ref, top_ref, bottom_ref, left_ref, right_ref):
+def norm_kernel(side, evens_of, image_ref, gain_ref, out_ref, *edge_refs):
     step = pl.program_id(0)
+    *row_refs, left_ref, right_ref = edge_refs
     tokens = image_ref[...]
     normed = normalize(tokens.astype(F32), gain_ref[...])
     out_ref[...] = regions_of(normed, side).astype(BF16).reshape(out_ref.shape)
-    margin, width, border = top_ref.shape[0], tokens.shape[1], left_ref.shape[1]
+    margin, width, border = row_refs[0].shape[0], tokens.shape[1], left_ref.shape[1]
     left_ref[...] = image_ref[:, pl.ds(0, border), :]
     right_ref[...] = image_ref[:, pl.ds(width - border, border), :]
-
-    @pl.when(step == 0)
-    def _():
-        top_ref[...] = image_ref[pl.ds(0, margin)]
-
-    @pl.when(step == pl.num_programs(0) - 1)
-    def _():
-        bottom_ref[...] = image_ref[pl.ds(side - margin, margin)]
-
-
-def norm_regions(image, gain, side, margin, border):
+    row_even = evens_of()[0]
+
+    def put(even, odd, first):
+        def store(ref):
+            ref[...] = image_ref[pl.ds(first, margin)]
+
+        pl.when(row_even)(lambda: store(row_refs[even]))
+        pl.when(~row_even)(lambda: store(row_refs[odd]))
+
+    pl.when(step == 0)(lambda: put(1, 0, 0))
+    pl.when(step == pl.num_programs(0) - 1)(lambda: put(0, 1, side - margin))
+
+
+def norm_regions(image, gain, side, margin, border, evens_of):
     height, width, channels = image.shape
     per_row = width // side
     edge = jax.ShapeDtypeStruct((margin, width, channels), BF16)
     flank = jax.ShapeDtypeStruct((height, border, channels), BF16)
     return pl.pallas_call(
-        functools.partial(norm_kernel, side),
+        functools.partial(norm_kernel, side, evens_of),
         grid=(height // side,),
         in_specs=[
             pl.BlockSpec((side, width, channels), lambda i: (i, 0, 0)),
@@ -101,11 +109,12 @@
 def context_kernel(
     side,
     margin,
+    evens_of,
     image_ref,
-    above_ref,
-    below_ref,
-    left_ref,
-    right_ref,
+    row_pair_ref,
+    row_other_ref,
+    col_pair_ref,
+    col_other_ref,
     gain_ref,
     weight_ref,
     lce_ref,
@@ -115,16 +124,19 @@
 ):
     step = pl.program_id(0)
     height, width, channels = image_ref.shape
-    border = left_ref.shape[1]
+    border = col_pair_ref.shape[1]
 
     @pl.when(step == 0)
     def _():
+        row_even, col_even = evens_of()
         inner = pl.ds(border, width)
-        padded[:margin, inner] = above_ref[...].astype(F32)
+        paired, other = row_pair_ref[...].astype(F32), row_other_ref[...].astype(F32)
+        padded[:margin, inner] = either(row_even, other, paired)
         padded[pl.ds(margin, height), inner] = image_ref[...].astype(F32)
-        padded[pl.ds(margin + height, margin), inner] = below_ref[...].astype(F32)
-        padded[:, :border] = left_ref[...].astype(F32)
-        padded[:, pl.ds(border + width, border)] = right_ref[...].astype(F32)
+        padded[pl.ds(margin + height, margin), inner] = either(row_even, paired, other)
+        paired, other = col_pair_ref[...].astype(F32), col_other_ref[...].astype(F32)
+        padded[:, :border] = either(col_even, other, paired)
+        padded[:, pl.ds(border + width, border)] = either(col_even, paired, other)
 
     rows = side + 2 * margin
     strip = padded[pl.ds(step * side, rows)]
@@ -144,14 +156,14 @@
     query_ref[...] = regions_of(inner, side).astype(BF16)
 
 
-def context_and_queries(image, around, gain, qkv_weight, lce_weight, side, margin):
+def context_and_queries(image, around, gain, qkv_weight, lce_weight, side, margin, evens_of):
     height, width, channels = image.shape
     border = around[-1].shape[1]
     tokens = height * width
     full = lambda a: pl.BlockSpec(a.shape, lambda i: (0,) * a.ndim)
     operands = (image, *around, gain.reshape(1, channels), qkv_weight, lce_weight)
     return pl.pallas_call(
-        functools.partial(context_kernel, side, margin),
+        functools.partial(context_kernel, side, margin, evens_of),
         grid=(height // side,),
         in_specs=[full(a) for a in operands],
         out_specs=[
@@ -176,21 +188,27 @@
     return (layer == 1) | (layer == 2)
 
 
-def frame_kernel(above_ref, below_ref, left_ref, right_ref, low_ref, high_ref):
-    margin, width = above_ref.shape[:2]
-    height, border = left_ref.shape[:2]
-    for out_ref, flank_ref, first in ((low_ref, left_ref, 0), (high_ref, right_ref, width - border)):
-        out_ref[pl.ds(0, margin)] = above_ref[:, pl.ds(first, border), :]
-        out_ref[pl.ds(margin, height)] = flank_ref[...]
-        out_ref[pl.ds(margin + height, margin)] = below_ref[:, pl.ds(first, border), :]
-
-
-def pack_kernel(jobs, options, outputs, framed, capacity, layers, place_of, wanted_ref, *refs):
+def frame_kernel(evens, row_refs, flank_refs, out_refs):
+    row_even, col_even = evens
+    margin, width = row_refs[0].shape[:2]
+    height, border = flank_refs[0].shape[:2]
+    paired, other = row_refs[0][...], row_refs[1][...]
+    above, below = either(row_even, other, paired), either(row_even, paired, other)
+    for out_ref, flag in ((out_refs[0], col_even), (out_refs[1], ~col_even)):
+        right = lambda rows: rows[:, width - border :]
+        left = lambda rows: rows[:, :border]
+        out_ref[pl.ds(0, margin)] = either(flag, right(above), left(above))
+        out_ref[pl.ds(margin, height)] = either(flag, flank_refs[1][...], flank_refs[0][...])
+        out_ref[pl.ds(margin + height, margin)] = either(flag, right(below), left(below))
+
+
+def pack_kernel(jobs, options, outputs, evens_of, capacity, layers, place_of, wanted_ref, *refs):
     peer, layer = place_of()
     sources = refs[: sum(options)]
     outs = refs[len(refs) - outputs :]
-    if framed:
-        frame_kernel(*refs[sum(options) : sum(options) + 4], *outs[-2:])
+    if evens_of is not None:
+        edges = refs[sum(options) : sum(options) + 4]
+        frame_kernel(evens_of(), edges[:2], edges[2:], outs[-2:])
     inside = is_inside(layer)
 
     def fill(source_ref, out_ref, place, distance, column):
@@ -215,7 +233,7 @@
         pl.when(~inside)(functools.partial(fill_all, 1, paired))
 
 
-def pack(jobs, shapes, sources, place_of, wanted, capacity, layers, frame=()):
+def pack(jobs, shapes, sources, place_of, wanted, capacity, layers, frame=(), evens_of=None):
     flat = sum(sources, [])
     if frame:
         margin, (height, border, channels) = frame[0].shape[0], frame[2].shape
@@ -227,7 +245,7 @@
             tuple(jobs),
             tuple(map(len, sources)),
             len(shapes),
-            len(frame) > 0,
+            evens_of,
             capacity,
             layers,
             place_of,
@@ -342,31 +360,27 @@
     return lifted * (0.5 + 0.5 * jnp.tanh(inner))
 
 
-def tail_kernel(side, picks, batch, early, options, place_of, position_ref, *refs):
-    late_count = sum(options)
-    late = refs[:late_count]
-    (
-        fetched_ref,
-        query_ref,
-        context_ref,
-        image_ref,
-        qkv_ref,
-        out_weight_ref,
-        gain_ref,
-        up_ref,
-        down_ref,
-        result_ref,
-        landed,
-        combined_ref,
-        sems,
-    ) = refs[late_count:]
+def tail_kernel(
+    side,
+    picks,
+    batch,
+    early,
+    position_ref,
+    late_ref,
+    fetched_ref,
+    query_ref,
+    context_ref,
+    image_ref,
+    qkv_ref,
+    out_weight_ref,
+    gain_ref,
+    up_ref,
+    down_ref,
+    result_ref,
+    combined_ref,
+):
     step = pl.program_id(0)
     last = pl.num_programs(0) - 2
-
-    @pl.when(step == 0)
-    def _():
-        combined_ref[...] = jnp.zeros_like(combined_ref)
-        load_all(options, late, landed, sems, place_of()[1])
 
     area, channels = fetched_ref.shape[1:]
     exponent = (channels // HEADS) ** (-0.5) * math.log2(math.e)
@@ -375,9 +389,8 @@
     def piece(which):
         at = position_ref[first + which]
         is_late = at >= early
-        return jnp.where(is_late, landed[jnp.where(is_late, at - early, 0)], fetched_ref[which])
-
-    previous = combined_ref[...]
+        return jnp.where(is_late, late_ref[jnp.where(is_late, at - early, 0)], fetched_ref[which])
+
     chunk = PAIR * area
 
     def attention(region):
@@ -402,7 +415,7 @@
     def feed_forward(part):
         columns = pl.ds(part * PAIR * side, PAIR * side)
         image = regions_of(image_ref[:, columns, :].astype(F32), side)
-        combined = previous[part * chunk : (part + 1) * chunk]
+        combined = combined_ref[pl.ds(part * chunk, chunk), :]
         residual = image + jnp.dot(combined, out_weight_ref[...], preferred_element_type=F32)
         yield True
         stored = residual.astype(BF16).astype(F32)
@@ -416,13 +429,18 @@
         result_ref[:, columns, :] = strip_of(refined, side, PAIR * side).astype(BF16)
         yield True
 
-    lines = [feed_forward(part) for part in range(batch // PAIR)]
-    lines += [attention(region) for region in range(batch)]
-    while lines:
-        lines = [line for line in lines if next(line, None) is not None]
-
-
-def tail(position, early, fetched, late, place_of, queries, context, image, weights, side, picks):
+    def run(forward, attend):
+        lines = [feed_forward(part) for part in range(batch // PAIR)] if forward else []
+        lines += [attention(region) for region in range(batch)] if attend else []
+        while lines:
+            lines = [line for line in lines if next(line, None) is not None]
+
+    pl.when(step == 0)(lambda: run(False, True))
+    pl.when((step > 0) & (step <= last))(lambda: run(True, True))
+    pl.when(step > last)(lambda: run(True, False))
+
+
+def tail(position, early, fetched, late, queries, context, image, weights, side, picks):
     height, width, channels = image.shape
     area = side * side
     per_row = width // side
@@ -438,31 +456,22 @@
         lambda i, position: (before(i) // halves, before(i) % halves, 0),
     )
     regions = pl.BlockSpec((batch * picks, area, channels), lambda i, position: (now(i), 0, 0))
-    total = rows_of(late)
-    flat = sum(late, [])
     return pl.pallas_call(
-        functools.partial(
-            tail_kernel, side, picks, batch, early, tuple(map(len, late)), place_of
-        ),
+        functools.partial(tail_kernel, side, picks, batch, early),
         grid_spec=pltpu.PrefetchScalarGridSpec(
             num_scalar_prefetch=1,
             grid=(steps + 1,),
-            in_specs=[pl.BlockSpec(memory_space=pl.ANY)] * len(flat)
-            + [regions, tokens, tokens, strip]
+            in_specs=[pl.BlockSpec(memory_space=pltpu.VMEM), regions, tokens, tokens, strip]
             + [full(w) for w in weights],
             out_specs=strip,
-            scratch_shapes=[
-                pltpu.VMEM((total, area, channels), BF16),
-                pltpu.VMEM((batch * area, channels), BF16),
-                pltpu.SemaphoreType.DMA((len(late),)),
-            ],
+            scratch_shapes=[pltpu.VMEM((batch * area, channels), BF16)],
         ),
         out_shape=jax.ShapeDtypeStruct(image.shape, BF16),
         cost_estimate=pl.CostEstimate(
             flops=image.size * 4000, bytes_accessed=16 * image.size, transcendentals=40 * image.size
         ),
         name="tail",
-    )(position, *flat, fetched, queries, context, image, *weights)
+    )(position, late, fetched, queries, context, image, *weights)
 
 
 def layer_blocks(block, layers):
@@ -498,6 +507,9 @@
 
     def place_of():
         return lax.axis_index("rows") * across + lax.axis_index("x"), lax.axis_index("z")
+
+    def evens_of():
+        return lax.axis_index("rows") % 2 == 0, lax.axis_index("x") % 2 == 0
 
     peer, layer = place_of()
 
@@ -529,14 +541,14 @@
     )
 
     margin = (lce_weight.shape[0] - 1) // 2
-    normed, *edges = norm_regions(image, norm_gain, side, margin, 8)
+    normed, *edges = norm_regions(image, norm_gain, side, margin, 8, evens_of)
 
     def swap(part, far):
         return lax.ppermute(part, ("rows", "x"), [(i, i ^ far) for i in range(peers)])
 
     held = layer_blocks(normed, layers)
     given = [swap(normed, far) for far in whole]
-    above, below = from_sides(*edges[:2], "rows")
+    near_rows = with_pairs(edges[:2], "rows", lax.axis_size("rows"))
 
     tile = normed.shape[1:]
     position, total = jnp.zeros_like(slot), 0
@@ -558,12 +570,20 @@
     shapes = [(len(relayed) * capacity, *tile)] + [(capacity, *tile)] * len(direct)
     shapes += [(peers, capacity, *tile)]
     sources = [[normed], *([part] for part in given), held[1]]
-    *parts, joint, low, high = pack(
-        jobs, shapes, sources, place_of, wanted, capacity, layers, (above, below, *edges[2:])
+    *parts, joint, paired, other = pack(
+        jobs,
+        shapes,
+        sources,
+        place_of,
+        wanted,
+        capacity,
+        layers,
+        (*near_rows, *edges[2:]),
+        evens_of,
     )
     got = [swap(part, far) for part, far in zip(parts, [twin, *direct])]
     joint = lax.all_to_all(joint, ("rows", "x"), 0, 0, tiled=True)
-    around = (above, below, *from_sides(low, high, ("z", "x")))
+    around = (*near_rows, *with_pairs((paired, other), ("z", "x"), layers * across))
     arrived.append([])
     landing([normed], ((step == 0) & (distance == 0), local_index))
     for far, part in zip(whole, given):
@@ -592,20 +612,20 @@
             got = lax.all_to_all(parts[0], ("rows", "x"), 0, 0, tiled=True)
         else:
             got = [swap(part, far) for far, part in enumerate(parts, 1)]
-        early = total
-        arrived.append([])
         landing(held[chunk], ((step == chunk) & (distance == 0), local_index))
         if last:
+            early = total
+            arrived.append([])
             elsewhere = (step == chunk) & (distance != 0)
             landing([got.reshape(-1, *tile)], (elsewhere, owner_peer * capacity + slot))
         else:
             for far, part in enumerate(got, 1):
                 landing([part], ((step == chunk) & (distance == far), slot))
-    late = arrived.pop()
+    ((late,),) = arrived.pop()
     fetched = collect(position, sum(arrived, []), place_of, math.gcd(pair_count, 8))
 
     context, queries = context_and_queries(
-        image, around, norm_gain, qkv_weight, lce_weight, side, margin
+        image, around, norm_gain, qkv_weight, lce_weight, side, margin, evens_of
     )
     weights = (
         qkv_weight,
@@ -614,7 +634,7 @@
         up_weight,
         down_weight,
     )
-    return tail(position, early, fetched, late, place_of, queries, context, image, weights, side, pick_count)
+    return tail(position, early, fetched, late, queries, context, image, weights, side, pick_count)
 
 
 def solution(mesh):

time: 124 us -> 124 us (level)
  waiting for transfers between devices: 31.5 us -> 38.3 us
  starting transfers between devices: 40.3 us -> 35.9 us
    ppermute x5, waiting for transfers between devices: 29.8 us -> 34.7 us  [hop(): return lax.ppermute(block, 'z', pairs)]
    ppermute x4, starting transfers between devices: 7.39 us -> 2.94 us  [with_pairs(): lax.ppermute(part, axis, pairs)]
    ppermute x12, waiting for transfers between devices: 1.65 us -> 3.64 us  [swap(): lax.ppermute(part, ('rows', 'x'), [(i, i ^ far) for i in range(peers)])]
    ppermute x12, starting transfers between devices: 18.3 us -> 19.9 us  [swap(): lax.ppermute(part, ('rows', 'x'), [(i, i ^ far) for i in range(peers)])]
    ppermute x5, starting transfers between devices: 7.2 us -> 5.66 us  [hop(): return lax.ppermute(block, 'z', pairs)]
    pallas_call x3, Pallas kernels: 23.3 us -> 22 us  [the longest x1 12.4 us: tail(): pl.pallas_call(functools.partial(tail_kernel, side, picks, batch, early),...]
    unnamed x49 -> x47, local copies, waits for them, and re-layouts: 4.17 us -> 4.21 us
  transfers between devices with their start and end apart: 23 -> 23, of which waited for: 5 -> 6; matrix products, arithmetic and copies ran while one was open for 2% -> 2% of each run, Pallas kernels for 16% -> 16%
where the time goes in v3:
time: 124 us
  waiting for transfers between devices  38.3 us (31%)
  Pallas kernels  36.2 us (29%)
  starting transfers between devices  35.9 us (29%)
  blocking collectives  7.62 us (6%)
  local copies, waits for them, and re-layouts  4.31 us (3%)
    ppermute x5, waiting for transfers between devices, hop(): return lax.ppermute(block, 'z', pairs)  34.7 us
    ppermute x12, starting transfers between devices, swap(): lax.ppermute(part, ('rows', 'x'), [(i, i ^ far) for i in range(peers)])  19.9 us
    pallas_call x1, Pallas kernels, tail(): pl.pallas_call(functools.partial(tail_kernel, side, picks, batch, early),...  12.4 us
    pallas_call x3, Pallas kernels, pack(): pl.pallas_call(functools.partial(pack_kernel, tuple(jobs), tuple(map(len,...  7.73 us
    all_to_all x1, blocking collectives, block(): lax.all_to_all(requests.reshape(peers, 1, lanes), ('rows', 'x'), 0, 0, ti...  7.62 us
    pallas_call x1, Pallas kernels, collect(): pl.pallas_call(functools.partial(collect_kernel, tuple(map(len, sources))...  6.48 us
    pallas_call x1, Pallas kernels, context_and_queries(): pl.pallas_call(functools.partial(context_kernel, side, margin, evens_of),...  5.94 us
    ppermute x5, starting transfers between devices, hop(): return lax.ppermute(block, 'z', pairs)  5.66 us
  transfers between devices with their start and end apart: 23, of which 6 were waited for; matrix products, arithmetic and copies ran while one was open for 2% of the time, Pallas kernels for 16%

profile of v3, /device:TPU:0, one launch (start us, length us, event | category | flops | bytes accessed | tf_op | source)
XLA Modules:
  0.0 123.7 jit_solution(12540867564162064785)
XLA Ops:
  0.0 3.7 %norm_regions.1 = (bf16[32,64,128]{2,1,0:T(8,128)(2,1)}, bf16[2,64,128]{2,1,0:T(8,128)(2,1)}, bf16[2,64,128]{2,1,0:T(8,128)(2,1)}, bf16[32,8,128]{2,1,0:T(8,128)(2,1)}, bf16[32,8,128]{2,1,0:T(8,128)(2,1)}) custom-call(bf16[32,64,128]{2,1,0:T(8,128)(2,1)} %image_ref.5, f32[1,128]{1,0:T(1,128)} %bitcast.8), custom_call_target="tpu_custom_call" | custom-call | flops 2621440 | bytes 1048576 | tf_op jit(solution)/shard_map/norm_regions/pallas_call | solution.py:81
  3.7 3.1 %collective-permute-start.5 = (bf16[32,64,128]{2,1,0:T(8,128)(2,1)}, bf16[32,64,128]{2,1,0:T(8,128)(2,1)S(1)}, u32[]{:S(2)}, u32[]{:S(2)}) collective-permute-start(bf16[32,64,128]{2,1,0:T(8,128)(2,1)} %get-tuple-element.25.refs_0_), channel_id=1, source_target_pairs={{0,16},{1,17},{8,24},{9,25},{16,0},{17,1},{24,8},{25,9},{2,18},{3,... | collective-permute-start | bytes 1572872 | tf_op jit(solution)/shard_map/ppermute | solution.py:547
  6.7 1.5 %collective-permute-start.4 = (bf16[32,64,128]{2,1,0:T(8,128)(2,1)}, bf16[32,64,128]{2,1,0:T(8,128)(2,1)S(1)}, u32[]{:S(2)}, u32[]{:S(2)}) collective-permute-start(bf16[32,64,128]{2,1,0:T(8,128)(2,1)} %get-tuple-element.25.refs_0_), channel_id=1, source_target_pairs={{0,1},{1,0},{8,9},{9,8},{16,17},{17,16},{24,25},{25,24},{2,3},{3,2... | collective-permute-start | bytes 1572872 | tf_op jit(solution)/shard_map/ppermute | solution.py:547
  8.2 1.6 %collective-permute-start.1 = (bf16[32,64,128]{2,1,0:T(8,128)(2,1)}, bf16[32,64,128]{2,1,0:T(8,128)(2,1)}, u32[]{:S(2)}, u32[]{:S(2)}) collective-permute-start(bf16[32,64,128]{2,1,0:T(8,128)(2,1)} %get-tuple-element.25.refs_0_), channel_id=1, source_target_pairs={{0,2},{2,0},{4,6},{6,4},{1,3},{3,1},{5,7},{7,5},{8,10},{10,8},{12,... | collective-permute-start | bytes 1572872 | tf_op jit(solution)/shard_map/ppermute | solution.py:485
  9.8 0.7 collective-permute-start.7
  10.5 0.8 copy.12
  11.3 0.1 reshape.306
  11.4 0.2 convert_reduce_fusion
  11.6 10.0 %collective-permute-done.1.refs_3_.refs_6_ = bf16[32,64,128]{2,1,0:T(8,128)(2,1)} collective-permute-done((bf16[32,64,128]{2,1,0:T(8,128)(2,1)}, bf16[32,64,128]{2,1,0:T(8,128)(2,1)}, u32[]{:S(2)}, u32[]{:S(2)}) %collective-permute-start.1) | collective-permute-done | bytes 524320 | tf_op jit(solution)/shard_map/ppermute | solution.py:485
  21.6 0.7 collective-permute-start.2
  22.3 0.6 and_select_fusion.19
  22.9 0.2 select_reduce_fusion
  23.1 7.6 %all_to_all.15.wanted_ref = s32[8,1,128]{2,1,0:T(1,128)} all-to-all(s32[8,1,128]{2,1,0:T(1,128)S(1)} %bitcast.7), channel_id=1, replica_groups=mesh['rows'=4,'z'=4,'x'=2] {'rows','x'}, dimensions={0} | all-to-all | bytes 8192 | tf_op jit(solution)/shard_map/all_to_all | solution.py:539
  30.7 0.0 collective-permute-done.5.refs_2_
  30.8 0.5 copy-done.18
  31.3 0.0 copy-done.19
  31.3 0.2 copy-done.4
  31.5 0.2 copy-done.5
  31.8 3.1 %pack.4 = (bf16[24,64,128]{2,1,0:T(8,128)(2,1)}, bf16[8,64,128]{2,1,0:T(8,128)(2,1)}, bf16[8,64,128]{2,1,0:T(8,128)(2,1)}, bf16[8,8,64,128]{3,2,1,0:T(8,128)(2,1...) custom-call(s32[8,1,128]{2,1,0:T(1,128)} %all_to_all.15.wanted_ref, ...), custom_call_target="tpu_custom_call" | custom-call | bytes 3702784 | tf_op jit(solution)/shard_map/pack/pallas_call | solution.py:242
  34.9 3.6 %all-to-all-start.2 = ((bf16[8,8,64,128]{3,2,1,0:T(8,128)(2,1)}), bf16[8,8,64,128]{3,2,1,0:T(8,128)(2,1)S(1)}, u32[]{:S(2)}, u32[]{:S(2)}) async-start(bf16[8,8,64,128]{3,2,1,0:T(8,128)(2,1)} %get-tuple-element.33), calls=%async_computation.2 | async-start | bytes 2097152 | tf_op jit(solution)/shard_map/all_to_all | solution.py:585
  38.4 0.8 collective-permute-start
  39.3 1.3 %collective-permute-start.3 = (bf16[32,64,128]{2,1,0:T(8,128)(2,1)S(1)}, bf16[32,64,128]{2,1,0:T(8,128)(2,1)S(1)}, u32[]{:S(2)}, u32[]{:S(2)}) collective-permute-start(bf16[32,64,128]{2,1,0:T(8,128)(2,1)S(1)} %collective-permute-done.2.refs_0_.refs_8_), channel_id=1, source_target_pairs={{2,0},{4,6},{3,1},{5,7},{10,8},{12,14},{11,9},{13,15},{18,16},{20,... | collective-permute-start | bytes 1572872 | tf_op jit(solution)/shard_map/ppermute | solution.py:485
  40.6 18.2 %collective-permute-done.3.refs_1_.refs_18_ = bf16[32,64,128]{2,1,0:T(8,128)(2,1)S(1)} collective-permute-done((bf16[32,64,128]{2,1,0:T(8,128)(2,1)S(1)}, bf16[32,64,128]{2,1,0:T(8,128)(2,1)S(1)}, u32[]{:S(2)}, u32[]{:S(2)}) %collective-permute-start.3) | collective-permute-done | bytes 524320 | tf_op jit(solution)/shard_map/ppermute | solution.py:485
  58.8 0.8 copy-done.7
  59.7 2.4 %pack.3 = bf16[8,8,64,128]{3,2,1,0:T(8,128)(2,1)} custom-call(s32[8,1,128]{2,1,0:T(1,128)} %all_to_all.15.wanted_ref, bf16[32,64,128]{2,1,0:T(8,128)(2,1)} %copy-done.6, bf16[32,64,128]{2,1,0:T(8,128)(2,1)} %copy-done.7), custom_call_target="tpu_custom_call" | custom-call | bytes 2097152 | tf_op jit(solution)/shard_map/pack/pallas_call | solution.py:242
  62.0 3.9 %all-to-all-start.1 = ((bf16[8,8,64,128]{3,2,1,0:T(8,128)(2,1)}), bf16[8,8,64,128]{3,2,1,0:T(8,128)(2,1)S(1)}, u32[]{:S(2)}, u32[]{:S(2)}) async-start(bf16[8,8,64,128]{3,2,1,0:T(8,128)(2,1)} %pack.3), calls=%async_computation.1 | async-start | bytes 2097152 | tf_op jit(solution)/shard_map/all_to_all | solution.py:612
  65.9 1.3 %collective-permute-start.11 = (bf16[32,64,128]{2,1,0:T(8,128)(2,1)}, bf16[32,64,128]{2,1,0:T(8,128)(2,1)S(1)}, u32[]{:S(2)}, u32[]{:S(2)}) collective-permute-start(bf16[32,64,128]{2,1,0:T(8,128)(2,1)} %copy-done.6), channel_id=1, source_target_pairs={{2,0},{4,6},{3,1},{5,7},{10,8},{12,14},{11,9},{13,15},{18,16},{20,... | collective-permute-start | bytes 1572872 | tf_op jit(solution)/shard_map/ppermute | solution.py:485
  67.2 0.6 collective-permute-start.8
  67.7 1.6 %collective-permute-start.19 = (bf16[36,8,128]{2,1,0:T(8,128)(2,1)}, bf16[36,8,128]{2,1,0:T(8,128)(2,1)S(1)}, u32[]{:S(2)}, u32[]{:S(2)}) collective-permute-start(bf16[36,8,128]{2,1,0:T(8,128)(2,1)} %get-tuple-element.41), channel_id=1, source_target_pairs={{0,1},{1,0},{2,3},{3,2},{4,5},{5,4},{6,7},{7,6},{8,9},{9,8},{10,11... | collective-permute-start | bytes 221192 | tf_op jit(solution)/shard_map/ppermute | solution.py:23
  69.4 0.7 collective-permute-start.20
  70.0 6.3 %collective-permute-start.9 = (bf16[8,64,128]{2,1,0:T(8,128)(2,1)}, bf16[8,64,128]{2,1,0:T(8,128)(2,1)S(1)}, u32[]{:S(2)}, u32[]{:S(2)}) collective-permute-start(bf16[8,64,128]{2,1,0:T(8,128)(2,1)} %get-tuple-element.31), channel_id=1, source_target_pairs={{0,17},{1,16},{8,25},{9,24},{16,1},{17,0},{24,9},{25,8},{2,19},{3,... | collective-permute-start | bytes 393224 | tf_op jit(solution)/shard_map/ppermute | solution.py:547
  76.3 6.4 %collective-permute-done.11.refs_1_.refs_9_ = bf16[32,64,128]{2,1,0:T(8,128)(2,1)S(1)} collective-permute-done((bf16[32,64,128]{2,1,0:T(8,128)(2,1)}, bf16[32,64,128]{2,1,0:T(8,128)(2,1)S(1)}, u32[]{:S(2)}, u32[]{:S(2)}) %collective-permute-start.11) | collective-permute-done | bytes 524320 | tf_op jit(solution)/shard_map/ppermute | solution.py:485
  82.8 0.9 collective-permute-start.10
  83.7 2.3 %pack.5 = (bf16[8,64,128]{2,1,0:T(8,128)(2,1)}, bf16[8,64,128]{2,1,0:T(8,128)(2,1)}, bf16[8,64,128]{2,1,0:T(8,128)(2,1)}, bf16[8,64,128]{2,1,0:T(8,128)(2,1)}, b...) custom-call(s32[8,1,128]{2,1,0:T(1,128)} %all_to_all.15.wanted_ref, ...), custom_call_target="tpu_custom_call" | custom-call | bytes 1835008 | tf_op jit(solution)/shard_map/pack/pallas_call | solution.py:242
  86.0 1.1 collective-permute-start.12
  87.1 1.3 %collective-permute-start.13 = (bf16[8,64,128]{2,1,0:T(8,128)(2,1)}, bf16[8,64,128]{2,1,0:T(8,128)(2,1)S(1)}, u32[]{:S(2)}, u32[]{:S(2)}) collective-permute-start(bf16[8,64,128]{2,1,0:T(8,128)(2,1)} %get-tuple-element.35), channel_id=1, source_target_pairs={{0,8},{1,9},{8,0},{9,1},{16,24},{17,25},{24,16},{25,17},{2,10},{3,... | collective-permute-start | bytes 393224 | tf_op jit(solution)/shard_map/ppermute | solution.py:547
  88.4 0.4 collective-permute-start.14
  88.8 0.4 collective-permute-done.10.refs_5_
  89.2 0.9 collective-permute-start.15
  90.1 2.0 %collective-permute-start.16 = (bf16[8,64,128]{2,1,0:T(8,128)(2,1)}, bf16[8,64,128]{2,1,0:T(8,128)(2,1)S(1)}, u32[]{:S(2)}, u32[]{:S(2)}) collective-permute-start(bf16[8,64,128]{2,1,0:T(8,128)(2,1)} %get-tuple-element.38), channel_id=1, source_target_pairs={{0,17},{1,16},{8,25},{9,24},{16,1},{17,0},{24,9},{25,8},{2,19},{3,... | collective-permute-start | bytes 393224 | tf_op jit(solution)/shard_map/ppermute | solution.py:547
  92.1 0.2 collective-permute-done.12.refs_10_
  92.4 1.9 %collective-permute-start.18 = (bf16[8,64,128]{2,1,0:T(8,128)(2,1)}, bf16[8,64,128]{2,1,0:T(8,128)(2,1)}, u32[]{:S(2)}, u32[]{:S(2)}) collective-permute-start(bf16[8,64,128]{2,1,0:T(8,128)(2,1)} %get-tuple-element.40), channel_id=1, source_target_pairs={{0,25},{1,24},{8,17},{9,16},{16,9},{17,8},{24,1},{25,0},{2,27},{3,... | collective-permute-start | bytes 393224 | tf_op jit(solution)/shard_map/ppermute | solution.py:547
  94.3 5.9 %context.1 = (f32[2048,128]{1,0:T(8,128)}, bf16[2048,128]{1,0:T(8,128)(2,1)}) custom-call(bf16[32,64,128]{2,1,0:T(8,128)(2,1)} %image_ref.5, bf16[2,64,128]{2,1,0:T(8,128)(2,1)} %copy-done.18, bf16[2,64,128]{2,1,0:T(8,128)(2,1)} %copy-done.19, bf16[36,8,128]{2,1,0:T(8,128)(2,1)} %copy-done.20, bf16[36,8,128]{2,1,0:T(8,128)(2,1)} %copy-done.21, ...), custom_call_target="tpu_custom_call" | custom-call | flops 157286400 | bytes 2621440 | tf_op jit(solution)/shard_map/context/pallas_call | solution.py:165
  100.3 3.0 %collective-permute-done.17.refs_15_ = bf16[8,64,128]{2,1,0:T(8,128)(2,1)S(1)} collective-permute-done((bf16[8,64,128]{2,1,0:T(8,128)(2,1)}, bf16[8,64,128]{2,1,0:T(8,128)(2,1)S(1)}, u32[]{:S(2)}, u32[]{:S(2)}) %collective-permute-start.17) | collective-permute-done | bytes 131104 | tf_op jit(solution)/shard_map/ppermute | solution.py:547
  103.3 0.6 copy-done.17
  103.9 6.5 %collect.1.fetched_ref = bf16[128,64,128]{2,1,0:T(8,128)(2,1)} custom-call(s32[128]{0:T(128)} %get-tuple-element.45.position_ref, bf16[32,64,128]{2,1,0:T(8,128)(2,1)} %get-tuple-element.25.refs_0_, bf16[32,64,128]{2,1,0:T(8,128)(2,1)} %copy-done.5, bf16[32,64,128]{2,1,0:T(8,128)(2,1)} %copy-done.4, bf16[24,64,128]{2,1,0:T(8,128)(2,1)} %copy-done.9, ...), custom_call_target="tpu_custom_call" | custom-call | bytes 7864320 | tf_op jit(solution)/shard_map/collect/pallas_call | solution.py:308
  110.4 1.0 copy-done.8
  111.4 12.4 %tail.1 = bf16[32,64,128]{2,1,0:T(8,128)(2,1)} custom-call(s32[128]{0:T(128)} %get-tuple-element.45.position_ref, bf16[64,64,128]{2,1,0:T(8,128)(2,1)} %bitcast.6, bf16[128,64,128]{2,1,0:T(8,128)(2,1)} %collect.1.fetched_ref, bf16[2048,128]{1,0:T(8,128)(2,1)} %get-tuple-element.43.query_ref, f32[2048,128]{1,0:T(8,128)} %get-tuple-element.44.context_ref, ...), custom_call_target="tpu_custom_call" | custom-call | flops 1048576000 | bytes 4194304 | tf_op jit(solution)/shard_map/tail/pallas_call | solution.py:459
  (59 shorter events, 0.2 us)
Async XLA Ops:
  3.7 27.1 %collective-permute-start.5 = (bf16[32,64,128]{2,1,0:T(8,128)(2,1)}, bf16[32,64,128]{2,1,0:T(8,128)(2,1)S(1)}, u32[]{:S(2)}, u32[]{:S(2)}) collective-permute-start(bf16[32,64,128]{2,1,0:T(8,128)(2,1)} %get-tuple-element.25.refs_0_), channel_id=1, source_target_pairs={{0,16},{1,17},{8,24},{9,25},{16,0},{17,1},{24,8},{25,9},{2,18},{3,... | collective-permute-start | bytes 1572872 | tf_op jit(solution)/shard_map/ppermute | solution.py:547
  6.7 24.0 %collective-permute-start.4 = (bf16[32,64,128]{2,1,0:T(8,128)(2,1)}, bf16[32,64,128]{2,1,0:T(8,128)(2,1)S(1)}, u32[]{:S(2)}, u32[]{:S(2)}) collective-permute-start(bf16[32,64,128]{2,1,0:T(8,128)(2,1)} %get-tuple-element.25.refs_0_), channel_id=1, source_target_pairs={{0,1},{1,0},{8,9},{9,8},{16,17},{17,16},{24,25},{25,24},{2,3},{3,2... | collective-permute-start | bytes 1572872 | tf_op jit(solution)/shard_map/ppermute | solution.py:547
  8.2 13.4 %collective-permute-start.1 = (bf16[32,64,128]{2,1,0:T(8,128)(2,1)}, bf16[32,64,128]{2,1,0:T(8,128)(2,1)}, u32[]{:S(2)}, u32[]{:S(2)}) collective-permute-start(bf16[32,64,128]{2,1,0:T(8,128)(2,1)} %get-tuple-element.25.refs_0_), channel_id=1, source_target_pairs={{0,2},{2,0},{4,6},{6,4},{1,3},{3,1},{5,7},{7,5},{8,10},{10,8},{12,... | collective-permute-start | bytes 1572872 | tf_op jit(solution)/shard_map/ppermute | solution.py:485
  9.8 20.9 %collective-permute-start.6 = (bf16[2,64,128]{2,1,0:T(8,128)(2,1)}, bf16[2,64,128]{2,1,0:T(8,128)(2,1)S(1)}, u32[]{:S(2)}, u32[]{:S(2)}) collective-permute-start(bf16[2,64,128]{2,1,0:T(8,128)(2,1)} %get-tuple-element.26), channel_id=1, source_target_pairs={{0,8},{8,0},{16,24},{24,16},{1,9},{9,1},{17,25},{25,17},{2,10},{10... | collective-permute-start | bytes 98312 | tf_op jit(solution)/shard_map/ppermute | solution.py:23
  9.8 20.9 %collective-permute-start.7 = (bf16[2,64,128]{2,1,0:T(8,128)(2,1)}, bf16[2,64,128]{2,1,0:T(8,128)(2,1)S(1)}, u32[]{:S(2)}, u32[]{:S(2)}) collective-permute-start(bf16[2,64,128]{2,1,0:T(8,128)(2,1)} %get-tuple-element.27), channel_id=1, source_target_pairs={{8,16},{16,8},{9,17},{17,9},{10,18},{18,10},{11,19},{19,11},{12,20... | collective-permute-start | bytes 98312 | tf_op jit(solution)/shard_map/ppermute | solution.py:23
  21.6 17.6 %collective-permute-start.2 = (bf16[32,64,128]{2,1,0:T(8,128)(2,1)}, bf16[32,64,128]{2,1,0:T(8,128)(2,1)S(1)}, u32[]{:S(2)}, u32[]{:S(2)}) collective-permute-start(bf16[32,64,128]{2,1,0:T(8,128)(2,1)} %collective-permute-done.1.refs_3_.refs_6_), channel_id=1, source_target_pairs={{2,4},{4,2},{3,5},{5,3},{10,12},{12,10},{11,13},{13,11},{18,20},{2... | collective-permute-start | bytes 1572872 | tf_op jit(solution)/shard_map/ppermute | solution.py:485
  30.7 0.6 copy-start.18
  30.7 0.6 copy-start.19
  30.8 0.8 copy-start.4
  30.8 1.0 copy-start.5
  31.8 6.7 %copy-start.3 = (bf16[32,64,128]{2,1,0:T(8,128)(2,1)S(1)}, bf16[32,64,128]{2,1,0:T(8,128)(2,1)}, u32[]{:S(2)}) copy-start(bf16[32,64,128]{2,1,0:T(8,128)(2,1)} %get-tuple-element.25.refs_0_) | copy-start | bytes 1572868
  34.9 27.1 %all-to-all-start.2 = ((bf16[8,8,64,128]{3,2,1,0:T(8,128)(2,1)}), bf16[8,8,64,128]{3,2,1,0:T(8,128)(2,1)S(1)}, u32[]{:S(2)}, u32[]{:S(2)}) async-start(bf16[8,8,64,128]{3,2,1,0:T(8,128)(2,1)} %get-tuple-element.33), calls=%async_computation.2 | async-start | bytes 2097152 | tf_op jit(solution)/shard_map/all_to_all | solution.py:585
  38.4 44.3 %copy-start.22 = (bf16[8,64,128]{2,1,0:T(8,128)(2,1)S(1)}, bf16[8,64,128]{2,1,0:T(8,128)(2,1)}, u32[]{:S(2)}) copy-start(bf16[8,64,128]{2,1,0:T(8,128)(2,1)} %get-tuple-element.32) | copy-start | bytes 393220
  38.4 2.2 %collective-permute-start = (bf16[32,64,128]{2,1,0:T(8,128)(2,1)S(1)}, bf16[32,64,128]{2,1,0:T(8,128)(2,1)S(1)}, u32[]{:S(2)}, u32[]{:S(2)}) collective-permute-start(bf16[32,64,128]{2,1,0:T(8,128)(2,1)S(1)} %copy-done.3), channel_id=1, source_target_pairs={{2,4},{4,2},{3,5},{5,3},{10,12},{12,10},{11,13},{13,11},{18,20},{2... | collective-permute-start | bytes 1572872 | tf_op jit(solution)/shard_map/ppermute | solution.py:485
  39.3 22.7 %copy-start.1 = (bf16[32,64,128]{2,1,0:T(8,128)(2,1)}, bf16[32,64,128]{2,1,0:T(8,128)(2,1)S(1)}, u32[]{:S(2)}) copy-start(bf16[32,64,128]{2,1,0:T(8,128)(2,1)S(1)} %collective-permute-done.2.refs_0_.refs_8_) | copy-start | bytes 1572868
  39.3 19.5 %collective-permute-start.3 = (bf16[32,64,128]{2,1,0:T(8,128)(2,1)S(1)}, bf16[32,64,128]{2,1,0:T(8,128)(2,1)S(1)}, u32[]{:S(2)}, u32[]{:S(2)}) collective-permute-start(bf16[32,64,128]{2,1,0:T(8,128)(2,1)S(1)} %collective-permute-done.2.refs_0_.refs_8_), channel_id=1, source_target_pairs={{2,0},{4,6},{3,1},{5,7},{10,8},{12,14},{11,9},{13,15},{18,16},{20,... | collective-permute-start | bytes 1572872 | tf_op jit(solution)/shard_map/ppermute | solution.py:485
  40.6 18.2 %copy-start.6 = (bf16[32,64,128]{2,1,0:T(8,128)(2,1)}, bf16[32,64,128]{2,1,0:T(8,128)(2,1)S(1)}, u32[]{:S(2)}) copy-start(bf16[32,64,128]{2,1,0:T(8,128)(2,1)S(1)} %collective-permute-done.refs_0_.refs_17_) | copy-start | bytes 1572868
  58.8 0.8 copy-start.7
  62.0 41.2 %copy-start = (bf16[8,8,64,128]{3,2,1,0:T(8,128)(2,1)}, bf16[8,8,64,128]{3,2,1,0:T(8,128)(2,1)S(1)}, u32[]{:S(2)}) copy-start(bf16[8,8,64,128]{3,2,1,0:T(8,128)(2,1)S(1)} %all-to-all-done.2) | copy-start | bytes 3145732
  62.0 48.4 %all-to-all-start.1 = ((bf16[8,8,64,128]{3,2,1,0:T(8,128)(2,1)}), bf16[8,8,64,128]{3,2,1,0:T(8,128)(2,1)S(1)}, u32[]{:S(2)}, u32[]{:S(2)}) async-start(bf16[8,8,64,128]{3,2,1,0:T(8,128)(2,1)} %pack.3), calls=%async_computation.1 | async-start | bytes 2097152 | tf_op jit(solution)/shard_map/all_to_all | solution.py:612
  65.9 16.9 %collective-permute-start.11 = (bf16[32,64,128]{2,1,0:T(8,128)(2,1)}, bf16[32,64,128]{2,1,0:T(8,128)(2,1)S(1)}, u32[]{:S(2)}, u32[]{:S(2)}) collective-permute-start(bf16[32,64,128]{2,1,0:T(8,128)(2,1)} %copy-done.6), channel_id=1, source_target_pairs={{2,0},{4,6},{3,1},{5,7},{10,8},{12,14},{11,9},{13,15},{18,16},{20,... | collective-permute-start | bytes 1572872 | tf_op jit(solution)/shard_map/ppermute | solution.py:485
  67.2 22.9 %collective-permute-start.8 = (bf16[24,64,128]{2,1,0:T(8,128)(2,1)}, bf16[24,64,128]{2,1,0:T(8,128)(2,1)S(1)}, u32[]{:S(2)}, u32[]{:S(2)}) collective-permute-start(bf16[24,64,128]{2,1,0:T(8,128)(2,1)} %get-tuple-element.30), channel_id=1, source_target_pairs={{0,8},{1,9},{8,0},{9,1},{16,24},{17,25},{24,16},{25,17},{2,10},{3,... | collective-permute-start | bytes 1179656 | tf_op jit(solution)/shard_map/ppermute | solution.py:547
  67.7 18.3 %collective-permute-start.19 = (bf16[36,8,128]{2,1,0:T(8,128)(2,1)}, bf16[36,8,128]{2,1,0:T(8,128)(2,1)S(1)}, u32[]{:S(2)}, u32[]{:S(2)}) collective-permute-start(bf16[36,8,128]{2,1,0:T(8,128)(2,1)} %get-tuple-element.41), channel_id=1, source_target_pairs={{0,1},{1,0},{2,3},{3,2},{4,5},{5,4},{6,7},{7,6},{8,9},{9,8},{10,11... | collective-permute-start | bytes 221192 | tf_op jit(solution)/shard_map/ppermute | solution.py:23
  69.4 17.7 %collective-permute-start.20 = (bf16[36,8,128]{2,1,0:T(8,128)(2,1)}, bf16[36,8,128]{2,1,0:T(8,128)(2,1)S(1)}, u32[]{:S(2)}, u32[]{:S(2)}) collective-permute-start(bf16[36,8,128]{2,1,0:T(8,128)(2,1)} %get-tuple-element.42), channel_id=1, source_target_pairs={{1,2},{2,1},{3,4},{4,3},{5,6},{6,5},{9,10},{10,9},{11,12},{12,11},... | collective-permute-start | bytes 221192 | tf_op jit(solution)/shard_map/ppermute | solution.py:23
  70.0 18.4 %collective-permute-start.9 = (bf16[8,64,128]{2,1,0:T(8,128)(2,1)}, bf16[8,64,128]{2,1,0:T(8,128)(2,1)S(1)}, u32[]{:S(2)}, u32[]{:S(2)}) collective-permute-start(bf16[8,64,128]{2,1,0:T(8,128)(2,1)} %get-tuple-element.31), channel_id=1, source_target_pairs={{0,17},{1,16},{8,25},{9,24},{16,1},{17,0},{24,9},{25,8},{2,19},{3,... | collective-permute-start | bytes 393224 | tf_op jit(solution)/shard_map/ppermute | solution.py:547
  82.8 0.9 copy-start.2
  82.8 6.4 %collective-permute-start.10 = (bf16[8,64,128]{2,1,0:T(8,128)(2,1)S(1)}, bf16[8,64,128]{2,1,0:T(8,128)(2,1)S(1)}, u32[]{:S(2)}, u32[]{:S(2)}) collective-permute-start(bf16[8,64,128]{2,1,0:T(8,128)(2,1)S(1)} %copy-done.22), channel_id=1, source_target_pairs={{0,25},{1,24},{8,17},{9,16},{16,9},{17,8},{24,1},{25,0},{2,27},{3,... | collective-permute-start | bytes 393224 | tf_op jit(solution)/shard_map/ppermute | solution.py:547
  86.0 4.1 %copy-start.20 = (bf16[36,8,128]{2,1,0:T(8,128)(2,1)}, bf16[36,8,128]{2,1,0:T(8,128)(2,1)S(1)}, u32[]{:S(2)}) copy-start(bf16[36,8,128]{2,1,0:T(8,128)(2,1)S(1)} %collective-permute-done.19.col_pair_ref) | copy-start | bytes 221188
  86.0 6.4 %collective-permute-start.12 = (bf16[8,64,128]{2,1,0:T(8,128)(2,1)}, bf16[8,64,128]{2,1,0:T(8,128)(2,1)S(1)}, u32[]{:S(2)}, u32[]{:S(2)}) collective-permute-start(bf16[8,64,128]{2,1,0:T(8,128)(2,1)} %get-tuple-element.34), channel_id=1, source_target_pairs={{0,1},{1,0},{8,9},{9,8},{16,17},{17,16},{24,25},{25,24},{2,3},{3,2... | collective-permute-start | bytes 393224 | tf_op jit(solution)/shard_map/ppermute | solution.py:547
  87.1 3.0 %copy-start.21 = (bf16[36,8,128]{2,1,0:T(8,128)(2,1)}, bf16[36,8,128]{2,1,0:T(8,128)(2,1)S(1)}, u32[]{:S(2)}) copy-start(bf16[36,8,128]{2,1,0:T(8,128)(2,1)S(1)} %collective-permute-done.20.col_other_ref) | copy-start | bytes 221188
  87.1 5.3 %collective-permute-start.13 = (bf16[8,64,128]{2,1,0:T(8,128)(2,1)}, bf16[8,64,128]{2,1,0:T(8,128)(2,1)S(1)}, u32[]{:S(2)}, u32[]{:S(2)}) collective-permute-start(bf16[8,64,128]{2,1,0:T(8,128)(2,1)} %get-tuple-element.35), channel_id=1, source_target_pairs={{0,8},{1,9},{8,0},{9,1},{16,24},{17,25},{24,16},{25,17},{2,10},{3,... | collective-permute-start | bytes 393224 | tf_op jit(solution)/shard_map/ppermute | solution.py:547
  88.4 14.9 %copy-start.10 = (bf16[8,64,128]{2,1,0:T(8,128)(2,1)}, bf16[8,64,128]{2,1,0:T(8,128)(2,1)S(1)}, u32[]{:S(2)}) copy-start(bf16[8,64,128]{2,1,0:T(8,128)(2,1)S(1)} %collective-permute-done.9.refs_4_) | copy-start | bytes 393220
  88.4 11.8 %collective-permute-start.14 = (bf16[8,64,128]{2,1,0:T(8,128)(2,1)}, bf16[8,64,128]{2,1,0:T(8,128)(2,1)S(1)}, u32[]{:S(2)}, u32[]{:S(2)}) collective-permute-start(bf16[8,64,128]{2,1,0:T(8,128)(2,1)} %get-tuple-element.36), channel_id=1, source_target_pairs={{0,9},{1,8},{8,1},{9,0},{16,25},{17,24},{24,17},{25,16},{2,11},{3,... | collective-permute-start | bytes 393224 | tf_op jit(solution)/shard_map/ppermute | solution.py:547
  89.2 14.1 %copy-start.11 = (bf16[8,64,128]{2,1,0:T(8,128)(2,1)}, bf16[8,64,128]{2,1,0:T(8,128)(2,1)S(1)}, u32[]{:S(2)}) copy-start(bf16[8,64,128]{2,1,0:T(8,128)(2,1)S(1)} %collective-permute-done.10.refs_5_) | copy-start | bytes 393220
  89.2 11.0 %collective-permute-start.15 = (bf16[8,64,128]{2,1,0:T(8,128)(2,1)}, bf16[8,64,128]{2,1,0:T(8,128)(2,1)S(1)}, u32[]{:S(2)}, u32[]{:S(2)}) collective-permute-start(bf16[8,64,128]{2,1,0:T(8,128)(2,1)} %get-tuple-element.37), channel_id=1, source_target_pairs={{0,16},{1,17},{8,24},{9,25},{16,0},{17,1},{24,8},{25,9},{2,18},{3,... | collective-permute-start | bytes 393224 | tf_op jit(solution)/shard_map/ppermute | solution.py:547
  90.1 13.2 %copy-start.9 = (bf16[24,64,128]{2,1,0:T(8,128)(2,1)}, bf16[24,64,128]{2,1,0:T(8,128)(2,1)S(1)}, u32[]{:S(2)}) copy-start(bf16[24,64,128]{2,1,0:T(8,128)(2,1)S(1)} %collective-permute-done.8.refs_3_) | copy-start | bytes 1179652
  90.1 10.2 %collective-permute-start.16 = (bf16[8,64,128]{2,1,0:T(8,128)(2,1)}, bf16[8,64,128]{2,1,0:T(8,128)(2,1)S(1)}, u32[]{:S(2)}, u32[]{:S(2)}) collective-permute-start(bf16[8,64,128]{2,1,0:T(8,128)(2,1)} %get-tuple-element.38), channel_id=1, source_target_pairs={{0,17},{1,16},{8,25},{9,24},{16,1},{17,0},{24,9},{25,8},{2,19},{3,... | collective-permute-start | bytes 393224 | tf_op jit(solution)/shard_map/ppermute | solution.py:547
  92.4 10.9 %copy-start.12 = (bf16[8,64,128]{2,1,0:T(8,128)(2,1)}, bf16[8,64,128]{2,1,0:T(8,128)(2,1)S(1)}, u32[]{:S(2)}) copy-start(bf16[8,64,128]{2,1,0:T(8,128)(2,1)S(1)} %collective-permute-done.12.refs_10_) | copy-start | bytes 393220
  92.4 10.9 %collective-permute-start.17 = (bf16[8,64,128]{2,1,0:T(8,128)(2,1)}, bf16[8,64,128]{2,1,0:T(8,128)(2,1)S(1)}, u32[]{:S(2)}, u32[]{:S(2)}) collective-permute-start(bf16[8,64,128]{2,1,0:T(8,128)(2,1)} %get-tuple-element.39), channel_id=1, source_target_pairs={{0,24},{1,25},{8,16},{9,17},{16,8},{17,9},{24,0},{25,1},{2,26},{3,... | collective-permute-start | bytes 393224 | tf_op jit(solution)/shard_map/ppermute | solution.py:547
  92.4 10.9 %copy-start.13 = (bf16[8,64,128]{2,1,0:T(8,128)(2,1)}, bf16[8,64,128]{2,1,0:T(8,128)(2,1)S(1)}, u32[]{:S(2)}) copy-start(bf16[8,64,128]{2,1,0:T(8,128)(2,1)S(1)} %collective-permute-done.13.refs_11_) | copy-start | bytes 393220
  92.4 10.9 %collective-permute-start.18 = (bf16[8,64,128]{2,1,0:T(8,128)(2,1)}, bf16[8,64,128]{2,1,0:T(8,128)(2,1)}, u32[]{:S(2)}, u32[]{:S(2)}) collective-permute-start(bf16[8,64,128]{2,1,0:T(8,128)(2,1)} %get-tuple-element.40), channel_id=1, source_target_pairs={{0,25},{1,24},{8,17},{9,16},{16,9},{17,8},{24,1},{25,0},{2,27},{3,... | collective-permute-start | bytes 393224 | tf_op jit(solution)/shard_map/ppermute | solution.py:547
  100.2 3.1 %copy-start.14 = (bf16[8,64,128]{2,1,0:T(8,128)(2,1)}, bf16[8,64,128]{2,1,0:T(8,128)(2,1)S(1)}, u32[]{:S(2)}) copy-start(bf16[8,64,128]{2,1,0:T(8,128)(2,1)S(1)} %collective-permute-done.14.refs_12_) | copy-start | bytes 393220
  100.2 3.1 %copy-start.15 = (bf16[8,64,128]{2,1,0:T(8,128)(2,1)}, bf16[8,64,128]{2,1,0:T(8,128)(2,1)S(1)}, u32[]{:S(2)}) copy-start(bf16[8,64,128]{2,1,0:T(8,128)(2,1)S(1)} %collective-permute-done.15.refs_13_) | copy-start | bytes 393220
  100.3 3.1 %copy-start.16 = (bf16[8,64,128]{2,1,0:T(8,128)(2,1)}, bf16[8,64,128]{2,1,0:T(8,128)(2,1)S(1)}, u32[]{:S(2)}) copy-start(bf16[8,64,128]{2,1,0:T(8,128)(2,1)S(1)} %collective-permute-done.16.refs_14_) | copy-start | bytes 393220
  103.2 0.6 copy-start.17
  110.4 1.0 copy-start.8

commit v4 on v3

--- a/solution.py
+++ b/solution.py
@@ -106,84 +106,6 @@
     )(image, gain.reshape(1, channels))
 
 
-def context_kernel(
-    side,
-    margin,
-    evens_of,
-    image_ref,
-    row_pair_ref,
-    row_other_ref,
-    col_pair_ref,
-    col_other_ref,
-    gain_ref,
-    weight_ref,
-    lce_ref,
-    context_ref,
-    query_ref,
-    padded,
-):
-    step = pl.program_id(0)
-    height, width, channels = image_ref.shape
-    border = col_pair_ref.shape[1]
-
-    @pl.when(step == 0)
-    def _():
-        row_even, col_even = evens_of()
-        inner = pl.ds(border, width)
-        paired, other = row_pair_ref[...].astype(F32), row_other_ref[...].astype(F32)
-        padded[:margin, inner] = either(row_even, other, paired)
-        padded[pl.ds(margin, height), inner] = image_ref[...].astype(F32)
-        padded[pl.ds(margin + height, margin), inner] = either(row_even, paired, other)
-        paired, other = col_pair_ref[...].astype(F32), col_other_ref[...].astype(F32)
-        padded[:, :border] = either(col_even, other, paired)
-        padded[:, pl.ds(border + width, border)] = either(col_even, paired, other)
-
-    rows = side + 2 * margin
-    strip = padded[pl.ds(step * side, rows)]
-    wide = strip.shape[1]
-    normed = normalize(strip, gain_ref[...]).astype(BF16).reshape(rows * wide, channels)
-    weight = jnp.concatenate([weight_ref[:, :channels], weight_ref[:, 2 * channels :]], axis=1)
-    projected = jnp.dot(normed, weight, preferred_element_type=F32).astype(BF16)
-    values = projected[:, channels:].astype(F32).reshape(rows, wide, channels)
-    summed = jnp.zeros((side, width, channels), F32)
-    for col in range(2 * margin + 1):
-        moved = pltpu.roll(values, wide - (border - margin + col), 1)[:, :width]
-        for row in range(2 * margin + 1):
-            summed = summed + moved[row : row + side] * lce_ref[row, pl.ds(col, 1), :]
-    context_ref[...] = regions_of(summed, side)
-    queries = projected[:, :channels].astype(F32).reshape(rows, wide, channels)
-    inner = queries[margin : margin + side, border : border + width]
-    query_ref[...] = regions_of(inner, side).astype(BF16)
-
-
-def context_and_queries(image, around, gain, qkv_weight, lce_weight, side, margin, evens_of):
-    height, width, channels = image.shape
-    border = around[-1].shape[1]
-    tokens = height * width
-    full = lambda a: pl.BlockSpec(a.shape, lambda i: (0,) * a.ndim)
-    operands = (image, *around, gain.reshape(1, channels), qkv_weight, lce_weight)
-    return pl.pallas_call(
-        functools.partial(context_kernel, side, margin, evens_of),
-        grid=(height // side,),
-        in_specs=[full(a) for a in operands],
-        out_specs=[
-            pl.BlockSpec((side * width, channels), lambda i: (i, 0)),
-            pl.BlockSpec((side * width, channels), lambda i: (i, 0)),
-        ],
-        out_shape=[
-            jax.ShapeDtypeStruct((tokens, channels), F32),
-            jax.ShapeDtypeStruct((tokens, channels), BF16),
-        ],
-        scratch_shapes=[
-            pltpu.VMEM((height + 2 * margin, width + 2 * border, channels), F32),
-        ],
-        cost_estimate=pl.CostEstimate(
-            flops=tokens * channels * 600, bytes_accessed=10 * tokens * channels, transcendentals=0
-        ),
-        name="context",
-    )(*operands)
-
-
 def is_inside(layer):
     return (layer == 1) | (layer == 2)
 
@@ -260,8 +182,8 @@
     )(wanted, *flat, *frame)
 
 
-def load_all(options, sources, landed, sems, layer):
-    waits, start, at = [], 0, 0
+def load_all(options, sources, landed, sems, layer, wait):
+    start, at = 0, 0
     inside = is_inside(layer)
     for i, count in enumerate(options):
         size = sources[at].shape[0]
@@ -269,60 +191,136 @@
             pltpu.make_async_copy(source, landed.at[pl.ds(start, size)], sems.at[i])
             for source in sources[at : at + count]
         ]
-        if count == 1:
+        if wait:
+            copies[0].wait()
+        elif count == 1:
             copies[0].start()
         else:
             pl.when(inside)(copies[0].start)
             pl.when(~inside)(copies[1].start)
-        waits.append(copies[0])
         start += size
         at += count
-    for copy in waits:
-        copy.wait()
 
 
 def rows_of(sources):
     return sum(options[0].shape[0] for options in sources)
 
 
-def collect_kernel(options, place_of, position_ref, *refs):
-    sources, out_ref, landed, sems = refs[: sum(options)], refs[-3], refs[-2], refs[-1]
+def context_kernel(
+    side,
+    margin,
+    evens_of,
+    place_of,
+    options,
+    position_ref,
+    image_ref,
+    row_pair_ref,
+    row_other_ref,
+    col_pair_ref,
+    col_other_ref,
+    gain_ref,
+    weight_ref,
+    lce_ref,
+    *refs,
+):
+    sources = refs[: sum(options)]
+    context_ref, query_ref, fetched_ref, padded, landed, sems = refs[sum(options) :]
     step = pl.program_id(0)
+    height, width, channels = image_ref.shape
+    strips = height // side
+    border = col_pair_ref.shape[1]
 
     @pl.when(step == 0)
     def _():
-        load_all(options, sources, landed, sems, place_of()[1])
-
-    total = landed.shape[0]
-    per_step = out_ref.shape[0]
-    for i in range(per_step):
-        at = position_ref[step * per_step + i]
-        out_ref[i] = landed[jnp.where(at < total, at, 0)]
-
-
-def collect(position, sources, place_of, steps):
-    shape = sources[0][0].shape[1:]
-    total = rows_of(sources)
+        load_all(options, sources, landed, sems, place_of()[1], False)
+        row_even, col_even = evens_of()
+        inner = pl.ds(border, width)
+        paired, other = row_pair_ref[...].astype(F32), row_other_ref[...].astype(F32)
+        padded[:margin, inner] = either(row_even, other, paired)
+        padded[pl.ds(margin, height), inner] = image_ref[...].astype(F32)
+        padded[pl.ds(margin + height, margin), inner] = either(row_even, paired, other)
+        paired, other = col_pair_ref[...].astype(F32), col_other_ref[...].astype(F32)
+        padded[:, :border] = either(col_even, other, paired)
+        padded[:, pl.ds(border + width, border)] = either(col_even, paired, other)
+
+    @pl.when(step < strips)
+    def _():
+        rows = side + 2 * margin
+        strip = padded[pl.ds(jnp.minimum(step, strips - 1) * side, rows)]
+        wide = strip.shape[1]
+        normed = normalize(strip, gain_ref[...]).astype(BF16).reshape(rows * wide, channels)
+        weight = jnp.concatenate([weight_ref[:, :channels], weight_ref[:, 2 * channels :]], axis=1)
+        projected = jnp.dot(normed, weight, preferred_element_type=F32).astype(BF16)
+        values = projected[:, channels:].astype(F32).reshape(rows, wide, channels)
+        summed = jnp.zeros((side, width, channels), F32)
+        for col in range(2 * margin + 1):
+            moved = pltpu.roll(values, wide - (border - margin + col), 1)[:, :width]
+            for row in range(2 * margin + 1):
+                summed = summed + moved[row : row + side] * lce_ref[row, pl.ds(col, 1), :]
+        context_ref[...] = regions_of(summed, side)
+        queries = projected[:, :channels].astype(F32).reshape(rows, wide, channels)
+        inner = queries[margin : margin + side, border : border + width]
+        query_ref[...] = regions_of(inner, side).astype(BF16)
+
+    @pl.when(step == strips)
+    def _():
+        load_all(options, sources, landed, sems, place_of()[1], True)
+
+    @pl.when(step >= strips)
+    def _():
+        total = landed.shape[0]
+        per_step = fetched_ref.shape[0]
+        for i in range(per_step):
+            at = position_ref[jnp.maximum(step - strips, 0) * per_step + i]
+            fetched_ref[i] = landed[jnp.where(at < total, at, 0)]
+
+
+def context_and_regions(
+    position, sources, image, around, gain, qkv_weight, lce_weight, side, margin, evens_of, place_of
+):
+    height, width, channels = image.shape
+    border = around[-1].shape[1]
+    tokens = height * width
+    strips = height // side
     pairs = position.shape[0]
+    rounds = math.gcd(pairs, 4)
+    tile = sources[0][0].shape[1:]
+    full = lambda a: pl.BlockSpec(a.shape, lambda i, _: (0,) * a.ndim)
+    operands = (image, *around, gain.reshape(1, channels), qkv_weight, lce_weight)
     flat = sum(sources, [])
+    strip = pl.BlockSpec((side * width, channels), lambda i, _: (jnp.minimum(i, strips - 1), 0))
     return pl.pallas_call(
-        functools.partial(collect_kernel, tuple(map(len, sources)), place_of),
+        functools.partial(
+            context_kernel, side, margin, evens_of, place_of, tuple(map(len, sources))
+        ),
         grid_spec=pltpu.PrefetchScalarGridSpec(
             num_scalar_prefetch=1,
-            grid=(steps,),
-            in_specs=[pl.BlockSpec(memory_space=pl.ANY)] * len(flat),
-            out_specs=pl.BlockSpec((pairs // steps, *shape), lambda i, _: (i, 0, 0)),
+            grid=(strips + rounds,),
+            in_specs=[full(a) for a in operands]
+            + [pl.BlockSpec(memory_space=pl.ANY)] * len(flat),
+            out_specs=[
+                strip,
+                strip,
+                pl.BlockSpec(
+                    (pairs // rounds, *tile), lambda i, _: (jnp.maximum(i - strips, 0), 0, 0)
+                ),
+            ],
             scratch_shapes=[
-                pltpu.VMEM((total, *shape), BF16),
+                pltpu.VMEM((height + 2 * margin, width + 2 * border, channels), F32),
+                pltpu.VMEM((rows_of(sources), *tile), BF16),
                 pltpu.SemaphoreType.DMA((len(sources),)),
             ],
         ),
-        out_shape=jax.ShapeDtypeStruct((pairs, *shape), BF16),
+        out_shape=[
+            jax.ShapeDtypeStruct((tokens, channels), F32),
+            jax.ShapeDtypeStruct((tokens, channels), BF16),
+            jax.ShapeDtypeStruct((pairs, *tile), BF16),
+        ],
         cost_estimate=pl.CostEstimate(
-            flops=0, bytes_accessed=2 * (total + pairs) * math.prod(shape), transcendentals=0
-        ),
-        name="collect",
-    )(position, *flat)
+            flops=tokens * channels * 600, bytes_accessed=40 * tokens * channels, transcendentals=0
+        ),
+        name="context",
+    )(position, *operands, *flat)
 
 
 def project(fetched, weight_ref):
@@ -365,8 +363,12 @@
     picks,
     batch,
     early,
+    late_count,
     position_ref,
-    late_ref,
+    *refs,
+):
+    late_refs = refs[:late_count]
+    (
     fetched_ref,
     query_ref,
     context_ref,
@@ -377,10 +379,18 @@
     up_ref,
     down_ref,
     result_ref,
+    late_ref,
     combined_ref,
-):
+    ) = refs[late_count:]
     step = pl.program_id(0)
     last = pl.num_programs(0) - 2
+
+    @pl.when(step == 0)
+    def _():
+        start = 0
+        for part in late_refs:
+            late_ref[pl.ds(start, part.shape[0])] = part[...]
+            start += part.shape[0]
 
     area, channels = fetched_ref.shape[1:]
     exponent = (channels // HEADS) ** (-0.5) * math.log2(math.e)
@@ -457,21 +467,25 @@
     )
     regions = pl.BlockSpec((batch * picks, area, channels), lambda i, position: (now(i), 0, 0))
     return pl.pallas_call(
-        functools.partial(tail_kernel, side, picks, batch, early),
+        functools.partial(tail_kernel, side, picks, batch, early, len(late)),
         grid_spec=pltpu.PrefetchScalarGridSpec(
             num_scalar_prefetch=1,
             grid=(steps + 1,),
-            in_specs=[pl.BlockSpec(memory_space=pltpu.VMEM), regions, tokens, tokens, strip]
+            in_specs=[pl.BlockSpec(memory_space=pltpu.VMEM)] * len(late)
+            + [regions, tokens, tokens, strip]
             + [full(w) for w in weights],
             out_specs=strip,
-            scratch_shapes=[pltpu.VMEM((batch * area, channels), BF16)],
+            scratch_shapes=[
+                pltpu.VMEM((sum(part.shape[0] for part in late), area, channels), BF16),
+                pltpu.VMEM((batch * area, channels), BF16),
+            ],
         ),
         out_shape=jax.ShapeDtypeStruct(image.shape, BF16),
         cost_estimate=pl.CostEstimate(
             flops=image.size * 4000, bytes_accessed=16 * image.size, transcendentals=40 * image.size
         ),
         name="tail",
-    )(position, late, fetched, queries, context, image, *weights)
+    )(position, *late, fetched, queries, context, image, *weights)
 
 
 def layer_blocks(block, layers):
@@ -605,27 +619,29 @@
 
     for chunk in range(2, layers):
         last = chunk == layers - 1
-        jobs = [(0 if last else far - 1, None if last else 0, 0, far, chunk) for far in range(1, peers)]
-        shapes = [(peers, capacity, *tile)] if last else [(capacity, *tile)] * (peers - 1)
+        jobs = [(far - 1, 0, 0, far, chunk) for far in range(1, peers)]
+        shapes = [(capacity, *tile)] * (peers - 1)
         parts = pack(jobs, shapes, [held[chunk]], place_of, wanted, capacity, layers)
-        if last:
-            got = lax.all_to_all(parts[0], ("rows", "x"), 0, 0, tiled=True)
-        else:
-            got = [swap(part, far) for far, part in enumerate(parts, 1)]
+        got = [swap(part, far) for far, part in enumerate(parts, 1)]
         landing(held[chunk], ((step == chunk) & (distance == 0), local_index))
         if last:
             early = total
             arrived.append([])
-            elsewhere = (step == chunk) & (distance != 0)
-            landing([got.reshape(-1, *tile)], (elsewhere, owner_peer * capacity + slot))
-        else:
-            for far, part in enumerate(got, 1):
-                landing([part], ((step == chunk) & (distance == far), slot))
-    ((late,),) = arrived.pop()
-    fetched = collect(position, sum(arrived, []), place_of, math.gcd(pair_count, 8))
-
-    context, queries = context_and_queries(
-        image, around, norm_gain, qkv_weight, lce_weight, side, margin, evens_of
+        for far, part in enumerate(got, 1):
+            landing([part], ((step == chunk) & (distance == far), slot))
+    late = sum(arrived.pop(), [])
+    context, queries, fetched = context_and_regions(
+        position,
+        sum(arrived, []),
+        image,
+        around,
+        norm_gain,
+        qkv_weight,
+        lce_weight,
+        side,
+        margin,
+        evens_of,
+        place_of,
     )
     weights = (
         qkv_weight,

time: 124 us -> 116 us (0.935)
  the two profiles are of different devices: /device:TPU:0 before, /device:TPU:17 now
where the time goes in v4:
time: 116 us; the launch traced here: 115 us
  starting transfers between devices  44 us (38%)
  Pallas kernels  32.2 us (28%)
  waiting for transfers between devices  25.3 us (22%)
  blocking collectives  7.98 us (7%)
  local copies, waits for them, and re-layouts  4.57 us (4%)
    ppermute x19, starting transfers between devices, swap(): lax.ppermute(part, ('rows', 'x'), [(i, i ^ far) for i in range(peers)])  20.9 us
    ppermute x4, waiting for transfers between devices, with_pairs(): lax.ppermute(part, axis, pairs)  13.1 us
    pallas_call x1, Pallas kernels, tail(): pl.pallas_call(functools.partial(tail_kernel, side, picks, batch, early,...  12.6 us
    ppermute x4, starting transfers between devices, with_pairs(): lax.ppermute(part, axis, pairs)  10.6 us
    pallas_call x1, Pallas kernels, context_and_regions(): pl.pallas_call(functools.partial(context_kernel, side, margin, evens_of,...  8.4 us
    ppermute x5, starting transfers between devices, hop(): return lax.ppermute(block, 'z', pairs)  8.23 us
    all_to_all x1, blocking collectives, block(): lax.all_to_all(requests.reshape(peers, 1, lanes), ('rows', 'x'), 0, 0, ti...  7.98 us
    pallas_call x3, Pallas kernels, pack(): pl.pallas_call(functools.partial(pack_kernel, tuple(jobs), tuple(map(len,...  7.6 us
  transfers between devices with their start and end apart: 29, of which 4 were waited for; matrix products, arithmetic and copies ran while one was open for 2% of the time, Pallas kernels for 14%

profile of v4, /device:TPU:17, one launch (start us, length us, event | category | flops | bytes accessed | tf_op | source)
XLA Modules:
  0.0 115.5 jit_solution(16871560135407016393)
XLA Ops:
  0.0 3.7 %norm_regions.1 = (bf16[32,64,128]{2,1,0:T(8,128)(2,1)}, bf16[2,64,128]{2,1,0:T(8,128)(2,1)}, bf16[2,64,128]{2,1,0:T(8,128)(2,1)}, bf16[32,8,128]{2,1,0:T(8,128)(2,1)}, bf16[32,8,128]{2,1,0:T(8,128)(2,1)}) custom-call(bf16[32,64,128]{2,1,0:T(8,128)(2,1)} %refs_10_.1, f32[1,128]{1,0:T(1,128)} %bitcast.6), custom_call_target="tpu_custom_call" | custom-call | flops 2621440 | bytes 1048576 | tf_op jit(solution)/shard_map/norm_regions/pallas_call | solution.py:81
  3.7 1.4 %collective-permute-start.1 = (bf16[32,64,128]{2,1,0:T(8,128)(2,1)}, bf16[32,64,128]{2,1,0:T(8,128)(2,1)S(1)}, u32[]{:S(2)}, u32[]{:S(2)}) collective-permute-start(bf16[32,64,128]{2,1,0:T(8,128)(2,1)} %get-tuple-element.33.refs_0_), channel_id=1, source_target_pairs={{0,2},{2,0},{4,6},{6,4},{1,3},{3,1},{5,7},{7,5},{8,10},{10,8},{12,... | collective-permute-start | bytes 1572872 | tf_op jit(solution)/shard_map/ppermute | solution.py:499
  5.0 1.2 %collective-permute-start.13 = (bf16[32,64,128]{2,1,0:T(8,128)(2,1)}, bf16[32,64,128]{2,1,0:T(8,128)(2,1)S(1)}, u32[]{:S(2)}, u32[]{:S(2)}) collective-permute-start(bf16[32,64,128]{2,1,0:T(8,128)(2,1)} %get-tuple-element.33.refs_0_), channel_id=1, source_target_pairs={{0,1},{1,0},{8,9},{9,8},{16,17},{17,16},{24,25},{25,24},{2,3},{3,2... | collective-permute-start | bytes 1572872 | tf_op jit(solution)/shard_map/ppermute | solution.py:561
  6.2 1.2 %collective-permute-start.14 = (bf16[32,64,128]{2,1,0:T(8,128)(2,1)}, bf16[32,64,128]{2,1,0:T(8,128)(2,1)S(1)}, u32[]{:S(2)}, u32[]{:S(2)}) collective-permute-start(bf16[32,64,128]{2,1,0:T(8,128)(2,1)} %get-tuple-element.33.refs_0_), channel_id=1, source_target_pairs={{0,16},{1,17},{8,24},{9,25},{16,0},{17,1},{24,8},{25,9},{2,18},{3,... | collective-permute-start | bytes 1572872 | tf_op jit(solution)/shard_map/ppermute | solution.py:561
  7.5 1.9 %collective-permute-start = (bf16[32,64,128]{2,1,0:T(8,128)(2,1)}, bf16[32,64,128]{2,1,0:T(8,128)(2,1)S(1)}, u32[]{:S(2)}, u32[]{:S(2)}) collective-permute-start(bf16[32,64,128]{2,1,0:T(8,128)(2,1)} %get-tuple-element.33.refs_0_), channel_id=1, source_target_pairs={{2,4},{4,2},{3,5},{5,3},{10,12},{12,10},{11,13},{13,11},{18,20},{2... | collective-permute-start | bytes 1572872 | tf_op jit(solution)/shard_map/ppermute | solution.py:499
  9.4 1.6 %collective-permute-start.11 = (bf16[2,64,128]{2,1,0:T(8,128)(2,1)}, bf16[2,64,128]{2,1,0:T(8,128)(2,1)S(1)}, u32[]{:S(2)}, u32[]{:S(2)}) collective-permute-start(bf16[2,64,128]{2,1,0:T(8,128)(2,1)} %get-tuple-element.41), channel_id=1, source_target_pairs={{0,8},{8,0},{16,24},{24,16},{1,9},{9,1},{17,25},{25,17},{2,10},{10... | collective-permute-start | bytes 98312 | tf_op jit(solution)/shard_map/ppermute | solution.py:23
  11.0 0.8 copy.12
  11.9 4.9 %collective-permute-done.1.refs_3_.refs_6_ = bf16[32,64,128]{2,1,0:T(8,128)(2,1)S(1)} collective-permute-done((bf16[32,64,128]{2,1,0:T(8,128)(2,1)}, bf16[32,64,128]{2,1,0:T(8,128)(2,1)S(1)}, u32[]{:S(2)}, u32[]{:S(2)}) %collective-permute-start.1) | collective-permute-done | bytes 524320 | tf_op jit(solution)/shard_map/ppermute | solution.py:499
  16.7 2.1 %collective-permute-start.2 = (bf16[32,64,128]{2,1,0:T(8,128)(2,1)S(1)}, bf16[32,64,128]{2,1,0:T(8,128)(2,1)S(1)}, u32[]{:S(2)}, u32[]{:S(2)}) collective-permute-start(bf16[32,64,128]{2,1,0:T(8,128)(2,1)S(1)} %collective-permute-done.1.refs_3_.refs_6_), channel_id=1, source_target_pairs={{2,4},{4,2},{3,5},{5,3},{10,12},{12,10},{11,13},{13,11},{18,20},{2... | collective-permute-start | bytes 1572872 | tf_op jit(solution)/shard_map/ppermute | solution.py:499
  19.0 0.6 and_select_fusion.25
  19.7 4.8 %collective-permute-start.12 = (bf16[2,64,128]{2,1,0:T(8,128)(2,1)}, bf16[2,64,128]{2,1,0:T(8,128)(2,1)S(1)}, u32[]{:S(2)}, u32[]{:S(2)}) collective-permute-start(bf16[2,64,128]{2,1,0:T(8,128)(2,1)} %get-tuple-element.42), channel_id=1, source_target_pairs={{8,16},{16,8},{9,17},{17,9},{10,18},{18,10},{11,19},{19,11},{12,20... | collective-permute-start | bytes 98312 | tf_op jit(solution)/shard_map/ppermute | solution.py:23
  24.5 1.6 %collective-permute-start.20 = (bf16[32,64,128]{2,1,0:T(8,128)(2,1)S(1)}, bf16[32,64,128]{2,1,0:T(8,128)(2,1)S(1)}, u32[]{:S(2)}, u32[]{:S(2)}) collective-permute-start(bf16[32,64,128]{2,1,0:T(8,128)(2,1)S(1)} %collective-permute-done.refs_0_.refs_17_), channel_id=1, source_target_pairs={{2,0},{4,6},{3,1},{5,7},{10,8},{12,14},{11,9},{13,15},{18,16},{20,... | collective-permute-start | bytes 1572872 | tf_op jit(solution)/shard_map/ppermute | solution.py:499
  26.1 0.2 select_reduce_fusion
  26.3 8.0 %all_to_all.10.wanted_ref = s32[8,1,128]{2,1,0:T(1,128)} all-to-all(s32[8,1,128]{2,1,0:T(1,128)S(1)} %bitcast.5), channel_id=1, replica_groups=mesh['rows'=4,'z'=4,'x'=2] {'rows','x'}, dimensions={0} | all-to-all | bytes 8192 | tf_op jit(solution)/shard_map/all_to_all | solution.py:553
  34.4 0.5 copy-done.17
  34.9 0.2 copy-done.6
  35.3 3.0 %pack.4 = (bf16[24,64,128]{2,1,0:T(8,128)(2,1)}, bf16[8,64,128]{2,1,0:T(8,128)(2,1)}, bf16[8,64,128]{2,1,0:T(8,128)(2,1)}, bf16[8,8,64,128]{3,2,1,0:T(8,128)(2,1...) custom-call(s32[8,1,128]{2,1,0:T(1,128)} %all_to_all.10.wanted_ref, ...), custom_call_target="tpu_custom_call" | custom-call | bytes 3702784 | tf_op jit(solution)/shard_map/pack/pallas_call | solution.py:164
  38.3 4.3 %all-to-all-start.1 = ((bf16[8,8,64,128]{3,2,1,0:T(8,128)(2,1)}), bf16[8,8,64,128]{3,2,1,0:T(8,128)(2,1)S(1)}, u32[]{:S(2)}, u32[]{:S(2)}) async-start(bf16[8,8,64,128]{3,2,1,0:T(8,128)(2,1)} %get-tuple-element.50), calls=%async_computation.1 | async-start | bytes 2097152 | tf_op jit(solution)/shard_map/all_to_all | solution.py:599
  42.6 1.3 %collective-permute-start.3 = (bf16[32,64,128]{2,1,0:T(8,128)(2,1)S(1)}, bf16[32,64,128]{2,1,0:T(8,128)(2,1)S(1)}, u32[]{:S(2)}, u32[]{:S(2)}) collective-permute-start(bf16[32,64,128]{2,1,0:T(8,128)(2,1)S(1)} %collective-permute-done.2.refs_0_.refs_8_), channel_id=1, source_target_pairs={{2,0},{4,6},{3,1},{5,7},{10,8},{12,14},{11,9},{13,15},{18,16},{20,... | collective-permute-start | bytes 1572872 | tf_op jit(solution)/shard_map/ppermute | solution.py:499
  44.1 1.6 %collective-permute-start.15 = (bf16[36,8,128]{2,1,0:T(8,128)(2,1)}, bf16[36,8,128]{2,1,0:T(8,128)(2,1)S(1)}, u32[]{:S(2)}, u32[]{:S(2)}) collective-permute-start(bf16[36,8,128]{2,1,0:T(8,128)(2,1)} %get-tuple-element.45), channel_id=1, source_target_pairs={{0,1},{1,0},{2,3},{3,2},{4,5},{5,4},{6,7},{7,6},{8,9},{9,8},{10,11... | collective-permute-start | bytes 221192 | tf_op jit(solution)/shard_map/ppermute | solution.py:23
  45.8 1.2 %collective-permute-start.18 = (bf16[8,64,128]{2,1,0:T(8,128)(2,1)}, bf16[8,64,128]{2,1,0:T(8,128)(2,1)}, u32[]{:S(2)}, u32[]{:S(2)}) collective-permute-start(bf16[8,64,128]{2,1,0:T(8,128)(2,1)} %get-tuple-element.48), channel_id=1, source_target_pairs={{0,17},{1,16},{8,25},{9,24},{16,1},{17,0},{24,9},{25,8},{2,19},{3,... | collective-permute-start | bytes 393224 | tf_op jit(solution)/shard_map/ppermute | solution.py:561
  47.0 10.8 %collective-permute-done.15.col_pair_ref = bf16[36,8,128]{2,1,0:T(8,128)(2,1)S(1)} collective-permute-done((bf16[36,8,128]{2,1,0:T(8,128)(2,1)}, bf16[36,8,128]{2,1,0:T(8,128)(2,1)S(1)}, u32[]{:S(2)}, u32[]{:S(2)}) %collective-permute-start.15) | collective-permute-done | bytes 73760 | tf_op jit(solution)/shard_map/ppermute | solution.py:23
  57.7 2.6 %collective-permute-start.19 = (bf16[8,64,128]{2,1,0:T(8,128)(2,1)}, bf16[8,64,128]{2,1,0:T(8,128)(2,1)}, u32[]{:S(2)}, u32[]{:S(2)}) collective-permute-start(bf16[8,64,128]{2,1,0:T(8,128)(2,1)} %get-tuple-element.49), channel_id=1, source_target_pairs={{0,25},{1,24},{8,17},{9,16},{16,9},{17,8},{24,1},{25,0},{2,27},{3,... | collective-permute-start | bytes 393224 | tf_op jit(solution)/shard_map/ppermute | solution.py:561
  60.4 2.5 %collective-permute-start.16 = (bf16[36,8,128]{2,1,0:T(8,128)(2,1)}, bf16[36,8,128]{2,1,0:T(8,128)(2,1)S(1)}, u32[]{:S(2)}, u32[]{:S(2)}) collective-permute-start(bf16[36,8,128]{2,1,0:T(8,128)(2,1)} %get-tuple-element.46), channel_id=1, source_target_pairs={{1,2},{2,1},{3,4},{4,3},{5,6},{6,5},{9,10},{10,9},{11,12},{12,11},... | collective-permute-start | bytes 221192 | tf_op jit(solution)/shard_map/ppermute | solution.py:23
  62.9 2.3 %pack.5 = (bf16[8,64,128]{2,1,0:T(8,128)(2,1)}, bf16[8,64,128]{2,1,0:T(8,128)(2,1)}, bf16[8,64,128]{2,1,0:T(8,128)(2,1)}, bf16[8,64,128]{2,1,0:T(8,128)(2,1)}, b...) custom-call(s32[8,1,128]{2,1,0:T(1,128)} %all_to_all.10.wanted_ref, ...), custom_call_target="tpu_custom_call" | custom-call | bytes 1835008 | tf_op jit(solution)/shard_map/pack/pallas_call | solution.py:164
  65.2 2.4 %collective-permute-done.16.col_other_ref = bf16[36,8,128]{2,1,0:T(8,128)(2,1)S(1)} collective-permute-done((bf16[36,8,128]{2,1,0:T(8,128)(2,1)}, bf16[36,8,128]{2,1,0:T(8,128)(2,1)S(1)}, u32[]{:S(2)}, u32[]{:S(2)}) %collective-permute-start.16) | collective-permute-done | bytes 73760 | tf_op jit(solution)/shard_map/ppermute | solution.py:23
  67.6 0.6 copy-done.19
  68.2 0.4 collective-permute-start.21
  68.6 0.4 collective-permute-start.22
  69.0 1.3 %collective-permute-start.23 = (bf16[8,64,128]{2,1,0:T(8,128)(2,1)}, bf16[8,64,128]{2,1,0:T(8,128)(2,1)S(1)}, u32[]{:S(2)}, u32[]{:S(2)}) collective-permute-start(bf16[8,64,128]{2,1,0:T(8,128)(2,1)} %get-tuple-element.53), channel_id=1, source_target_pairs={{0,9},{1,8},{8,1},{9,0},{16,25},{17,24},{24,17},{25,16},{2,11},{3,... | collective-permute-start | bytes 393224 | tf_op jit(solution)/shard_map/ppermute | solution.py:561
  70.3 0.4 collective-permute-start.24
  70.8 0.4 copy-done.4
  71.2 2.3 %pack.3 = (bf16[8,64,128]{2,1,0:T(8,128)(2,1)}, bf16[8,64,128]{2,1,0:T(8,128)(2,1)}, bf16[8,64,128]{2,1,0:T(8,128)(2,1)}, bf16[8,64,128]{2,1,0:T(8,128)(2,1)}, b...) custom-call(s32[8,1,128]{2,1,0:T(1,128)} %all_to_all.10.wanted_ref, ...), custom_call_target="tpu_custom_call" | custom-call | bytes 1835008 | tf_op jit(solution)/shard_map/pack/pallas_call | solution.py:164
  73.5 1.3 %collective-permute-start.25 = (bf16[8,64,128]{2,1,0:T(8,128)(2,1)}, bf16[8,64,128]{2,1,0:T(8,128)(2,1)S(1)}, u32[]{:S(2)}, u32[]{:S(2)}) collective-permute-start(bf16[8,64,128]{2,1,0:T(8,128)(2,1)} %get-tuple-element.55), channel_id=1, source_target_pairs={{0,17},{1,16},{8,25},{9,24},{16,1},{17,0},{24,9},{25,8},{2,19},{3,... | collective-permute-start | bytes 393224 | tf_op jit(solution)/shard_map/ppermute | solution.py:561
  74.7 1.5 %collective-permute-start.26 = (bf16[8,64,128]{2,1,0:T(8,128)(2,1)}, bf16[8,64,128]{2,1,0:T(8,128)(2,1)S(1)}, u32[]{:S(2)}, u32[]{:S(2)}) collective-permute-start(bf16[8,64,128]{2,1,0:T(8,128)(2,1)} %get-tuple-element.56), channel_id=1, source_target_pairs={{0,24},{1,25},{8,16},{9,17},{16,8},{17,9},{24,0},{25,1},{2,26},{3,... | collective-permute-start | bytes 393224 | tf_op jit(solution)/shard_map/ppermute | solution.py:561
  76.3 0.6 collective-permute-start.27
  76.8 2.1 %collective-permute-start.10 = (bf16[8,64,128]{2,1,0:T(8,128)(2,1)}, bf16[8,64,128]{2,1,0:T(8,128)(2,1)S(1)}, u32[]{:S(2)}, u32[]{:S(2)}) collective-permute-start(bf16[8,64,128]{2,1,0:T(8,128)(2,1)} %get-tuple-element.40), channel_id=1, source_target_pairs={{0,25},{1,24},{8,17},{9,16},{16,9},{17,8},{24,1},{25,0},{2,27},{3,... | collective-permute-start | bytes 393224 | tf_op jit(solution)/shard_map/ppermute | solution.py:561
  78.9 0.5 collective-permute-start.4
  79.5 1.9 %collective-permute-start.5 = (bf16[8,64,128]{2,1,0:T(8,128)(2,1)}, bf16[8,64,128]{2,1,0:T(8,128)(2,1)S(1)}, u32[]{:S(2)}, u32[]{:S(2)}) collective-permute-start(bf16[8,64,128]{2,1,0:T(8,128)(2,1)} %get-tuple-element.35), channel_id=1, source_target_pairs={{0,8},{1,9},{8,0},{9,1},{16,24},{17,25},{24,16},{25,17},{2,10},{3,... | collective-permute-start | bytes 393224 | tf_op jit(solution)/shard_map/ppermute | solution.py:561
  81.3 7.2 %collective-permute-done.26.refs_15_ = bf16[8,64,128]{2,1,0:T(8,128)(2,1)S(1)} collective-permute-done((bf16[8,64,128]{2,1,0:T(8,128)(2,1)}, bf16[8,64,128]{2,1,0:T(8,128)(2,1)S(1)}, u32[]{:S(2)}, u32[]{:S(2)}) %collective-permute-start.26) | collective-permute-done | bytes 131104 | tf_op jit(solution)/shard_map/ppermute | solution.py:561
  88.6 0.9 collective-permute-start.6
  89.5 0.8 collective-permute-start.7
  90.4 1.2 %collective-permute-start.8 = (bf16[8,64,128]{2,1,0:T(8,128)(2,1)}, bf16[8,64,128]{2,1,0:T(8,128)(2,1)S(1)}, u32[]{:S(2)}, u32[]{:S(2)}) collective-permute-start(bf16[8,64,128]{2,1,0:T(8,128)(2,1)} %get-tuple-element.38), channel_id=1, source_target_pairs={{0,17},{1,16},{8,25},{9,24},{16,1},{17,0},{24,9},{25,8},{2,19},{3,... | collective-permute-start | bytes 393224 | tf_op jit(solution)/shard_map/ppermute | solution.py:561
  91.5 1.2 collective-permute-start.9
  92.8 0.9 copy-done
  93.7 8.4 %context.1 = (f32[2048,128]{1,0:T(8,128)}, bf16[2048,128]{1,0:T(8,128)(2,1)}, bf16[128,64,128]{2,1,0:T(8,128)(2,1)}) custom-call(s32[128]{0:T(128)} %get-tuple-element.61.position_ref, bf16[32,64,128]{2,1,0:T(8,128)(2,1)} %refs_10_.1, bf16[2,64,128]{2,1,0:T(8,128)(2,1)} %copy-done.16, bf16[2,64,128]{2,1,0:T(8,128)(2,1)} %copy-done.17, ...), custom_call_target="tpu_custom_call" | custom-call | flops 157286400 | bytes 10485760 | tf_op jit(solution)/shard_map/context/pallas_call | solution.py:292
  102.2 0.5 copy-done.22
  102.9 12.6 %tail.1 = bf16[32,64,128]{2,1,0:T(8,128)(2,1)} custom-call(s32[128]{0:T(128)} %get-tuple-element.61.position_ref, bf16[8,64,128]{2,1,0:T(8,128)(2,1)} %copy-done.21, bf16[8,64,128]{2,1,0:T(8,128)(2,1)} %copy-done.22, bf16[8,64,128]{2,1,0:T(8,128)(2,1)} %copy-done.23, bf16[8,64,128]{2,1,0:T(8,128)(2,1)} %copy-done.24, bf16[8,64,128]{2,1,0:T(8,128)(2,1)} %copy-done.25, ...), custom_call_target="tpu_custom_call" | custom-call | flops 1048576000 | bytes 4194304 | tf_op jit(solution)/shard_map/tail/pallas_call | solution.py:469
  (78 shorter events, 1.0 us)
Async XLA Ops:
  3.7 13.1 %collective-permute-start.1 = (bf16[32,64,128]{2,1,0:T(8,128)(2,1)}, bf16[32,64,128]{2,1,0:T(8,128)(2,1)S(1)}, u32[]{:S(2)}, u32[]{:S(2)}) collective-permute-start(bf16[32,64,128]{2,1,0:T(8,128)(2,1)} %get-tuple-element.33.refs_0_), channel_id=1, source_target_pairs={{0,2},{2,0},{4,6},{6,4},{1,3},{3,1},{5,7},{7,5},{8,10},{10,8},{12,... | collective-permute-start | bytes 1572872 | tf_op jit(solution)/shard_map/ppermute | solution.py:499
  5.0 29.3 %collective-permute-start.13 = (bf16[32,64,128]{2,1,0:T(8,128)(2,1)}, bf16[32,64,128]{2,1,0:T(8,128)(2,1)S(1)}, u32[]{:S(2)}, u32[]{:S(2)}) collective-permute-start(bf16[32,64,128]{2,1,0:T(8,128)(2,1)} %get-tuple-element.33.refs_0_), channel_id=1, source_target_pairs={{0,1},{1,0},{8,9},{9,8},{16,17},{17,16},{24,25},{25,24},{2,3},{3,2... | collective-permute-start | bytes 1572872 | tf_op jit(solution)/shard_map/ppermute | solution.py:561
  6.2 28.1 %collective-permute-start.14 = (bf16[32,64,128]{2,1,0:T(8,128)(2,1)}, bf16[32,64,128]{2,1,0:T(8,128)(2,1)S(1)}, u32[]{:S(2)}, u32[]{:S(2)}) collective-permute-start(bf16[32,64,128]{2,1,0:T(8,128)(2,1)} %get-tuple-element.33.refs_0_), channel_id=1, source_target_pairs={{0,16},{1,17},{8,24},{9,25},{16,0},{17,1},{24,8},{25,9},{2,18},{3,... | collective-permute-start | bytes 1572872 | tf_op jit(solution)/shard_map/ppermute | solution.py:561
  7.5 17.0 %collective-permute-start = (bf16[32,64,128]{2,1,0:T(8,128)(2,1)}, bf16[32,64,128]{2,1,0:T(8,128)(2,1)S(1)}, u32[]{:S(2)}, u32[]{:S(2)}) collective-permute-start(bf16[32,64,128]{2,1,0:T(8,128)(2,1)} %get-tuple-element.33.refs_0_), channel_id=1, source_target_pairs={{2,4},{4,2},{3,5},{5,3},{10,12},{12,10},{11,13},{13,11},{18,20},{2... | collective-permute-start | bytes 1572872 | tf_op jit(solution)/shard_map/ppermute | solution.py:499
  9.4 10.3 %collective-permute-start.11 = (bf16[2,64,128]{2,1,0:T(8,128)(2,1)}, bf16[2,64,128]{2,1,0:T(8,128)(2,1)S(1)}, u32[]{:S(2)}, u32[]{:S(2)}) collective-permute-start(bf16[2,64,128]{2,1,0:T(8,128)(2,1)} %get-tuple-element.41), channel_id=1, source_target_pairs={{0,8},{8,0},{16,24},{24,16},{1,9},{9,1},{17,25},{25,17},{2,10},{10... | collective-permute-start | bytes 98312 | tf_op jit(solution)/shard_map/ppermute | solution.py:23
  16.7 17.6 %copy-start.5 = (bf16[32,64,128]{2,1,0:T(8,128)(2,1)}, bf16[32,64,128]{2,1,0:T(8,128)(2,1)S(1)}, u32[]{:S(2)}) copy-start(bf16[32,64,128]{2,1,0:T(8,128)(2,1)S(1)} %collective-permute-done.1.refs_3_.refs_6_) | copy-start | bytes 1572868
  16.7 25.9 %collective-permute-start.2 = (bf16[32,64,128]{2,1,0:T(8,128)(2,1)S(1)}, bf16[32,64,128]{2,1,0:T(8,128)(2,1)S(1)}, u32[]{:S(2)}, u32[]{:S(2)}) collective-permute-start(bf16[32,64,128]{2,1,0:T(8,128)(2,1)S(1)} %collective-permute-done.1.refs_3_.refs_6_), channel_id=1, source_target_pairs={{2,4},{4,2},{3,5},{5,3},{10,12},{12,10},{11,13},{13,11},{18,20},{2... | collective-permute-start | bytes 1572872 | tf_op jit(solution)/shard_map/ppermute | solution.py:499
  19.7 14.7 %copy-start.16 = (bf16[2,64,128]{2,1,0:T(8,128)(2,1)}, bf16[2,64,128]{2,1,0:T(8,128)(2,1)S(1)}, u32[]{:S(2)}) copy-start(bf16[2,64,128]{2,1,0:T(8,128)(2,1)S(1)} %collective-permute-done.11.refs_4_.row_pair_ref) | copy-start | bytes 98308
  19.7 14.6 %collective-permute-start.12 = (bf16[2,64,128]{2,1,0:T(8,128)(2,1)}, bf16[2,64,128]{2,1,0:T(8,128)(2,1)S(1)}, u32[]{:S(2)}, u32[]{:S(2)}) collective-permute-start(bf16[2,64,128]{2,1,0:T(8,128)(2,1)} %get-tuple-element.42), channel_id=1, source_target_pairs={{8,16},{16,8},{9,17},{17,9},{10,18},{18,10},{11,19},{19,11},{12,20... | collective-permute-start | bytes 98312 | tf_op jit(solution)/shard_map/ppermute | solution.py:23
  24.5 13.8 %copy-start.1 = (bf16[32,64,128]{2,1,0:T(8,128)(2,1)}, bf16[32,64,128]{2,1,0:T(8,128)(2,1)S(1)}, u32[]{:S(2)}) copy-start(bf16[32,64,128]{2,1,0:T(8,128)(2,1)S(1)} %collective-permute-done.refs_0_.refs_17_) | copy-start | bytes 1572868
  24.5 35.8 %collective-permute-start.20 = (bf16[32,64,128]{2,1,0:T(8,128)(2,1)S(1)}, bf16[32,64,128]{2,1,0:T(8,128)(2,1)S(1)}, u32[]{:S(2)}, u32[]{:S(2)}) collective-permute-start(bf16[32,64,128]{2,1,0:T(8,128)(2,1)S(1)} %collective-permute-done.refs_0_.refs_17_), channel_id=1, source_target_pairs={{2,0},{4,6},{3,1},{5,7},{10,8},{12,14},{11,9},{13,15},{18,16},{20,... | collective-permute-start | bytes 1572872 | tf_op jit(solution)/shard_map/ppermute | solution.py:499
  34.3 1.0 copy-start.7
  38.3 54.4 %all-to-all-start.1 = ((bf16[8,8,64,128]{3,2,1,0:T(8,128)(2,1)}), bf16[8,8,64,128]{3,2,1,0:T(8,128)(2,1)S(1)}, u32[]{:S(2)}, u32[]{:S(2)}) async-start(bf16[8,8,64,128]{3,2,1,0:T(8,128)(2,1)} %get-tuple-element.50), calls=%async_computation.1 | async-start | bytes 2097152 | tf_op jit(solution)/shard_map/all_to_all | solution.py:599
  42.6 20.3 %copy-start.2 = (bf16[32,64,128]{2,1,0:T(8,128)(2,1)}, bf16[32,64,128]{2,1,0:T(8,128)(2,1)S(1)}, u32[]{:S(2)}) copy-start(bf16[32,64,128]{2,1,0:T(8,128)(2,1)S(1)} %collective-permute-done.2.refs_0_.refs_8_) | copy-start | bytes 1572868
  42.6 27.7 %collective-permute-start.3 = (bf16[32,64,128]{2,1,0:T(8,128)(2,1)S(1)}, bf16[32,64,128]{2,1,0:T(8,128)(2,1)S(1)}, u32[]{:S(2)}, u32[]{:S(2)}) collective-permute-start(bf16[32,64,128]{2,1,0:T(8,128)(2,1)S(1)} %collective-permute-done.2.refs_0_.refs_8_), channel_id=1, source_target_pairs={{2,0},{4,6},{3,1},{5,7},{10,8},{12,14},{11,9},{13,15},{18,16},{20,... | collective-permute-start | bytes 1572872 | tf_op jit(solution)/shard_map/ppermute | solution.py:499
  44.0 29.5 %collective-permute-start.17 = (bf16[24,64,128]{2,1,0:T(8,128)(2,1)}, bf16[24,64,128]{2,1,0:T(8,128)(2,1)S(1)}, u32[]{:S(2)}, u32[]{:S(2)}) collective-permute-start(bf16[24,64,128]{2,1,0:T(8,128)(2,1)} %get-tuple-element.47), channel_id=1, source_target_pairs={{0,8},{1,9},{8,0},{9,1},{16,24},{17,25},{24,16},{25,17},{2,10},{3,... | collective-permute-start | bytes 1179656 | tf_op jit(solution)/shard_map/ppermute | solution.py:561
  44.1 13.6 %collective-permute-start.15 = (bf16[36,8,128]{2,1,0:T(8,128)(2,1)}, bf16[36,8,128]{2,1,0:T(8,128)(2,1)S(1)}, u32[]{:S(2)}, u32[]{:S(2)}) collective-permute-start(bf16[36,8,128]{2,1,0:T(8,128)(2,1)} %get-tuple-element.45), channel_id=1, source_target_pairs={{0,1},{1,0},{2,3},{3,2},{4,5},{5,4},{6,7},{7,6},{8,9},{9,8},{10,11... | collective-permute-start | bytes 221192 | tf_op jit(solution)/shard_map/ppermute | solution.py:23
  45.8 22.8 %collective-permute-start.18 = (bf16[8,64,128]{2,1,0:T(8,128)(2,1)}, bf16[8,64,128]{2,1,0:T(8,128)(2,1)}, u32[]{:S(2)}, u32[]{:S(2)}) collective-permute-start(bf16[8,64,128]{2,1,0:T(8,128)(2,1)} %get-tuple-element.48), channel_id=1, source_target_pairs={{0,17},{1,16},{8,25},{9,24},{16,1},{17,0},{24,9},{25,8},{2,19},{3,... | collective-permute-start | bytes 393224 | tf_op jit(solution)/shard_map/ppermute | solution.py:561
  57.7 2.6 %copy-start.18 = (bf16[36,8,128]{2,1,0:T(8,128)(2,1)}, bf16[36,8,128]{2,1,0:T(8,128)(2,1)S(1)}, u32[]{:S(2)}) copy-start(bf16[36,8,128]{2,1,0:T(8,128)(2,1)S(1)} %collective-permute-done.15.col_pair_ref) | copy-start | bytes 221188
  57.7 11.3 %collective-permute-start.19 = (bf16[8,64,128]{2,1,0:T(8,128)(2,1)}, bf16[8,64,128]{2,1,0:T(8,128)(2,1)}, u32[]{:S(2)}, u32[]{:S(2)}) collective-permute-start(bf16[8,64,128]{2,1,0:T(8,128)(2,1)} %get-tuple-element.49), channel_id=1, source_target_pairs={{0,25},{1,24},{8,17},{9,16},{16,9},{17,8},{24,1},{25,0},{2,27},{3,... | collective-permute-start | bytes 393224 | tf_op jit(solution)/shard_map/ppermute | solution.py:561
  60.4 2.6 %copy-start.3 = (bf16[32,64,128]{2,1,0:T(8,128)(2,1)}, bf16[32,64,128]{2,1,0:T(8,128)(2,1)S(1)}, u32[]{:S(2)}) copy-start(bf16[32,64,128]{2,1,0:T(8,128)(2,1)S(1)} %collective-permute-done.20.refs_1_.refs_9_) | copy-start | bytes 1572868
  60.4 7.2 %collective-permute-start.16 = (bf16[36,8,128]{2,1,0:T(8,128)(2,1)}, bf16[36,8,128]{2,1,0:T(8,128)(2,1)S(1)}, u32[]{:S(2)}, u32[]{:S(2)}) collective-permute-start(bf16[36,8,128]{2,1,0:T(8,128)(2,1)} %get-tuple-element.46), channel_id=1, source_target_pairs={{1,2},{2,1},{3,4},{4,3},{5,6},{6,5},{9,10},{10,9},{11,12},{12,11},... | collective-permute-start | bytes 221192 | tf_op jit(solution)/shard_map/ppermute | solution.py:23
  68.2 6.5 %collective-permute-start.21 = (bf16[8,64,128]{2,1,0:T(8,128)(2,1)}, bf16[8,64,128]{2,1,0:T(8,128)(2,1)S(1)}, u32[]{:S(2)}, u32[]{:S(2)}) collective-permute-start(bf16[8,64,128]{2,1,0:T(8,128)(2,1)} %get-tuple-element.51), channel_id=1, source_target_pairs={{0,1},{1,0},{8,9},{9,8},{16,17},{17,16},{24,25},{25,24},{2,3},{3,2... | collective-permute-start | bytes 393224 | tf_op jit(solution)/shard_map/ppermute | solution.py:561
  68.6 7.6 %collective-permute-start.22 = (bf16[8,64,128]{2,1,0:T(8,128)(2,1)}, bf16[8,64,128]{2,1,0:T(8,128)(2,1)S(1)}, u32[]{:S(2)}, u32[]{:S(2)}) collective-permute-start(bf16[8,64,128]{2,1,0:T(8,128)(2,1)} %get-tuple-element.52), channel_id=1, source_target_pairs={{0,8},{1,9},{8,0},{9,1},{16,24},{17,25},{24,16},{25,17},{2,10},{3,... | collective-permute-start | bytes 393224 | tf_op jit(solution)/shard_map/ppermute | solution.py:561
  69.0 7.8 %collective-permute-start.23 = (bf16[8,64,128]{2,1,0:T(8,128)(2,1)}, bf16[8,64,128]{2,1,0:T(8,128)(2,1)S(1)}, u32[]{:S(2)}, u32[]{:S(2)}) collective-permute-start(bf16[8,64,128]{2,1,0:T(8,128)(2,1)} %get-tuple-element.53), channel_id=1, source_target_pairs={{0,9},{1,8},{8,1},{9,0},{16,25},{17,24},{24,17},{25,16},{2,11},{3,... | collective-permute-start | bytes 393224 | tf_op jit(solution)/shard_map/ppermute | solution.py:561
  70.3 0.9 copy-start.4
  70.3 8.6 %collective-permute-start.24 = (bf16[8,64,128]{2,1,0:T(8,128)(2,1)}, bf16[8,64,128]{2,1,0:T(8,128)(2,1)S(1)}, u32[]{:S(2)}, u32[]{:S(2)}) collective-permute-start(bf16[8,64,128]{2,1,0:T(8,128)(2,1)} %get-tuple-element.54), channel_id=1, source_target_pairs={{0,16},{1,17},{8,24},{9,25},{16,0},{17,1},{24,8},{25,9},{2,18},{3,... | collective-permute-start | bytes 393224 | tf_op jit(solution)/shard_map/ppermute | solution.py:561
  73.5 19.2 %copy-start.8 = (bf16[24,64,128]{2,1,0:T(8,128)(2,1)}, bf16[24,64,128]{2,1,0:T(8,128)(2,1)S(1)}, u32[]{:S(2)}) copy-start(bf16[24,64,128]{2,1,0:T(8,128)(2,1)S(1)} %collective-permute-done.17.refs_3_) | copy-start | bytes 1179652
  73.5 6.0 %collective-permute-start.25 = (bf16[8,64,128]{2,1,0:T(8,128)(2,1)}, bf16[8,64,128]{2,1,0:T(8,128)(2,1)S(1)}, u32[]{:S(2)}, u32[]{:S(2)}) collective-permute-start(bf16[8,64,128]{2,1,0:T(8,128)(2,1)} %get-tuple-element.55), channel_id=1, source_target_pairs={{0,17},{1,16},{8,25},{9,24},{16,1},{17,0},{24,9},{25,8},{2,19},{3,... | collective-permute-start | bytes 393224 | tf_op jit(solution)/shard_map/ppermute | solution.py:561
  74.7 18.0 %copy-start.9 = (bf16[8,64,128]{2,1,0:T(8,128)(2,1)}, bf16[8,64,128]{2,1,0:T(8,128)(2,1)S(1)}, u32[]{:S(2)}) copy-start(bf16[8,64,128]{2,1,0:T(8,128)(2,1)S(1)} %collective-permute-done.21.refs_10_) | copy-start | bytes 393220
  74.7 13.8 %collective-permute-start.26 = (bf16[8,64,128]{2,1,0:T(8,128)(2,1)}, bf16[8,64,128]{2,1,0:T(8,128)(2,1)S(1)}, u32[]{:S(2)}, u32[]{:S(2)}) collective-permute-start(bf16[8,64,128]{2,1,0:T(8,128)(2,1)} %get-tuple-element.56), channel_id=1, source_target_pairs={{0,24},{1,25},{8,16},{9,17},{16,8},{17,9},{24,0},{25,1},{2,26},{3,... | collective-permute-start | bytes 393224 | tf_op jit(solution)/shard_map/ppermute | solution.py:561
  76.2 16.5 %copy-start.10 = (bf16[8,64,128]{2,1,0:T(8,128)(2,1)}, bf16[8,64,128]{2,1,0:T(8,128)(2,1)S(1)}, u32[]{:S(2)}) copy-start(bf16[8,64,128]{2,1,0:T(8,128)(2,1)S(1)} %collective-permute-done.22.refs_11_) | copy-start | bytes 393220
  76.3 13.3 %collective-permute-start.27 = (bf16[8,64,128]{2,1,0:T(8,128)(2,1)}, bf16[8,64,128]{2,1,0:T(8,128)(2,1)S(1)}, u32[]{:S(2)}, u32[]{:S(2)}) collective-permute-start(bf16[8,64,128]{2,1,0:T(8,128)(2,1)} %get-tuple-element.57), channel_id=1, source_target_pairs={{0,25},{1,24},{8,17},{9,16},{16,9},{17,8},{24,1},{25,0},{2,27},{3,... | collective-permute-start | bytes 393224 | tf_op jit(solution)/shard_map/ppermute | solution.py:561
  76.8 15.9 %copy-start.11 = (bf16[8,64,128]{2,1,0:T(8,128)(2,1)}, bf16[8,64,128]{2,1,0:T(8,128)(2,1)S(1)}, u32[]{:S(2)}) copy-start(bf16[8,64,128]{2,1,0:T(8,128)(2,1)S(1)} %collective-permute-done.23.refs_12_) | copy-start | bytes 393220
  76.8 13.5 %collective-permute-start.10 = (bf16[8,64,128]{2,1,0:T(8,128)(2,1)}, bf16[8,64,128]{2,1,0:T(8,128)(2,1)S(1)}, u32[]{:S(2)}, u32[]{:S(2)}) collective-permute-start(bf16[8,64,128]{2,1,0:T(8,128)(2,1)} %get-tuple-element.40), channel_id=1, source_target_pairs={{0,25},{1,24},{8,17},{9,16},{16,9},{17,8},{24,1},{25,0},{2,27},{3,... | collective-permute-start | bytes 393224 | tf_op jit(solution)/shard_map/ppermute | solution.py:561
  78.9 13.8 %copy-start.12 = (bf16[8,64,128]{2,1,0:T(8,128)(2,1)}, bf16[8,64,128]{2,1,0:T(8,128)(2,1)S(1)}, u32[]{:S(2)}) copy-start(bf16[8,64,128]{2,1,0:T(8,128)(2,1)S(1)} %collective-permute-done.24.refs_13_) | copy-start | bytes 393220
  78.9 12.6 %collective-permute-start.4 = (bf16[8,64,128]{2,1,0:T(8,128)(2,1)}, bf16[8,64,128]{2,1,0:T(8,128)(2,1)S(1)}, u32[]{:S(2)}, u32[]{:S(2)}) collective-permute-start(bf16[8,64,128]{2,1,0:T(8,128)(2,1)} %get-tuple-element.34), channel_id=1, source_target_pairs={{0,1},{1,0},{8,9},{9,8},{16,17},{17,16},{24,25},{25,24},{2,3},{3,2... | collective-permute-start | bytes 393224 | tf_op jit(solution)/shard_map/ppermute | solution.py:561
  79.5 13.3 %copy-start.13 = (bf16[8,64,128]{2,1,0:T(8,128)(2,1)}, bf16[8,64,128]{2,1,0:T(8,128)(2,1)S(1)}, u32[]{:S(2)}) copy-start(bf16[8,64,128]{2,1,0:T(8,128)(2,1)S(1)} %collective-permute-done.25.refs_14_) | copy-start | bytes 393220
  79.5 22.6 %collective-permute-start.5 = (bf16[8,64,128]{2,1,0:T(8,128)(2,1)}, bf16[8,64,128]{2,1,0:T(8,128)(2,1)S(1)}, u32[]{:S(2)}, u32[]{:S(2)}) collective-permute-start(bf16[8,64,128]{2,1,0:T(8,128)(2,1)} %get-tuple-element.35), channel_id=1, source_target_pairs={{0,8},{1,9},{8,0},{9,1},{16,24},{17,25},{24,16},{25,17},{2,10},{3,... | collective-permute-start | bytes 393224 | tf_op jit(solution)/shard_map/ppermute | solution.py:561
  88.6 4.2 %copy-start.14 = (bf16[8,64,128]{2,1,0:T(8,128)(2,1)}, bf16[8,64,128]{2,1,0:T(8,128)(2,1)S(1)}, u32[]{:S(2)}) copy-start(bf16[8,64,128]{2,1,0:T(8,128)(2,1)S(1)} %collective-permute-done.26.refs_15_) | copy-start | bytes 393220
  88.6 13.5 %collective-permute-start.6 = (bf16[8,64,128]{2,1,0:T(8,128)(2,1)}, bf16[8,64,128]{2,1,0:T(8,128)(2,1)S(1)}, u32[]{:S(2)}, u32[]{:S(2)}) collective-permute-start(bf16[8,64,128]{2,1,0:T(8,128)(2,1)} %get-tuple-element.36), channel_id=1, source_target_pairs={{0,9},{1,8},{8,1},{9,0},{16,25},{17,24},{24,17},{25,16},{2,11},{3,... | collective-permute-start | bytes 393224 | tf_op jit(solution)/shard_map/ppermute | solution.py:561
  89.5 3.2 %copy-start.15 = (bf16[8,64,128]{2,1,0:T(8,128)(2,1)}, bf16[8,64,128]{2,1,0:T(8,128)(2,1)S(1)}, u32[]{:S(2)}) copy-start(bf16[8,64,128]{2,1,0:T(8,128)(2,1)S(1)} %collective-permute-done.27.refs_16_) | copy-start | bytes 393220
  89.5 12.6 %collective-permute-start.7 = (bf16[8,64,128]{2,1,0:T(8,128)(2,1)}, bf16[8,64,128]{2,1,0:T(8,128)(2,1)S(1)}, u32[]{:S(2)}, u32[]{:S(2)}) collective-permute-start(bf16[8,64,128]{2,1,0:T(8,128)(2,1)} %get-tuple-element.37), channel_id=1, source_target_pairs={{0,16},{1,17},{8,24},{9,25},{16,0},{17,1},{24,8},{25,9},{2,18},{3,... | collective-permute-start | bytes 393224 | tf_op jit(solution)/shard_map/ppermute | solution.py:561
  90.4 11.8 %copy-start.20 = (bf16[8,64,128]{2,1,0:T(8,128)(2,1)}, bf16[8,64,128]{2,1,0:T(8,128)(2,1)S(1)}, u32[]{:S(2)}) copy-start(bf16[8,64,128]{2,1,0:T(8,128)(2,1)S(1)} %collective-permute-done.10.refs_6_) | copy-start | bytes 393220
  90.4 11.8 %collective-permute-start.8 = (bf16[8,64,128]{2,1,0:T(8,128)(2,1)}, bf16[8,64,128]{2,1,0:T(8,128)(2,1)S(1)}, u32[]{:S(2)}, u32[]{:S(2)}) collective-permute-start(bf16[8,64,128]{2,1,0:T(8,128)(2,1)} %get-tuple-element.38), channel_id=1, source_target_pairs={{0,17},{1,16},{8,25},{9,24},{16,1},{17,0},{24,9},{25,8},{2,19},{3,... | collective-permute-start | bytes 393224 | tf_op jit(solution)/shard_map/ppermute | solution.py:561
  91.5 10.6 %copy-start.21 = (bf16[8,64,128]{2,1,0:T(8,128)(2,1)}, bf16[8,64,128]{2,1,0:T(8,128)(2,1)S(1)}, u32[]{:S(2)}) copy-start(bf16[8,64,128]{2,1,0:T(8,128)(2,1)S(1)} %collective-permute-done.4.refs_0_) | copy-start | bytes 393220
  91.5 10.6 %collective-permute-start.9 = (bf16[8,64,128]{2,1,0:T(8,128)(2,1)}, bf16[8,64,128]{2,1,0:T(8,128)(2,1)S(1)}, u32[]{:S(2)}, u32[]{:S(2)}) collective-permute-start(bf16[8,64,128]{2,1,0:T(8,128)(2,1)} %get-tuple-element.39), channel_id=1, source_target_pairs={{0,24},{1,25},{8,16},{9,17},{16,8},{17,9},{24,0},{25,1},{2,26},{3,... | collective-permute-start | bytes 393224 | tf_op jit(solution)/shard_map/ppermute | solution.py:561
  92.7 1.0 copy-start
  (8 other events, 5.6 us)

commit v5 on v4

--- a/solution.py
+++ b/solution.py
@@ -10,7 +10,7 @@
 from jax.sharding import PartitionSpec as P
 
 HEADS = 4
-PAIR = 2
+PAIR = 4
 EPSILON = 1e-06
 F32 = jnp.float32
 BF16 = jnp.bfloat16
@@ -54,12 +54,12 @@
 def norm_kernel(side, evens_of, image_ref, gain_ref, out_ref, *edge_refs):
     step = pl.program_id(0)
     *row_refs, left_ref, right_ref = edge_refs
-    tokens = image_ref[...]
-    normed = normalize(tokens.astype(F32), gain_ref[...])
+    tokens = image_ref[...].astype(F32)
+    normed = normalize(tokens, gain_ref[...])
     out_ref[...] = regions_of(normed, side).astype(BF16).reshape(out_ref.shape)
     margin, width, border = row_refs[0].shape[0], tokens.shape[1], left_ref.shape[1]
-    left_ref[...] = image_ref[:, pl.ds(0, border), :]
-    right_ref[...] = image_ref[:, pl.ds(width - border, border), :]
+    left_ref[...] = tokens[:, :border].astype(BF16)
+    right_ref[...] = tokens[:, width - border :].astype(BF16)
     row_even = evens_of()[0]
 
     def put(even, odd, first):
@@ -114,14 +114,16 @@
     row_even, col_even = evens
     margin, width = row_refs[0].shape[:2]
     height, border = flank_refs[0].shape[:2]
-    paired, other = row_refs[0][...], row_refs[1][...]
+    paired, other = row_refs[0][...].astype(F32), row_refs[1][...].astype(F32)
     above, below = either(row_even, other, paired), either(row_even, paired, other)
     for out_ref, flag in ((out_refs[0], col_even), (out_refs[1], ~col_even)):
         right = lambda rows: rows[:, width - border :]
         left = lambda rows: rows[:, :border]
-        out_ref[pl.ds(0, margin)] = either(flag, right(above), left(above))
+        out_ref[pl.ds(0, margin)] = either(flag, right(above), left(above)).astype(BF16)
         out_ref[pl.ds(margin, height)] = either(flag, flank_refs[1][...], flank_refs[0][...])
-        out_ref[pl.ds(margin + height, margin)] = either(flag, right(below), left(below))
+        out_ref[pl.ds(margin + height, margin)] = either(flag, right(below), left(below)).astype(
+            BF16
+        )
 
 
 def pack_kernel(jobs, options, outputs, evens_of, capacity, layers, place_of, wanted_ref, *refs):
@@ -228,7 +230,7 @@
     step = pl.program_id(0)
     height, width, channels = image_ref.shape
     strips = height // side
-    border = col_pair_ref.shape[1]
+    beside, border = col_pair_ref.shape[1], 8
 
     @pl.when(step == 0)
     def _():
@@ -240,8 +242,8 @@
         padded[pl.ds(margin, height), inner] = image_ref[...].astype(F32)
         padded[pl.ds(margin + height, margin), inner] = either(row_even, paired, other)
         paired, other = col_pair_ref[...].astype(F32), col_other_ref[...].astype(F32)
-        padded[:, :border] = either(col_even, other, paired)
-        padded[:, pl.ds(border + width, border)] = either(col_even, paired, other)
+        padded[:, pl.ds(border - beside, beside)] = either(col_even, other, paired)
+        padded[:, pl.ds(border + width, beside)] = either(col_even, paired, other)
 
     @pl.when(step < strips)
     def _():
@@ -279,7 +281,7 @@
     position, sources, image, around, gain, qkv_weight, lce_weight, side, margin, evens_of, place_of
 ):
     height, width, channels = image.shape
-    border = around[-1].shape[1]
+    border = 8
     tokens = height * width
     strips = height // side
     pairs = position.shape[0]
@@ -454,7 +456,7 @@
     height, width, channels = image.shape
     area = side * side
     per_row = width // side
-    batch = math.gcd(per_row, 4)
+    batch = math.gcd(per_row, 8)
     halves = per_row // batch
     steps = height // side * halves
     full = lambda a: pl.BlockSpec(a.shape, lambda i, position: (0,) * a.ndim)
@@ -555,7 +557,7 @@
     )
 
     margin = (lce_weight.shape[0] - 1) // 2
-    normed, *edges = norm_regions(image, norm_gain, side, margin, 8, evens_of)
+    normed, *edges = norm_regions(image, norm_gain, side, margin, margin, evens_of)
 
     def swap(part, far):
         return lax.ppermute(part, ("rows", "x"), [(i, i ^ far) for i in range(peers)])

time: 116 us -> 112 us (0.966)
  waiting for transfers between devices: 25.3 us -> 22.7 us
  Pallas kernels: 32.2 us -> 30 us
    ppermute x4, waiting for transfers between devices: 13.1 us -> 10.7 us  [with_pairs(): lax.ppermute(part, axis, pairs)]
    pallas_call x1, Pallas kernels: 12.6 us -> 10.3 us  [tail(): pl.pallas_call(functools.partial(tail_kernel, side, picks, batch, early,...]
where the time goes in v5:
time: 112 us; the launch traced here: 111 us
  starting transfers between devices  45.1 us (40%)
  Pallas kernels  30 us (27%)
  waiting for transfers between devices  22.7 us (20%)
  blocking collectives  8.09 us (7%)
  local copies, waits for them, and re-layouts  4.13 us (4%)
    ppermute x19, starting transfers between devices, swap(): lax.ppermute(part, ('rows', 'x'), [(i, i ^ far) for i in range(peers)])  21.9 us
    ppermute x4, waiting for transfers between devices, with_pairs(): lax.ppermute(part, axis, pairs)  10.7 us
    ppermute x4, starting transfers between devices, with_pairs(): lax.ppermute(part, axis, pairs)  10.6 us
    pallas_call x1, Pallas kernels, tail(): pl.pallas_call(functools.partial(tail_kernel, side, picks, batch, early,...  10.3 us
    pallas_call x1, Pallas kernels, context_and_regions(): pl.pallas_call(functools.partial(context_kernel, side, margin, evens_of,...  8.41 us
    ppermute x5, starting transfers between devices, hop(): return lax.ppermute(block, 'z', pairs)  8.23 us
    all_to_all x1, blocking collectives, block(): lax.all_to_all(requests.reshape(peers, 1, lanes), ('rows', 'x'), 0, 0, ti...  8.09 us
    pallas_call x3, Pallas kernels, pack(): pl.pallas_call(functools.partial(pack_kernel, tuple(jobs), tuple(map(len,...  7.59 us
  transfers between devices with their start and end apart: 29, of which 4 were waited for; matrix products, arithmetic and copies ran while one was open for 2% of the time, Pallas kernels for 14%

profile of v5, /device:TPU:17, one launch (start us, length us, event | category | flops | bytes accessed | tf_op | source)
XLA Modules:
  0.0 111.2 jit_solution(8910427998294316781)
XLA Ops:
  0.0 3.7 %norm_regions.1 = (bf16[32,64,128]{2,1,0:T(8,128)(2,1)}, bf16[2,64,128]{2,1,0:T(8,128)(2,1)}, bf16[2,64,128]{2,1,0:T(8,128)(2,1)}, bf16[32,2,128]{2,1,0:T(2,128)(2,1)}, bf16[32,2,128]{2,1,0:T(2,128)(2,1)}) custom-call(bf16[32,64,128]{2,1,0:T(8,128)(2,1)} %refs_10_.1, f32[1,128]{1,0:T(1,128)} %bitcast.6), custom_call_target="tpu_custom_call" | custom-call | flops 2621440 | bytes 1048576 | tf_op jit(solution)/shard_map/norm_regions/pallas_call | solution.py:81
  3.7 1.4 %collective-permute-start.1 = (bf16[32,64,128]{2,1,0:T(8,128)(2,1)}, bf16[32,64,128]{2,1,0:T(8,128)(2,1)S(1)}, u32[]{:S(2)}, u32[]{:S(2)}) collective-permute-start(bf16[32,64,128]{2,1,0:T(8,128)(2,1)} %get-tuple-element.33.refs_0_), channel_id=1, source_target_pairs={{0,2},{2,0},{4,6},{6,4},{1,3},{3,1},{5,7},{7,5},{8,10},{10,8},{12,... | collective-permute-start | bytes 1572872 | tf_op jit(solution)/shard_map/ppermute | solution.py:501
  5.0 1.2 %collective-permute-start.13 = (bf16[32,64,128]{2,1,0:T(8,128)(2,1)}, bf16[32,64,128]{2,1,0:T(8,128)(2,1)S(1)}, u32[]{:S(2)}, u32[]{:S(2)}) collective-permute-start(bf16[32,64,128]{2,1,0:T(8,128)(2,1)} %get-tuple-element.33.refs_0_), channel_id=1, source_target_pairs={{0,1},{1,0},{8,9},{9,8},{16,17},{17,16},{24,25},{25,24},{2,3},{3,2... | collective-permute-start | bytes 1572872 | tf_op jit(solution)/shard_map/ppermute | solution.py:563
  6.2 1.2 %collective-permute-start.14 = (bf16[32,64,128]{2,1,0:T(8,128)(2,1)}, bf16[32,64,128]{2,1,0:T(8,128)(2,1)S(1)}, u32[]{:S(2)}, u32[]{:S(2)}) collective-permute-start(bf16[32,64,128]{2,1,0:T(8,128)(2,1)} %get-tuple-element.33.refs_0_), channel_id=1, source_target_pairs={{0,16},{1,17},{8,24},{9,25},{16,0},{17,1},{24,8},{25,9},{2,18},{3,... | collective-permute-start | bytes 1572872 | tf_op jit(solution)/shard_map/ppermute | solution.py:563
  7.5 1.9 %collective-permute-start = (bf16[32,64,128]{2,1,0:T(8,128)(2,1)}, bf16[32,64,128]{2,1,0:T(8,128)(2,1)S(1)}, u32[]{:S(2)}, u32[]{:S(2)}) collective-permute-start(bf16[32,64,128]{2,1,0:T(8,128)(2,1)} %get-tuple-element.33.refs_0_), channel_id=1, source_target_pairs={{2,4},{4,2},{3,5},{5,3},{10,12},{12,10},{11,13},{13,11},{18,20},{2... | collective-permute-start | bytes 1572872 | tf_op jit(solution)/shard_map/ppermute | solution.py:501
  9.4 1.6 %collective-permute-start.11 = (bf16[2,64,128]{2,1,0:T(8,128)(2,1)}, bf16[2,64,128]{2,1,0:T(8,128)(2,1)S(1)}, u32[]{:S(2)}, u32[]{:S(2)}) collective-permute-start(bf16[2,64,128]{2,1,0:T(8,128)(2,1)} %get-tuple-element.41), channel_id=1, source_target_pairs={{0,8},{8,0},{16,24},{24,16},{1,9},{9,1},{17,25},{25,17},{2,10},{10... | collective-permute-start | bytes 98312 | tf_op jit(solution)/shard_map/ppermute | solution.py:23
  11.0 0.8 copy.12
  11.9 4.9 %collective-permute-done.1.refs_3_.refs_6_ = bf16[32,64,128]{2,1,0:T(8,128)(2,1)S(1)} collective-permute-done((bf16[32,64,128]{2,1,0:T(8,128)(2,1)}, bf16[32,64,128]{2,1,0:T(8,128)(2,1)S(1)}, u32[]{:S(2)}, u32[]{:S(2)}) %collective-permute-start.1) | collective-permute-done | bytes 524320 | tf_op jit(solution)/shard_map/ppermute | solution.py:501
  16.7 2.1 %collective-permute-start.2 = (bf16[32,64,128]{2,1,0:T(8,128)(2,1)S(1)}, bf16[32,64,128]{2,1,0:T(8,128)(2,1)S(1)}, u32[]{:S(2)}, u32[]{:S(2)}) collective-permute-start(bf16[32,64,128]{2,1,0:T(8,128)(2,1)S(1)} %collective-permute-done.1.refs_3_.refs_6_), channel_id=1, source_target_pairs={{2,4},{4,2},{3,5},{5,3},{10,12},{12,10},{11,13},{13,11},{18,20},{2... | collective-permute-start | bytes 1572872 | tf_op jit(solution)/shard_map/ppermute | solution.py:501
  19.0 0.5 and_select_fusion.25
  19.6 4.8 %collective-permute-start.12 = (bf16[2,64,128]{2,1,0:T(8,128)(2,1)}, bf16[2,64,128]{2,1,0:T(8,128)(2,1)S(1)}, u32[]{:S(2)}, u32[]{:S(2)}) collective-permute-start(bf16[2,64,128]{2,1,0:T(8,128)(2,1)} %get-tuple-element.42), channel_id=1, source_target_pairs={{8,16},{16,8},{9,17},{17,9},{10,18},{18,10},{11,19},{19,11},{12,20... | collective-permute-start | bytes 98312 | tf_op jit(solution)/shard_map/ppermute | solution.py:23
  24.4 1.6 %collective-permute-start.20 = (bf16[32,64,128]{2,1,0:T(8,128)(2,1)S(1)}, bf16[32,64,128]{2,1,0:T(8,128)(2,1)S(1)}, u32[]{:S(2)}, u32[]{:S(2)}) collective-permute-start(bf16[32,64,128]{2,1,0:T(8,128)(2,1)S(1)} %collective-permute-done.refs_0_.refs_17_), channel_id=1, source_target_pairs={{2,0},{4,6},{3,1},{5,7},{10,8},{12,14},{11,9},{13,15},{18,16},{20,... | collective-permute-start | bytes 1572872 | tf_op jit(solution)/shard_map/ppermute | solution.py:501
  26.0 0.2 select_reduce_fusion
  26.2 8.1 %all_to_all.10.wanted_ref = s32[8,1,128]{2,1,0:T(1,128)} all-to-all(s32[8,1,128]{2,1,0:T(1,128)S(1)} %bitcast.5), channel_id=1, replica_groups=mesh['rows'=4,'z'=4,'x'=2] {'rows','x'}, dimensions={0} | all-to-all | bytes 8192 | tf_op jit(solution)/shard_map/all_to_all | solution.py:555
  34.4 0.5 copy-done.17
  34.9 0.2 copy-done.6
  35.1 0.2 copy-done.7
  35.3 3.0 %pack.4 = (bf16[24,64,128]{2,1,0:T(8,128)(2,1)}, bf16[8,64,128]{2,1,0:T(8,128)(2,1)}, bf16[8,64,128]{2,1,0:T(8,128)(2,1)}, bf16[8,8,64,128]{3,2,1,0:T(8,128)(2,1...) custom-call(s32[8,1,128]{2,1,0:T(1,128)} %all_to_all.10.wanted_ref, ...), custom_call_target="tpu_custom_call" | custom-call | bytes 3481600 | tf_op jit(solution)/shard_map/pack/pallas_call | solution.py:166
  38.3 4.3 %all-to-all-start.1 = ((bf16[8,8,64,128]{3,2,1,0:T(8,128)(2,1)}), bf16[8,8,64,128]{3,2,1,0:T(8,128)(2,1)S(1)}, u32[]{:S(2)}, u32[]{:S(2)}) async-start(bf16[8,8,64,128]{3,2,1,0:T(8,128)(2,1)} %get-tuple-element.50), calls=%async_computation.1 | async-start | bytes 2097152 | tf_op jit(solution)/shard_map/all_to_all | solution.py:601
  42.6 1.3 %collective-permute-start.3 = (bf16[32,64,128]{2,1,0:T(8,128)(2,1)S(1)}, bf16[32,64,128]{2,1,0:T(8,128)(2,1)S(1)}, u32[]{:S(2)}, u32[]{:S(2)}) collective-permute-start(bf16[32,64,128]{2,1,0:T(8,128)(2,1)S(1)} %collective-permute-done.2.refs_0_.refs_8_), channel_id=1, source_target_pairs={{2,0},{4,6},{3,1},{5,7},{10,8},{12,14},{11,9},{13,15},{18,16},{20,... | collective-permute-start | bytes 1572872 | tf_op jit(solution)/shard_map/ppermute | solution.py:501
  44.0 0.2 collective-permute-start.17
  44.1 1.6 %collective-permute-start.15 = (bf16[36,2,128]{2,1,0:T(2,128)(2,1)}, bf16[36,2,128]{2,1,0:T(2,128)(2,1)S(1)}, u32[]{:S(2)}, u32[]{:S(2)}) collective-permute-start(bf16[36,2,128]{2,1,0:T(2,128)(2,1)} %get-tuple-element.45), channel_id=1, source_target_pairs={{0,1},{1,0},{2,3},{3,2},{4,5},{5,4},{6,7},{7,6},{8,9},{9,8},{10,11... | collective-permute-start | bytes 55304 | tf_op jit(solution)/shard_map/ppermute | solution.py:23
  45.8 1.2 %collective-permute-start.18 = (bf16[8,64,128]{2,1,0:T(8,128)(2,1)}, bf16[8,64,128]{2,1,0:T(8,128)(2,1)}, u32[]{:S(2)}, u32[]{:S(2)}) collective-permute-start(bf16[8,64,128]{2,1,0:T(8,128)(2,1)} %get-tuple-element.48), channel_id=1, source_target_pairs={{0,17},{1,16},{8,25},{9,24},{16,1},{17,0},{24,9},{25,8},{2,19},{3,... | collective-permute-start | bytes 393224 | tf_op jit(solution)/shard_map/ppermute | solution.py:563
  47.0 9.6 %collective-permute-done.15.col_pair_ref = bf16[36,2,128]{2,1,0:T(2,128)(2,1)S(1)} collective-permute-done((bf16[36,2,128]{2,1,0:T(2,128)(2,1)}, bf16[36,2,128]{2,1,0:T(2,128)(2,1)S(1)}, u32[]{:S(2)}, u32[]{:S(2)}) %collective-permute-start.15) | collective-permute-done | bytes 18464 | tf_op jit(solution)/shard_map/ppermute | solution.py:23
  56.5 2.6 %collective-permute-start.19 = (bf16[8,64,128]{2,1,0:T(8,128)(2,1)}, bf16[8,64,128]{2,1,0:T(8,128)(2,1)}, u32[]{:S(2)}, u32[]{:S(2)}) collective-permute-start(bf16[8,64,128]{2,1,0:T(8,128)(2,1)} %get-tuple-element.49), channel_id=1, source_target_pairs={{0,25},{1,24},{8,17},{9,16},{16,9},{17,8},{24,1},{25,0},{2,27},{3,... | collective-permute-start | bytes 393224 | tf_op jit(solution)/shard_map/ppermute | solution.py:563
  59.2 2.5 %collective-permute-start.16 = (bf16[36,2,128]{2,1,0:T(2,128)(2,1)}, bf16[36,2,128]{2,1,0:T(2,128)(2,1)S(1)}, u32[]{:S(2)}, u32[]{:S(2)}) collective-permute-start(bf16[36,2,128]{2,1,0:T(2,128)(2,1)} %get-tuple-element.46), channel_id=1, source_target_pairs={{1,2},{2,1},{3,4},{4,3},{5,6},{6,5},{9,10},{10,9},{11,12},{12,11},... | collective-permute-start | bytes 55304 | tf_op jit(solution)/shard_map/ppermute | solution.py:23
  61.7 2.3 %pack.5 = (bf16[8,64,128]{2,1,0:T(8,128)(2,1)}, bf16[8,64,128]{2,1,0:T(8,128)(2,1)}, bf16[8,64,128]{2,1,0:T(8,128)(2,1)}, bf16[8,64,128]{2,1,0:T(8,128)(2,1)}, b...) custom-call(s32[8,1,128]{2,1,0:T(1,128)} %all_to_all.10.wanted_ref, ...), custom_call_target="tpu_custom_call" | custom-call | bytes 1835008 | tf_op jit(solution)/shard_map/pack/pallas_call | solution.py:166
  64.0 1.1 %collective-permute-done.16.col_other_ref = bf16[36,2,128]{2,1,0:T(2,128)(2,1)S(1)} collective-permute-done((bf16[36,2,128]{2,1,0:T(2,128)(2,1)}, bf16[36,2,128]{2,1,0:T(2,128)(2,1)S(1)}, u32[]{:S(2)}, u32[]{:S(2)}) %collective-permute-start.16) | collective-permute-done | bytes 18464 | tf_op jit(solution)/shard_map/ppermute | solution.py:23
  65.2 0.6 copy-done.19
  65.8 0.8 collective-permute-start.21
  66.7 1.2 %collective-permute-start.23 = (bf16[8,64,128]{2,1,0:T(8,128)(2,1)}, bf16[8,64,128]{2,1,0:T(8,128)(2,1)S(1)}, u32[]{:S(2)}, u32[]{:S(2)}) collective-permute-start(bf16[8,64,128]{2,1,0:T(8,128)(2,1)} %get-tuple-element.53), channel_id=1, source_target_pairs={{0,9},{1,8},{8,1},{9,0},{16,25},{17,24},{24,17},{25,16},{2,11},{3,... | collective-permute-start | bytes 393224 | tf_op jit(solution)/shard_map/ppermute | solution.py:563
  67.9 1.1 collective-permute-start.24
  68.9 2.3 %pack.3 = (bf16[8,64,128]{2,1,0:T(8,128)(2,1)}, bf16[8,64,128]{2,1,0:T(8,128)(2,1)}, bf16[8,64,128]{2,1,0:T(8,128)(2,1)}, bf16[8,64,128]{2,1,0:T(8,128)(2,1)}, b...) custom-call(s32[8,1,128]{2,1,0:T(1,128)} %all_to_all.10.wanted_ref, ...), custom_call_target="tpu_custom_call" | custom-call | bytes 1835008 | tf_op jit(solution)/shard_map/pack/pallas_call | solution.py:166
  71.2 1.1 collective-permute-start.25
  72.3 1.5 %collective-permute-start.26 = (bf16[8,64,128]{2,1,0:T(8,128)(2,1)}, bf16[8,64,128]{2,1,0:T(8,128)(2,1)S(1)}, u32[]{:S(2)}, u32[]{:S(2)}) collective-permute-start(bf16[8,64,128]{2,1,0:T(8,128)(2,1)} %get-tuple-element.56), channel_id=1, source_target_pairs={{0,24},{1,25},{8,16},{9,17},{16,8},{17,9},{24,0},{25,1},{2,26},{3,... | collective-permute-start | bytes 393224 | tf_op jit(solution)/shard_map/ppermute | solution.py:563
  73.8 1.0 collective-permute-start.27
  74.8 1.7 %collective-permute-start.10 = (bf16[8,64,128]{2,1,0:T(8,128)(2,1)}, bf16[8,64,128]{2,1,0:T(8,128)(2,1)S(1)}, u32[]{:S(2)}, u32[]{:S(2)}) collective-permute-start(bf16[8,64,128]{2,1,0:T(8,128)(2,1)} %get-tuple-element.40), channel_id=1, source_target_pairs={{0,25},{1,24},{8,17},{9,16},{16,9},{17,8},{24,1},{25,0},{2,27},{3,... | collective-permute-start | bytes 393224 | tf_op jit(solution)/shard_map/ppermute | solution.py:563
  76.5 1.0 collective-permute-start.4
  77.5 1.8 %collective-permute-start.5 = (bf16[8,64,128]{2,1,0:T(8,128)(2,1)}, bf16[8,64,128]{2,1,0:T(8,128)(2,1)S(1)}, u32[]{:S(2)}, u32[]{:S(2)}) collective-permute-start(bf16[8,64,128]{2,1,0:T(8,128)(2,1)} %get-tuple-element.35), channel_id=1, source_target_pairs={{0,8},{1,9},{8,0},{9,1},{16,24},{17,25},{24,16},{25,17},{2,10},{3,... | collective-permute-start | bytes 393224 | tf_op jit(solution)/shard_map/ppermute | solution.py:563
  79.3 7.1 %collective-permute-done.26.refs_15_ = bf16[8,64,128]{2,1,0:T(8,128)(2,1)S(1)} collective-permute-done((bf16[8,64,128]{2,1,0:T(8,128)(2,1)}, bf16[8,64,128]{2,1,0:T(8,128)(2,1)S(1)}, u32[]{:S(2)}, u32[]{:S(2)}) %collective-permute-start.26) | collective-permute-done | bytes 131104 | tf_op jit(solution)/shard_map/ppermute | solution.py:563
  86.3 0.8 collective-permute-start.6
  87.1 0.8 collective-permute-start.7
  87.9 1.3 %collective-permute-start.8 = (bf16[8,64,128]{2,1,0:T(8,128)(2,1)}, bf16[8,64,128]{2,1,0:T(8,128)(2,1)S(1)}, u32[]{:S(2)}, u32[]{:S(2)}) collective-permute-start(bf16[8,64,128]{2,1,0:T(8,128)(2,1)} %get-tuple-element.38), channel_id=1, source_target_pairs={{0,17},{1,16},{8,25},{9,24},{16,1},{17,0},{24,9},{25,8},{2,19},{3,... | collective-permute-start | bytes 393224 | tf_op jit(solution)/shard_map/ppermute | solution.py:563
  89.3 1.4 %collective-permute-start.9 = (bf16[8,64,128]{2,1,0:T(8,128)(2,1)}, bf16[8,64,128]{2,1,0:T(8,128)(2,1)S(1)}, u32[]{:S(2)}, u32[]{:S(2)}) collective-permute-start(bf16[8,64,128]{2,1,0:T(8,128)(2,1)} %get-tuple-element.39), channel_id=1, source_target_pairs={{0,24},{1,25},{8,16},{9,17},{16,8},{17,9},{24,0},{25,1},{2,26},{3,... | collective-permute-start | bytes 393224 | tf_op jit(solution)/shard_map/ppermute | solution.py:563
  90.7 0.9 copy-done
  91.6 8.4 %context.1 = (f32[2048,128]{1,0:T(8,128)}, bf16[2048,128]{1,0:T(8,128)(2,1)}, bf16[128,64,128]{2,1,0:T(8,128)(2,1)}) custom-call(s32[128]{0:T(128)} %get-tuple-element.61.position_ref, bf16[32,64,128]{2,1,0:T(8,128)(2,1)} %refs_10_.1, bf16[2,64,128]{2,1,0:T(8,128)(2,1)} %copy-done.16, bf16[2,64,128]{2,1,0:T(8,128)(2,1)} %copy-done.17, ...), custom_call_target="tpu_custom_call" | custom-call | flops 157286400 | bytes 10485760 | tf_op jit(solution)/shard_map/context/pallas_call | solution.py:294
  100.2 0.5 copy-done.22
  100.9 10.3 %tail.1 = bf16[32,64,128]{2,1,0:T(8,128)(2,1)} custom-call(s32[128]{0:T(128)} %get-tuple-element.61.position_ref, bf16[8,64,128]{2,1,0:T(8,128)(2,1)} %copy-done.21, bf16[8,64,128]{2,1,0:T(8,128)(2,1)} %copy-done.22, bf16[8,64,128]{2,1,0:T(8,128)(2,1)} %copy-done.23, bf16[8,64,128]{2,1,0:T(8,128)(2,1)} %copy-done.24, bf16[8,64,128]{2,1,0:T(8,128)(2,1)} %copy-done.25, ...), custom_call_target="tpu_custom_call" | custom-call | flops 1048576000 | bytes 4194304 | tf_op jit(solution)/shard_map/tail/pallas_call | solution.py:471
  (78 shorter events, 0.8 us)
Async XLA Ops:
  3.7 13.1 %collective-permute-start.1 = (bf16[32,64,128]{2,1,0:T(8,128)(2,1)}, bf16[32,64,128]{2,1,0:T(8,128)(2,1)S(1)}, u32[]{:S(2)}, u32[]{:S(2)}) collective-permute-start(bf16[32,64,128]{2,1,0:T(8,128)(2,1)} %get-tuple-element.33.refs_0_), channel_id=1, source_target_pairs={{0,2},{2,0},{4,6},{6,4},{1,3},{3,1},{5,7},{7,5},{8,10},{10,8},{12,... | collective-permute-start | bytes 1572872 | tf_op jit(solution)/shard_map/ppermute | solution.py:501
  5.0 29.3 %collective-permute-start.13 = (bf16[32,64,128]{2,1,0:T(8,128)(2,1)}, bf16[32,64,128]{2,1,0:T(8,128)(2,1)S(1)}, u32[]{:S(2)}, u32[]{:S(2)}) collective-permute-start(bf16[32,64,128]{2,1,0:T(8,128)(2,1)} %get-tuple-element.33.refs_0_), channel_id=1, source_target_pairs={{0,1},{1,0},{8,9},{9,8},{16,17},{17,16},{24,25},{25,24},{2,3},{3,2... | collective-permute-start | bytes 1572872 | tf_op jit(solution)/shard_map/ppermute | solution.py:563
  6.2 28.1 %collective-permute-start.14 = (bf16[32,64,128]{2,1,0:T(8,128)(2,1)}, bf16[32,64,128]{2,1,0:T(8,128)(2,1)S(1)}, u32[]{:S(2)}, u32[]{:S(2)}) collective-permute-start(bf16[32,64,128]{2,1,0:T(8,128)(2,1)} %get-tuple-element.33.refs_0_), channel_id=1, source_target_pairs={{0,16},{1,17},{8,24},{9,25},{16,0},{17,1},{24,8},{25,9},{2,18},{3,... | collective-permute-start | bytes 1572872 | tf_op jit(solution)/shard_map/ppermute | solution.py:563
  7.5 16.9 %collective-permute-start = (bf16[32,64,128]{2,1,0:T(8,128)(2,1)}, bf16[32,64,128]{2,1,0:T(8,128)(2,1)S(1)}, u32[]{:S(2)}, u32[]{:S(2)}) collective-permute-start(bf16[32,64,128]{2,1,0:T(8,128)(2,1)} %get-tuple-element.33.refs_0_), channel_id=1, source_target_pairs={{2,4},{4,2},{3,5},{5,3},{10,12},{12,10},{11,13},{13,11},{18,20},{2... | collective-permute-start | bytes 1572872 | tf_op jit(solution)/shard_map/ppermute | solution.py:501
  9.4 10.2 %collective-permute-start.11 = (bf16[2,64,128]{2,1,0:T(8,128)(2,1)}, bf16[2,64,128]{2,1,0:T(8,128)(2,1)S(1)}, u32[]{:S(2)}, u32[]{:S(2)}) collective-permute-start(bf16[2,64,128]{2,1,0:T(8,128)(2,1)} %get-tuple-element.41), channel_id=1, source_target_pairs={{0,8},{8,0},{16,24},{24,16},{1,9},{9,1},{17,25},{25,17},{2,10},{10... | collective-permute-start | bytes 98312 | tf_op jit(solution)/shard_map/ppermute | solution.py:23
  16.7 17.6 %copy-start.5 = (bf16[32,64,128]{2,1,0:T(8,128)(2,1)}, bf16[32,64,128]{2,1,0:T(8,128)(2,1)S(1)}, u32[]{:S(2)}) copy-start(bf16[32,64,128]{2,1,0:T(8,128)(2,1)S(1)} %collective-permute-done.1.refs_3_.refs_6_) | copy-start | bytes 1572868
  16.7 25.9 %collective-permute-start.2 = (bf16[32,64,128]{2,1,0:T(8,128)(2,1)S(1)}, bf16[32,64,128]{2,1,0:T(8,128)(2,1)S(1)}, u32[]{:S(2)}, u32[]{:S(2)}) collective-permute-start(bf16[32,64,128]{2,1,0:T(8,128)(2,1)S(1)} %collective-permute-done.1.refs_3_.refs_6_), channel_id=1, source_target_pairs={{2,4},{4,2},{3,5},{5,3},{10,12},{12,10},{11,13},{13,11},{18,20},{2... | collective-permute-start | bytes 1572872 | tf_op jit(solution)/shard_map/ppermute | solution.py:501
  19.6 14.8 %copy-start.16 = (bf16[2,64,128]{2,1,0:T(8,128)(2,1)}, bf16[2,64,128]{2,1,0:T(8,128)(2,1)S(1)}, u32[]{:S(2)}) copy-start(bf16[2,64,128]{2,1,0:T(8,128)(2,1)S(1)} %collective-permute-done.11.refs_4_.row_pair_ref) | copy-start | bytes 98308
  19.6 14.7 %collective-permute-start.12 = (bf16[2,64,128]{2,1,0:T(8,128)(2,1)}, bf16[2,64,128]{2,1,0:T(8,128)(2,1)S(1)}, u32[]{:S(2)}, u32[]{:S(2)}) collective-permute-start(bf16[2,64,128]{2,1,0:T(8,128)(2,1)} %get-tuple-element.42), channel_id=1, source_target_pairs={{8,16},{16,8},{9,17},{17,9},{10,18},{18,10},{11,19},{19,11},{12,20... | collective-permute-start | bytes 98312 | tf_op jit(solution)/shard_map/ppermute | solution.py:23
  24.4 13.9 %copy-start.1 = (bf16[32,64,128]{2,1,0:T(8,128)(2,1)}, bf16[32,64,128]{2,1,0:T(8,128)(2,1)S(1)}, u32[]{:S(2)}) copy-start(bf16[32,64,128]{2,1,0:T(8,128)(2,1)S(1)} %collective-permute-done.refs_0_.refs_17_) | copy-start | bytes 1572868
  24.4 34.7 %collective-permute-start.20 = (bf16[32,64,128]{2,1,0:T(8,128)(2,1)S(1)}, bf16[32,64,128]{2,1,0:T(8,128)(2,1)S(1)}, u32[]{:S(2)}, u32[]{:S(2)}) collective-permute-start(bf16[32,64,128]{2,1,0:T(8,128)(2,1)S(1)} %collective-permute-done.refs_0_.refs_17_), channel_id=1, source_target_pairs={{2,0},{4,6},{3,1},{5,7},{10,8},{12,14},{11,9},{13,15},{18,16},{20,... | collective-permute-start | bytes 1572872 | tf_op jit(solution)/shard_map/ppermute | solution.py:501
  34.3 1.0 copy-start.7
  38.3 52.4 %all-to-all-start.1 = ((bf16[8,8,64,128]{3,2,1,0:T(8,128)(2,1)}), bf16[8,8,64,128]{3,2,1,0:T(8,128)(2,1)S(1)}, u32[]{:S(2)}, u32[]{:S(2)}) async-start(bf16[8,8,64,128]{3,2,1,0:T(8,128)(2,1)} %get-tuple-element.50), calls=%async_computation.1 | async-start | bytes 2097152 | tf_op jit(solution)/shard_map/all_to_all | solution.py:601
  42.6 19.1 %copy-start.2 = (bf16[32,64,128]{2,1,0:T(8,128)(2,1)}, bf16[32,64,128]{2,1,0:T(8,128)(2,1)S(1)}, u32[]{:S(2)}) copy-start(bf16[32,64,128]{2,1,0:T(8,128)(2,1)S(1)} %collective-permute-done.2.refs_0_.refs_8_) | copy-start | bytes 1572868
  42.6 25.2 %collective-permute-start.3 = (bf16[32,64,128]{2,1,0:T(8,128)(2,1)S(1)}, bf16[32,64,128]{2,1,0:T(8,128)(2,1)S(1)}, u32[]{:S(2)}, u32[]{:S(2)}) collective-permute-start(bf16[32,64,128]{2,1,0:T(8,128)(2,1)S(1)} %collective-permute-done.2.refs_0_.refs_8_), channel_id=1, source_target_pairs={{2,0},{4,6},{3,1},{5,7},{10,8},{12,14},{11,9},{13,15},{18,16},{20,... | collective-permute-start | bytes 1572872 | tf_op jit(solution)/shard_map/ppermute | solution.py:501
  44.0 27.3 %collective-permute-start.17 = (bf16[24,64,128]{2,1,0:T(8,128)(2,1)}, bf16[24,64,128]{2,1,0:T(8,128)(2,1)S(1)}, u32[]{:S(2)}, u32[]{:S(2)}) collective-permute-start(bf16[24,64,128]{2,1,0:T(8,128)(2,1)} %get-tuple-element.47), channel_id=1, source_target_pairs={{0,8},{1,9},{8,0},{9,1},{16,24},{17,25},{24,16},{25,17},{2,10},{3,... | collective-permute-start | bytes 1179656 | tf_op jit(solution)/shard_map/ppermute | solution.py:563
  44.1 12.4 %collective-permute-start.15 = (bf16[36,2,128]{2,1,0:T(2,128)(2,1)}, bf16[36,2,128]{2,1,0:T(2,128)(2,1)S(1)}, u32[]{:S(2)}, u32[]{:S(2)}) collective-permute-start(bf16[36,2,128]{2,1,0:T(2,128)(2,1)} %get-tuple-element.45), channel_id=1, source_target_pairs={{0,1},{1,0},{2,3},{3,2},{4,5},{5,4},{6,7},{7,6},{8,9},{9,8},{10,11... | collective-permute-start | bytes 55304 | tf_op jit(solution)/shard_map/ppermute | solution.py:23
  45.8 20.8 %collective-permute-start.18 = (bf16[8,64,128]{2,1,0:T(8,128)(2,1)}, bf16[8,64,128]{2,1,0:T(8,128)(2,1)}, u32[]{:S(2)}, u32[]{:S(2)}) collective-permute-start(bf16[8,64,128]{2,1,0:T(8,128)(2,1)} %get-tuple-element.48), channel_id=1, source_target_pairs={{0,17},{1,16},{8,25},{9,24},{16,1},{17,0},{24,9},{25,8},{2,19},{3,... | collective-permute-start | bytes 393224 | tf_op jit(solution)/shard_map/ppermute | solution.py:563
  56.5 2.6 %copy-start.18 = (bf16[36,2,128]{2,1,0:T(2,128)(2,1)}, bf16[36,2,128]{2,1,0:T(2,128)(2,1)S(1)}, u32[]{:S(2)}) copy-start(bf16[36,2,128]{2,1,0:T(2,128)(2,1)S(1)} %collective-permute-done.15.col_pair_ref) | copy-start | bytes 55300
  56.5 10.1 %collective-permute-start.19 = (bf16[8,64,128]{2,1,0:T(8,128)(2,1)}, bf16[8,64,128]{2,1,0:T(8,128)(2,1)}, u32[]{:S(2)}, u32[]{:S(2)}) collective-permute-start(bf16[8,64,128]{2,1,0:T(8,128)(2,1)} %get-tuple-element.49), channel_id=1, source_target_pairs={{0,25},{1,24},{8,17},{9,16},{16,9},{17,8},{24,1},{25,0},{2,27},{3,... | collective-permute-start | bytes 393224 | tf_op jit(solution)/shard_map/ppermute | solution.py:563
  59.2 2.6 %copy-start.3 = (bf16[32,64,128]{2,1,0:T(8,128)(2,1)}, bf16[32,64,128]{2,1,0:T(8,128)(2,1)S(1)}, u32[]{:S(2)}) copy-start(bf16[32,64,128]{2,1,0:T(8,128)(2,1)S(1)} %collective-permute-done.20.refs_1_.refs_9_) | copy-start | bytes 1572868
  59.2 6.0 %collective-permute-start.16 = (bf16[36,2,128]{2,1,0:T(2,128)(2,1)}, bf16[36,2,128]{2,1,0:T(2,128)(2,1)S(1)}, u32[]{:S(2)}, u32[]{:S(2)}) collective-permute-start(bf16[36,2,128]{2,1,0:T(2,128)(2,1)} %get-tuple-element.46), channel_id=1, source_target_pairs={{1,2},{2,1},{3,4},{4,3},{5,6},{6,5},{9,10},{10,9},{11,12},{12,11},... | collective-permute-start | bytes 55304 | tf_op jit(solution)/shard_map/ppermute | solution.py:23
  65.8 6.5 %collective-permute-start.21 = (bf16[8,64,128]{2,1,0:T(8,128)(2,1)}, bf16[8,64,128]{2,1,0:T(8,128)(2,1)S(1)}, u32[]{:S(2)}, u32[]{:S(2)}) collective-permute-start(bf16[8,64,128]{2,1,0:T(8,128)(2,1)} %get-tuple-element.51), channel_id=1, source_target_pairs={{0,1},{1,0},{8,9},{9,8},{16,17},{17,16},{24,25},{25,24},{2,3},{3,2... | collective-permute-start | bytes 393224 | tf_op jit(solution)/shard_map/ppermute | solution.py:563
  66.6 7.3 %collective-permute-start.22 = (bf16[8,64,128]{2,1,0:T(8,128)(2,1)}, bf16[8,64,128]{2,1,0:T(8,128)(2,1)S(1)}, u32[]{:S(2)}, u32[]{:S(2)}) collective-permute-start(bf16[8,64,128]{2,1,0:T(8,128)(2,1)} %get-tuple-element.52), channel_id=1, source_target_pairs={{0,8},{1,9},{8,0},{9,1},{16,24},{17,25},{24,16},{25,17},{2,10},{3,... | collective-permute-start | bytes 393224 | tf_op jit(solution)/shard_map/ppermute | solution.py:563
  66.7 8.1 %collective-permute-start.23 = (bf16[8,64,128]{2,1,0:T(8,128)(2,1)}, bf16[8,64,128]{2,1,0:T(8,128)(2,1)S(1)}, u32[]{:S(2)}, u32[]{:S(2)}) collective-permute-start(bf16[8,64,128]{2,1,0:T(8,128)(2,1)} %get-tuple-element.53), channel_id=1, source_target_pairs={{0,9},{1,8},{8,1},{9,0},{16,25},{17,24},{24,17},{25,16},{2,11},{3,... | collective-permute-start | bytes 393224 | tf_op jit(solution)/shard_map/ppermute | solution.py:563
  67.9 1.1 copy-start.4
  67.9 8.6 %collective-permute-start.24 = (bf16[8,64,128]{2,1,0:T(8,128)(2,1)}, bf16[8,64,128]{2,1,0:T(8,128)(2,1)S(1)}, u32[]{:S(2)}, u32[]{:S(2)}) collective-permute-start(bf16[8,64,128]{2,1,0:T(8,128)(2,1)} %get-tuple-element.54), channel_id=1, source_target_pairs={{0,16},{1,17},{8,24},{9,25},{16,0},{17,1},{24,8},{25,9},{2,18},{3,... | collective-permute-start | bytes 393224 | tf_op jit(solution)/shard_map/ppermute | solution.py:563
  71.2 19.5 %copy-start.8 = (bf16[24,64,128]{2,1,0:T(8,128)(2,1)}, bf16[24,64,128]{2,1,0:T(8,128)(2,1)S(1)}, u32[]{:S(2)}) copy-start(bf16[24,64,128]{2,1,0:T(8,128)(2,1)S(1)} %collective-permute-done.17.refs_3_) | copy-start | bytes 1179652
  71.2 6.3 %collective-permute-start.25 = (bf16[8,64,128]{2,1,0:T(8,128)(2,1)}, bf16[8,64,128]{2,1,0:T(8,128)(2,1)S(1)}, u32[]{:S(2)}, u32[]{:S(2)}) collective-permute-start(bf16[8,64,128]{2,1,0:T(8,128)(2,1)} %get-tuple-element.55), channel_id=1, source_target_pairs={{0,17},{1,16},{8,25},{9,24},{16,1},{17,0},{24,9},{25,8},{2,19},{3,... | collective-permute-start | bytes 393224 | tf_op jit(solution)/shard_map/ppermute | solution.py:563
  72.3 18.4 %copy-start.9 = (bf16[8,64,128]{2,1,0:T(8,128)(2,1)}, bf16[8,64,128]{2,1,0:T(8,128)(2,1)S(1)}, u32[]{:S(2)}) copy-start(bf16[8,64,128]{2,1,0:T(8,128)(2,1)S(1)} %collective-permute-done.21.refs_10_) | copy-start | bytes 393220
  72.3 14.0 %collective-permute-start.26 = (bf16[8,64,128]{2,1,0:T(8,128)(2,1)}, bf16[8,64,128]{2,1,0:T(8,128)(2,1)S(1)}, u32[]{:S(2)}, u32[]{:S(2)}) collective-permute-start(bf16[8,64,128]{2,1,0:T(8,128)(2,1)} %get-tuple-element.56), channel_id=1, source_target_pairs={{0,24},{1,25},{8,16},{9,17},{16,8},{17,9},{24,0},{25,1},{2,26},{3,... | collective-permute-start | bytes 393224 | tf_op jit(solution)/shard_map/ppermute | solution.py:563
  73.8 16.8 %copy-start.10 = (bf16[8,64,128]{2,1,0:T(8,128)(2,1)}, bf16[8,64,128]{2,1,0:T(8,128)(2,1)S(1)}, u32[]{:S(2)}) copy-start(bf16[8,64,128]{2,1,0:T(8,128)(2,1)S(1)} %collective-permute-done.22.refs_11_) | copy-start | bytes 393220
  73.8 13.3 %collective-permute-start.27 = (bf16[8,64,128]{2,1,0:T(8,128)(2,1)}, bf16[8,64,128]{2,1,0:T(8,128)(2,1)S(1)}, u32[]{:S(2)}, u32[]{:S(2)}) collective-permute-start(bf16[8,64,128]{2,1,0:T(8,128)(2,1)} %get-tuple-element.57), channel_id=1, source_target_pairs={{0,25},{1,24},{8,17},{9,16},{16,9},{17,8},{24,1},{25,0},{2,27},{3,... | collective-permute-start | bytes 393224 | tf_op jit(solution)/shard_map/ppermute | solution.py:563
  74.8 15.9 %copy-start.11 = (bf16[8,64,128]{2,1,0:T(8,128)(2,1)}, bf16[8,64,128]{2,1,0:T(8,128)(2,1)S(1)}, u32[]{:S(2)}) copy-start(bf16[8,64,128]{2,1,0:T(8,128)(2,1)S(1)} %collective-permute-done.23.refs_12_) | copy-start | bytes 393220
  74.8 13.2 %collective-permute-start.10 = (bf16[8,64,128]{2,1,0:T(8,128)(2,1)}, bf16[8,64,128]{2,1,0:T(8,128)(2,1)S(1)}, u32[]{:S(2)}, u32[]{:S(2)}) collective-permute-start(bf16[8,64,128]{2,1,0:T(8,128)(2,1)} %get-tuple-element.40), channel_id=1, source_target_pairs={{0,25},{1,24},{8,17},{9,16},{16,9},{17,8},{24,1},{25,0},{2,27},{3,... | collective-permute-start | bytes 393224 | tf_op jit(solution)/shard_map/ppermute | solution.py:563
  76.5 14.2 %copy-start.12 = (bf16[8,64,128]{2,1,0:T(8,128)(2,1)}, bf16[8,64,128]{2,1,0:T(8,128)(2,1)S(1)}, u32[]{:S(2)}) copy-start(bf16[8,64,128]{2,1,0:T(8,128)(2,1)S(1)} %collective-permute-done.24.refs_13_) | copy-start | bytes 393220
  76.5 12.8 %collective-permute-start.4 = (bf16[8,64,128]{2,1,0:T(8,128)(2,1)}, bf16[8,64,128]{2,1,0:T(8,128)(2,1)S(1)}, u32[]{:S(2)}, u32[]{:S(2)}) collective-permute-start(bf16[8,64,128]{2,1,0:T(8,128)(2,1)} %get-tuple-element.34), channel_id=1, source_target_pairs={{0,1},{1,0},{8,9},{9,8},{16,17},{17,16},{24,25},{25,24},{2,3},{3,2... | collective-permute-start | bytes 393224 | tf_op jit(solution)/shard_map/ppermute | solution.py:563
  77.5 13.2 %copy-start.13 = (bf16[8,64,128]{2,1,0:T(8,128)(2,1)}, bf16[8,64,128]{2,1,0:T(8,128)(2,1)S(1)}, u32[]{:S(2)}) copy-start(bf16[8,64,128]{2,1,0:T(8,128)(2,1)S(1)} %collective-permute-done.25.refs_14_) | copy-start | bytes 393220
  77.5 22.6 %collective-permute-start.5 = (bf16[8,64,128]{2,1,0:T(8,128)(2,1)}, bf16[8,64,128]{2,1,0:T(8,128)(2,1)S(1)}, u32[]{:S(2)}, u32[]{:S(2)}) collective-permute-start(bf16[8,64,128]{2,1,0:T(8,128)(2,1)} %get-tuple-element.35), channel_id=1, source_target_pairs={{0,8},{1,9},{8,0},{9,1},{16,24},{17,25},{24,16},{25,17},{2,10},{3,... | collective-permute-start | bytes 393224 | tf_op jit(solution)/shard_map/ppermute | solution.py:563
  86.3 4.4 %copy-start.14 = (bf16[8,64,128]{2,1,0:T(8,128)(2,1)}, bf16[8,64,128]{2,1,0:T(8,128)(2,1)S(1)}, u32[]{:S(2)}) copy-start(bf16[8,64,128]{2,1,0:T(8,128)(2,1)S(1)} %collective-permute-done.26.refs_15_) | copy-start | bytes 393220
  86.3 13.7 %collective-permute-start.6 = (bf16[8,64,128]{2,1,0:T(8,128)(2,1)}, bf16[8,64,128]{2,1,0:T(8,128)(2,1)S(1)}, u32[]{:S(2)}, u32[]{:S(2)}) collective-permute-start(bf16[8,64,128]{2,1,0:T(8,128)(2,1)} %get-tuple-element.36), channel_id=1, source_target_pairs={{0,9},{1,8},{8,1},{9,0},{16,25},{17,24},{24,17},{25,16},{2,11},{3,... | collective-permute-start | bytes 393224 | tf_op jit(solution)/shard_map/ppermute | solution.py:563
  87.1 3.6 %copy-start.15 = (bf16[8,64,128]{2,1,0:T(8,128)(2,1)}, bf16[8,64,128]{2,1,0:T(8,128)(2,1)S(1)}, u32[]{:S(2)}) copy-start(bf16[8,64,128]{2,1,0:T(8,128)(2,1)S(1)} %collective-permute-done.27.refs_16_) | copy-start | bytes 393220
  87.1 13.0 %collective-permute-start.7 = (bf16[8,64,128]{2,1,0:T(8,128)(2,1)}, bf16[8,64,128]{2,1,0:T(8,128)(2,1)S(1)}, u32[]{:S(2)}, u32[]{:S(2)}) collective-permute-start(bf16[8,64,128]{2,1,0:T(8,128)(2,1)} %get-tuple-element.37), channel_id=1, source_target_pairs={{0,16},{1,17},{8,24},{9,25},{16,0},{17,1},{24,8},{25,9},{2,18},{3,... | collective-permute-start | bytes 393224 | tf_op jit(solution)/shard_map/ppermute | solution.py:563
  87.9 12.2 %copy-start.20 = (bf16[8,64,128]{2,1,0:T(8,128)(2,1)}, bf16[8,64,128]{2,1,0:T(8,128)(2,1)S(1)}, u32[]{:S(2)}) copy-start(bf16[8,64,128]{2,1,0:T(8,128)(2,1)S(1)} %collective-permute-done.10.refs_6_) | copy-start | bytes 393220
  87.9 12.2 %collective-permute-start.8 = (bf16[8,64,128]{2,1,0:T(8,128)(2,1)}, bf16[8,64,128]{2,1,0:T(8,128)(2,1)S(1)}, u32[]{:S(2)}, u32[]{:S(2)}) collective-permute-start(bf16[8,64,128]{2,1,0:T(8,128)(2,1)} %get-tuple-element.38), channel_id=1, source_target_pairs={{0,17},{1,16},{8,25},{9,24},{16,1},{17,0},{24,9},{25,8},{2,19},{3,... | collective-permute-start | bytes 393224 | tf_op jit(solution)/shard_map/ppermute | solution.py:563
  89.3 10.9 %copy-start.21 = (bf16[8,64,128]{2,1,0:T(8,128)(2,1)}, bf16[8,64,128]{2,1,0:T(8,128)(2,1)S(1)}, u32[]{:S(2)}) copy-start(bf16[8,64,128]{2,1,0:T(8,128)(2,1)S(1)} %collective-permute-done.4.refs_0_) | copy-start | bytes 393220
  89.3 10.8 %collective-permute-start.9 = (bf16[8,64,128]{2,1,0:T(8,128)(2,1)}, bf16[8,64,128]{2,1,0:T(8,128)(2,1)S(1)}, u32[]{:S(2)}, u32[]{:S(2)}) collective-permute-start(bf16[8,64,128]{2,1,0:T(8,128)(2,1)} %get-tuple-element.39), channel_id=1, source_target_pairs={{0,24},{1,25},{8,16},{9,17},{16,8},{17,9},{24,0},{25,1},{2,26},{3,... | collective-permute-start | bytes 393224 | tf_op jit(solution)/shard_map/ppermute | solution.py:563
  90.7 1.0 copy-start
  (8 other events, 5.6 us)
